TPU v7x, 32 devices: a whole 2x2x4 slice. The times are simulated.
32 devices in a mesh: rep: 4 (over z), shard: 2 (over x), tp: 4 (over y, core).
Axes of the slice: x: 2, y: 2, z: 4, core: 2. Of those that a mesh axis runs over, the one named last changes fastest.
Arguments:
- inner_dense: float32 [4, 2, 768, 3072], P('rep', None, 'shard', 'tp'), may hold values from -6 to 6
- inner_emb: float32 [4, 8192, 768], P('rep', ('shard', 'tp')), may hold values from -6 to 6
- outer_dense: float32 [2, 2, 384, 3072], P(None, 'shard', ('rep', 'tp')), may hold values from -6 to 6
- moment_dense: float32 [2, 2, 384, 3072], P(None, 'shard', ('rep', 'tp')), may hold values from -3 to 3
- outer_emb: float32 [2, 4, 16, 64, 768], P('shard', None, ('rep', 'tp')), may hold values from -6 to 6
- moment_emb: float32 [2, 4, 16, 64, 768], P('shard', None, ('rep', 'tp')), may hold values from -3 to 3
- basis: float32 [64, 768], replicated, may hold values from -0.1875 to 0.1875
Outputs:
- new_outer_dense: float32 [2, 2, 384, 3072], P(None, 'shard', ('rep', 'tp'))
- new_moment_dense: float32 [2, 2, 384, 3072], P(None, 'shard', ('rep', 'tp'))
- new_outer_emb: float32 [2, 4, 16, 64, 768], P('shard', None, ('rep', 'tp'))
- new_moment_emb: float32 [2, 4, 16, 64, 768], P('shard', None, ('rep', 'tp'))
- train_dense: float32 [2, 768, 3072], P(None, 'shard', 'tp')
- train_emb: float32 [8192, 768], P(('shard', 'tp'))
All inputs are finite; a program needn't handle non-finite values.
Results may differ from a plain program's by a relative error of at most 0.00007.
Values sent between devices are 32-bit elements; how exact they have to be, the bound alone decides.
No kernel may reach another device: no remote copies, remote signals or barrier semaphores. Data moves between devices by JAX's collectives and lax.ppermute only.
A program may use at most 64 MiB of HBM per device.

v0:
```python
import jax
import jax.numpy as jnp
from jax import lax
from jax.sharding import PartitionSpec as P

momentum = 0.9
outer_rate = 0.7


def per_device(inner_dense, inner_emb, outer_dense, moment_dense, outer_emb, moment_emb, basis):
    groups = lax.axis_size("rep")
    tp_count = lax.axis_size("tp")
    width = basis.shape[1]
    dense_local = inner_dense[0]
    flat_rows = outer_dense.shape[2]
    piece_rows = outer_emb.shape[3]
    dense_outer = outer_dense[:, 0]
    emb_outer = outer_emb[0, :, 0]
    dense_recv, embed_recv = (
        lax.all_to_all(dense_local, ("rep", "tp"), split_axis=1, concat_axis=2, tiled=True),
        lax.all_to_all(inner_emb, ("rep", "tp"), split_axis=1, concat_axis=2, tiled=True),
    )
    embed_sum = (
        embed_recv.reshape(piece_rows, groups, tp_count, width).sum(axis=1).transpose(1, 0, 2)
    )
    emb_diff = emb_outer - embed_sum / groups
    factors = jnp.einsum(
        "tpd,kd->tpk",
        emb_diff,
        basis,
        precision=lax.Precision.HIGHEST,
        preferred_element_type=jnp.float32,
    )
    dense_sum = dense_recv.reshape(2, flat_rows, groups, -1).sum(axis=2)
    grad_emb = jnp.einsum(
        "tpk,kd->tpd",
        factors,
        basis,
        precision=lax.Precision.HIGHEST,
        preferred_element_type=jnp.float32,
    )
    grad_dense = dense_outer - dense_sum / groups
    moment_new = momentum * moment_dense[:, 0] + grad_dense
    dense_new = dense_outer - outer_rate * (grad_dense + momentum * moment_new)
    emb_moment_new = momentum * moment_emb[0, :, 0] + grad_emb
    emb_new = emb_outer - outer_rate * (grad_emb + momentum * emb_moment_new)
    emb_wide = emb_new.transpose(1, 0, 2).reshape(1, piece_rows, tp_count * width)
    dense_cols, embed_cols = (
        lax.all_to_all(dense_new, "tp", split_axis=2, concat_axis=1, tiled=True),
        lax.all_to_all(emb_wide, "tp", split_axis=2, concat_axis=1, tiled=True),
    )
    dense_train, embed_train = (
        lax.all_gather(dense_cols, "rep", axis=1, tiled=True),
        lax.all_gather(embed_cols, "rep", axis=1, tiled=True),
    )
    return (
        dense_new[:, None],
        moment_new[:, None],
        emb_new[None, :, None],
        emb_moment_new[None, :, None],
        dense_train,
        embed_train[0],
    )


def solution(mesh):
    in_specs = (
        P("rep", None, "shard", "tp"),
        P("rep", ("shard", "tp"), None),
        P(None, "shard", ("rep", "tp"), None),
        P(None, "shard", ("rep", "tp"), None),
        P("shard", None, ("rep", "tp"), None, None),
        P("shard", None, ("rep", "tp"), None, None),
        P(),
    )
    out_specs = (
        P(None, "shard", ("rep", "tp"), None),
        P(None, "shard", ("rep", "tp"), None),
        P("shard", None, ("rep", "tp"), None, None),
        P("shard", None, ("rep", "tp"), None, None),
        P(None, "shard", "tp"),
        P(("shard", "tp"), None),
    )
    return jax.shard_map(
        per_device, mesh=mesh, in_specs=in_specs, out_specs=out_specs, check_vma=False
    )
```

profile of v0, /device:TPU:0, one launch (start us, length us, event | category | flops | bytes accessed | tf_op | source)
XLA Modules:
  0.0 334.2 jit_solution(8532483720370222361)
XLA Ops:
  7.2 0.0 copy-start
  7.2 3.5 %copy.80 = f32[1,2,384,768]{3,1,2,0:T(2,128)S(1)} copy(f32[1,2,384,768]{3,2,1,0:T(8,128)} %param.7) | data formatting | bytes 4718592 | tf_op args[0]
  10.7 61.2 %all_to_all.66 = f32[2,384,768]{2,0,1:T(2,128)S(1)} all-to-all(f32[2,384,768]{2,0,1:T(2,128)S(1)} %bitcast.130), channel_id=1, replica_groups=mesh['rep'=4,'shard'=2,'tp'=4] {'rep','tp'}, dimensions={1} | all-to-all | bytes 4718592 | tf_op jit(solution)/shard_map/all_to_all | solution.py:20
  71.9 1.4 copy.79
  73.3 2.2 reshape.37
  75.4 3.2 reduce_sum.18
  78.6 0.0 copy-start.1
  78.6 0.8 copy-done.1
  79.4 0.0 copy-done.6
  79.4 0.0 copy-done.8
  79.4 1.0 fusion.6
  80.4 4.2 %copy.63 = f32[2,24,3072]{1,0,2:T(2,128)S(1)} copy(f32[2,24,3072]{2,1,0:T(8,128)} %fusion.6) | data formatting | bytes 1179648 | tf_op jit(solution)/shard_map/sub | solution.py:44
  84.6 6.2 %reshape.41 = f32[4,1,36864]{2,1,0:T(1,128)} reshape(f32[3072,2,24]{2,1,0:T(2,128)S(1)} %bitcast.126) | data formatting | bytes 1179648
  90.9 3.7 %all-to-all-start.2 = ((f32[4,1,36864]{2,1,0:T(1,128)}), f32[4,1,36864]{2,1,0:T(1,128)S(1)}, u32[]{:S(2)}, u32[]{:S(2)}) async-start(f32[4,1,36864]{2,1,0:T(1,128)} %reshape.41), calls=%async_computation.2 | async-start | bytes 1179648 | tf_op jit(solution)/shard_map/all_to_all | solution.py:49
  94.5 6.8 %copy.61 = f32[1,1024,768]{2,0,1:T(1,128)} copy(f32[1,1024,768]{2,1,0:T(8,128)} %param.8) | data formatting | bytes 6291456 | tf_op args[1]
  101.3 2.5 all-to-all-done.2
  103.9 0.8 copy-done.5
  104.7 3.7 %all-to-all-start.1 = ((f32[1,1024,768]{2,0,1:T(1,128)}), f32[1,1024,768]{2,0,1:T(1,128)S(1)}, u32[]{:S(2)}, u32[]{:S(2)}) async-start(f32[1,1024,768]{2,0,1:T(1,128)} %copy.61), calls=%async_computation.1 | async-start | bytes 6291456 | tf_op jit(solution)/shard_map/all_to_all | solution.py:21
  108.4 0.0 all-gather.3.cloned.1.call-start
  108.5 0.5 broadcast.54
  109.0 4.1 %reduce = f32[4,36864]{1,0:T(4,128)} reduce(f32[4,1,36864]{2,1,0:T(1,128)} %copy-done.5, f32[]{:T(128)} %broadcast.54), dimensions={1}, to_apply=%all_to_all.54.reduce_sub_computation | reduce | bytes 1179652 | tf_op jit(solution)/shard_map/all_to_all | solution.py:49
  113.1 7.8 %reshape.42 = f32[3072,2,24]{2,1,0:T(2,128)} reshape(f32[4,36864]{1,0:T(4,128)} %reduce) | data formatting | bytes 1179648
  120.9 5.1 %copy.64 = f32[2,4,24,768]{3,2,1,0:T(8,128)} copy(f32[2,4,24,768]{2,0,3,1:T(2,128)} %bitcast.127) | data formatting | bytes 1179648 | tf_op jit(solution)/shard_map/all_to_all | solution.py:49
  125.9 0.0 all-gather.3.cloned.1.call-update
  125.9 0.3 all-gather.5.cloned.1.call-start
  126.2 66.7 %all-to-all-done.1 = f32[1,1024,768]{2,0,1:T(1,128)S(1)} async-done(((f32[1,1024,768]{2,0,1:T(1,128)}), f32[1,1024,768]{2,0,1:T(1,128)S(1)}, u32[]{:S(2)}, u32[]{:S(2)}) %all-to-all-start.1) | async-done | bytes 3145760 | tf_op jit(solution)/shard_map/all_to_all | solution.py:21
  192.9 2.0 copy.76
  194.9 2.3 reduce_sum.19
  197.2 0.8 fusion
  198.0 2.0 fusion.16
  200.0 0.5 copy.73
  200.5 13.7 %reduce.1 = f32[3072,64]{1,0:T(8,128)S(1)} reduce(f32[3072,1,64]{2,1,0:T(1,128)S(1)} %bitcast.132, f32[]{:T(128)} %broadcast.54), dimensions={1}, to_apply=%bitcast.117.reduce_sub_computation | reduce | bytes 1572868
  214.2 1.0 reshape.43
  215.2 28.2 %all_to_all.67 = f32[4,1,49152]{2,1,0:T(1,128)S(1)} all-to-all(f32[4,1,49152]{2,1,0:T(1,128)S(1)} %reshape.43), channel_id=1, replica_groups=mesh['rep'=4,'shard'=2,'tp'=4] {'tp'}, dimensions={0} | all-to-all | bytes 1572864 | tf_op jit(solution)/shard_map/all_to_all | solution.py:50
  243.4 2.9 reduce.2
  246.3 1.9 reshape.44
  248.2 0.0 copy-start.2
  248.2 0.5 copy.74
  248.7 0.0 copy-start.7
  248.7 0.0 copy-start.9
  248.7 1.0 copy.68
  249.8 0.0 all-gather.5.cloned.1.call-update
  249.8 0.0 copy-done.7
  249.8 0.5 copy-done.9
  250.3 1.2 fusion.9
  251.5 70.9 %all-gather.5.cloned.1.call-done = f32[1,1024,768]{2,1,0:T(8,128)} async-done(((f32[1,256,768]{2,1,0:T(8,128)}), f32[1,1024,768]{2,1,0:T(8,128)}) %all-gather.5.cloned.1.call-update) | async-done | bytes 3145744 | tf_op jit(solution)/shard_map/all_gather | solution.py:54
  322.3 3.4 %copy.83 = f32[2,384,768]{2,1,0:T(8,128)} copy(f32[2,384,768]{2,1,0:T(8,128)} %all-gather.3.cloned.1.call-done) | data formatting | bytes 4718592
  325.7 1.7 copy.84
  (12 shorter events, 0.0 us)
Async XLA Ops:
  7.2 190.0 %copy-start = (f32[64,768]{1,0:T(8,128)S(1)}, f32[64,768]{1,0:T(8,128)}, u32[]{:S(2)}) copy-start(f32[64,768]{1,0:T(8,128)} %param.13) | copy-start | bytes 589828
  75.4 4.0 %copy-start.6 = (f32[2,1,24,3072]{3,2,1,0:T(8,128)S(1)}, f32[2,1,24,3072]{3,2,1,0:T(8,128)}, u32[]{:S(2)}) copy-start(f32[2,1,24,3072]{3,2,1,0:T(8,128)} %param.10) | copy-start | bytes 1769476
  75.4 4.0 %copy-start.8 = (f32[2,1,24,3072]{3,2,1,0:T(8,128)S(1)}, f32[2,1,24,3072]{3,2,1,0:T(8,128)}, u32[]{:S(2)}) copy-start(f32[2,1,24,3072]{3,2,1,0:T(8,128)} %param.9) | copy-start | bytes 1769476
  78.6 0.8 copy-start.1
  90.9 13.0 %all-to-all-start.2 = ((f32[4,1,36864]{2,1,0:T(1,128)}), f32[4,1,36864]{2,1,0:T(1,128)S(1)}, u32[]{:S(2)}, u32[]{:S(2)}) async-start(f32[4,1,36864]{2,1,0:T(1,128)} %reshape.41), calls=%async_computation.2 | async-start | bytes 1179648 | tf_op jit(solution)/shard_map/all_to_all | solution.py:49
  103.9 0.8 copy-start.5
  104.7 88.2 %all-to-all-start.1 = ((f32[1,1024,768]{2,0,1:T(1,128)}), f32[1,1024,768]{2,0,1:T(1,128)S(1)}, u32[]{:S(2)}, u32[]{:S(2)}) async-start(f32[1,1024,768]{2,0,1:T(1,128)} %copy.61), calls=%async_computation.1 | async-start | bytes 6291456 | tf_op jit(solution)/shard_map/all_to_all | solution.py:21
  108.4 143.0 %all-gather.3.cloned.1.call-start = ((), (), s32[]{:S(2)}) async-start(), calls=%async_computation.4 | async-start | bytes 2949120 | tf_op jit(solution)/shard_map/all_gather | solution.py:53
  125.9 196.4 %all-gather.5.cloned.1.call-start = ((), (), s32[]{:S(2)}) async-start(), calls=%async_computation.5 | async-start | bytes 3932160 | tf_op jit(solution)/shard_map/all_gather | solution.py:54
  194.9 2.3 copy-start.4
  194.9 3.1 copy-start.10
  248.2 1.6 copy-start.2
  248.7 1.1 copy-start.7
  248.7 1.6 copy-start.9
  322.3 3.4 %copy-start.3 = (f32[1,1024,768]{2,1,0:T(8,128)S(1)}, f32[1,1024,768]{2,1,0:T(8,128)}, u32[]{:S(2)}) copy-start(f32[1,1024,768]{2,1,0:T(8,128)} %all-gather.5.cloned.1.call-done) | copy-start | bytes 9437188
Sparse Core Ops, SparseCore 0:
  126.1 86.7 all-gather.2
  249.9 72.3 all-gather.4
where the time goes:
time: 335 us; the launch traced here: 334 us
  waiting for transfers between devices  140 us (42%)
  blocking collectives  89.4 us (27%)
  local copies, waits for them, and re-layouts  51.7 us (15%)
  other arithmetic  28.3 us (8%)
  between operations  14.2 us (4%)
  starting transfers between devices  7.7 us (2%)
    all_gather x1, waiting for transfers between devices, per_device(): lax.all_gather(embed_cols, 'rep', axis=1, tiled=True)  70.9 us
    all_to_all x1, waiting for transfers between devices, per_device(): lax.all_to_all(inner_emb, ('rep', 'tp'), split_axis=1, concat_axis=2, til...  66.7 us
    all_to_all x1, blocking collectives, per_device(): lax.all_to_all(dense_local, ('rep', 'tp'), split_axis=1, concat_axis=2, t...  61.2 us
    unnamed x31, local copies, waits for them, and re-layouts  36.4 us
    all_to_all x1, blocking collectives, per_device(): lax.all_to_all(emb_wide, 'tp', split_axis=2, concat_axis=1, tiled=True)  28.2 us
    unnamed x2, other arithmetic  14.9 us
  transfers between devices with their start and end apart: 4, of which 3 were waited for; matrix products, arithmetic and copies ran while one was open for 16% of the time, Pallas kernels for 0%

commit v1 on v0

v1 whole, which is shorter than its diff:
```python
import jax
import jax.numpy as jnp
from jax import lax
from jax.sharding import PartitionSpec as P

momentum = 0.9
outer_rate = 0.7
grad_weight = outer_rate * (1.0 + momentum)
moment_weight = outer_rate * momentum * momentum


def dot(a, b):
    return jnp.dot(a, b, precision=lax.Precision.HIGHEST, preferred_element_type=jnp.float32)


def pack(f, pieces):
    half = f.shape[0] // pieces // 2
    f = f.reshape(pieces, 2, half, f.shape[1])
    return jnp.concatenate([f[:, 0], f[:, 1]], axis=-1)


def unpack(f):
    k = f.shape[-1] // 2
    return jnp.concatenate([f[..., :k], f[..., k:]], axis=1)


def swap_tp(pieces):
    count = lax.axis_size("tp")
    me = lax.axis_index("tp")
    got = []
    for d in range(count):
        piece = lax.dynamic_index_in_dim(pieces, me ^ d, 0, keepdims=False)
        if d:
            piece = lax.ppermute(piece, "tp", [(i, i ^ d) for i in range(count)])
        got.append(piece)
    ordered = []
    for j in range(count):
        out = got[j]
        for i in range(1, count):
            out = jnp.where(me == i, got[j ^ i], out)
        ordered.append(out)
    return jnp.stack(ordered)


def per_device(inner_dense, inner_emb, outer_dense, moment_dense, outer_emb, moment_emb, basis):
    groups = lax.axis_size("rep")
    tp_count = lax.axis_size("tp")
    me = lax.axis_index("rep")
    up = [(i, (i + 1) % groups) for i in range(groups)]
    down = [((i + 1) % groups, i) for i in range(groups)]
    two = [(i, (i + 2) % groups) for i in range(groups)]

    def after(i):
        return lax.rem(me + groups + i, groups)

    def send(x, pairs):
        return lax.ppermute(x, "rep", pairs)

    width = basis.shape[1]
    dense = inner_dense[0]
    cols = dense.shape[2]
    block_rows = dense.shape[1] // groups
    flat_rows = outer_dense.shape[2]
    piece_rows = outer_emb.shape[3]
    emb_rows = tp_count * piece_rows

    def block(i, h):
        return lax.dynamic_slice(dense, (h, after(i) * block_rows, 0), (1, block_rows, cols))[0]

    far_up = send(block(2, 0), up)
    far_down = send(block(2, 1), down)
    near_up = send(block(1, 1), up)
    near_down = send(block(-1, 0), down)

    projected = pack(dot(inner_emb[0], basis.T), groups * tp_count)
    projected = projected.reshape((groups, tp_count) + projected.shape[1:])

    def part(i):
        return lax.dynamic_index_in_dim(projected, after(i), 0, keepdims=False)

    proj_sum = part(0) + send(part(1), up) + send(part(-1), down) + send(part(2), two)

    emb_outer = outer_emb[0, :, 0]
    emb_moment = moment_emb[0, :, 0]
    outer_proj = dot(emb_outer.reshape(-1, width), basis.T)
    outer_grad = dot(outer_proj, basis).reshape(emb_outer.shape)
    emb_base = swap_tp(emb_outer - moment_weight * emb_moment - grad_weight * outer_grad)
    dense_outer = outer_dense[:, 0]
    dense_moment = moment_dense[:, 0]
    dense_base = (1.0 - grad_weight) * dense_outer - moment_weight * dense_moment
    dense_base = swap_tp(
        dense_base.reshape(2, flat_rows, tp_count, cols).transpose(2, 0, 1, 3)
    ).transpose(1, 0, 2, 3).reshape(2, block_rows, cols)

    sum_up = send(block(1, 0) + far_up, up)
    sum_down = send(block(-1, 1) + far_down, down)
    dense_sum = (block(0, 0) + near_down + sum_up, block(0, 1) + near_up + sum_down)

    emb_block = emb_base.reshape(emb_rows, width) + (grad_weight / groups) * dot(
        unpack(proj_sum).reshape(emb_rows, -1), basis
    )
    emb_half = emb_rows // 2
    emb_parts = (emb_block[:emb_half], emb_block[emb_half:])
    dense_parts = tuple(dense_base[h] + (grad_weight / groups) * dense_sum[h] for h in (0, 1))

    def gather(parts):
        left0 = send(parts[0], up)
        right1 = send(parts[1], down)
        left1 = send(parts[1], up)
        right0 = send(parts[0], down)
        far0 = send(left0, up)
        far1 = send(right1, down)
        return {0: parts, -1: (left0, left1), 1: (right0, right1), 2: (far0, far1)}

    emb_all = gather(emb_parts)
    dense_all = gather(dense_parts)
    embed_train = jnp.zeros((groups * emb_rows, width), jnp.float32)
    for i, halves in emb_all.items():
        for h, value in enumerate(halves):
            embed_train = lax.dynamic_update_slice(
                embed_train, value, (after(i) * emb_rows + h * emb_half, 0)
            )
    dense_train = jnp.zeros(dense.shape, jnp.float32)
    for i, halves in dense_all.items():
        for h, value in enumerate(halves):
            dense_train = lax.dynamic_update_slice(
                dense_train, value[None], (h, after(i) * block_rows, 0)
            )

    dense_back = swap_tp(
        jnp.stack(dense_sum).reshape(2, tp_count, flat_rows, cols).transpose(1, 0, 2, 3)
    ).transpose(1, 2, 0, 3).reshape(2, flat_rows, tp_count * cols)
    grad_dense = dense_outer - dense_back / groups
    moment_new = momentum * dense_moment + grad_dense
    dense_new = dense_outer - outer_rate * (grad_dense + momentum * moment_new)
    proj_back = unpack(swap_tp(proj_sum)).reshape(tp_count * piece_rows, -1)
    factors = outer_proj - proj_back / groups
    grad_emb = dot(factors, basis).reshape(emb_outer.shape)
    emb_moment_new = momentum * emb_moment + grad_emb
    emb_new = emb_outer - outer_rate * (grad_emb + momentum * emb_moment_new)
    return (
        dense_new[:, None],
        moment_new[:, None],
        emb_new[None, :, None],
        emb_moment_new[None, :, None],
        dense_train,
        embed_train,
    )


def solution(mesh):
    in_specs = (
        P("rep", None, "shard", "tp"),
        P("rep", ("shard", "tp"), None),
        P(None, "shard", ("rep", "tp"), None),
        P(None, "shard", ("rep", "tp"), None),
        P("shard", None, ("rep", "tp"), None, None),
        P("shard", None, ("rep", "tp"), None, None),
        P(),
    )
    out_specs = (
        P(None, "shard", ("rep", "tp"), None),
        P(None, "shard", ("rep", "tp"), None),
        P("shard", None, ("rep", "tp"), None, None),
        P("shard", None, ("rep", "tp"), None, None),
        P(None, "shard", "tp"),
        P(("shard", "tp"), None),
    )
    return jax.shard_map(
        per_device, mesh=mesh, in_specs=in_specs, out_specs=out_specs, check_vma=False
    )
```

time: 335 us -> 182 us (0.54)
  blocking collectives: 89.4 us -> 0 us
  waiting for transfers between devices: 140 us -> 79 us
  starting transfers between devices: 7.7 us -> 39.6 us
  local copies, waits for them, and re-layouts: 51.7 us -> 34.3 us
  between operations: 14.2 us -> 0.92 us
  other arithmetic: 28.3 us -> 17.6 us
  matrix products: 2.8 us -> 9.92 us
    all_to_all x2 -> x0, blocking collectives: 89.4 us -> none  [the longest x1 61.2 us: per_device(): lax.all_to_all(dense_local, ('rep', 'tp'), split_axis=1, concat_axis=2, t...]
    ppermute x0 -> x33, waiting for transfers between devices: none -> 79 us  [the longest x21 77.3 us: send(): return lax.ppermute(x, 'rep', pairs)]
    all_gather x2 -> x0, waiting for transfers between devices: 70.9 us -> none  [the longest x1 70.9 us: per_device(): lax.all_gather(embed_cols, 'rep', axis=1, tiled=True)]
    all_to_all x2 -> x0, waiting for transfers between devices: 69.3 us -> none  [the longest x1 66.7 us: per_device(): lax.all_to_all(inner_emb, ('rep', 'tp'), split_axis=1, concat_axis=2, til...]
    ppermute x0 -> x33, starting transfers between devices: none -> 39.6 us  [the longest x21 31.3 us: send(): return lax.ppermute(x, 'rep', pairs)]
    unnamed x31 -> x27, local copies, waits for them, and re-layouts: 36.4 us -> 2.92 us
    dynamic_update_slice x0 -> x15, local copies, waits for them, and re-layouts: none -> 16.6 us  [the longest x8 11.2 us: per_device(): lax.dynamic_update_slice(dense_train, value[None], (h, after(i) * block_r...]
    unnamed x2 -> x0, other arithmetic: 14.9 us -> none
  transfers between devices with their start and end apart: 4 -> 33, of which waited for: 3 -> 14; matrix products, arithmetic and copies ran while one was open for 16% -> 29% of each run, Pallas kernels for 0% -> 0%
where the time goes in v1:
time: 182 us; the launch traced here: 181 us
  waiting for transfers between devices  79 us (43%)
  starting transfers between devices  39.6 us (22%)
  local copies, waits for them, and re-layouts  34.3 us (19%)
  other arithmetic  17.6 us (10%)
  matrix products  9.92 us (5%)
    ppermute x21, waiting for transfers between devices, send(): return lax.ppermute(x, 'rep', pairs)  77.3 us
    ppermute x21, starting transfers between devices, send(): return lax.ppermute(x, 'rep', pairs)  31.3 us
    dynamic_update_slice x8, local copies, waits for them, and re-layouts, per_device(): lax.dynamic_update_slice(dense_train, value[None], (h, after(i) * block_r...  11.2 us
    dot_general x5, matrix products, dot(): jnp.dot(a, b, precision=lax.Precision.HIGHEST, preferred_element_type=jnp...  9.92 us
    ppermute x12, starting transfers between devices, swap_tp(): piece = lax.ppermute(piece, 'tp', [(i, i ^ d) for i in range(count)])  8.27 us
    dynamic_update_slice x7, local copies, waits for them, and re-layouts, per_device(): lax.dynamic_update_slice(embed_train, value, (after(i) * emb_rows + h * e...  5.39 us
  transfers between devices with their start and end apart: 33, of which 14 were waited for; matrix products, arithmetic and copies ran while one was open for 29% of the time, Pallas kernels for 0%

profile of v1, /device:TPU:0, one launch (start us, length us, event | category | flops | bytes accessed | tf_op | source)
XLA Modules:
  0.0 181.4 jit_solution(9600543391356561033)
XLA Ops:
  0.7 2.2 %fusion.62 = f32[256,64]{0,1:T(8,128)S(1)} fusion(f32[256,768]{1,0:T(8,128)} %bitcast.229, f32[64,768]{1,0:T(8,128)} %param.13), kind=kOutput, calls=%fused_computation.145 | convolution fusion | flops 150994944 | bytes 1048576 | tf_op jit(solution)/shard_map/dot_general | solution.py:13
  2.8 2.6 %convolution_multiply_fusion.1 = f32[256,768]{1,0:T(8,128)} fusion(f32[256,64]{0,1:T(8,128)S(1)} %fusion.62, f32[64,768]{1,0:T(8,128)} %param.13), kind=kOutput, calls=%fused_computation.2 | convolution fusion | flops 151191552 | bytes 1048576 | tf_op jit(solution)/shard_map/dot_general | solution.py:13
  5.5 1.8 bitcast_subtract_fusion
  9.0 2.4 %collective-permute-start.24 = (f32[64,768]{1,0:T(8,128)}, f32[64,768]{1,0:T(8,128)}, u32[]{:S(2)}, u32[]{:S(2)}) collective-permute-start(f32[64,768]{1,0:T(8,128)} %get-tuple-element.28), channel_id=1, source_target_pairs={{0,3},{1,2},{2,1},{3,0},{4,7},{5,6},{6,5},{7,4},{8,11},{9,10},{10,... | collective-permute-start | bytes 589832 | tf_op jit(solution)/shard_map/ppermute | solution.py:34
  12.0 2.6 %fusion.4 = f32[16,2,32,64]{3,2,1,0:T(8,128)S(1)} fusion(f32[16,2,32,768]{3,2,1,0:T(8,128)S(1)} %bitcast.228, f32[64,768]{1,0:T(8,128)S(1)} %copy-done.1), kind=kOutput, calls=%fused_computation.49 | convolution fusion | flops 603979776 | bytes 3604480 | tf_op jit(solution)/shard_map/dot_general | solution.py:13
  15.4 1.8 fusion.40
  17.2 3.6 %collective-permute-start.10 = (f32[4,32,128]{2,1,0:T(8,128)}, f32[4,32,128]{2,1,0:T(8,128)}, u32[]{:S(2)}, u32[]{:S(2)}) collective-permute-start(f32[4,32,128]{2,1,0:T(8,128)} %get-tuple-element.48), channel_id=1, source_target_pairs={{8,0},{16,8},{24,16},{0,24},{9,1},{17,9},{25,17},{1,25},{10,2},{18... | collective-permute-start | bytes 196616 | tf_op jit(solution)/shard_map/ppermute | solution.py:57
  20.8 1.0 collective-permute-start.9
  21.8 2.1 %multiply_subtract_fusion.1 = f32[2,1,24,3072]{3,2,1,0:T(8,128)} fusion(f32[2,1,24,3072]{3,2,1,0:T(8,128)} %param.10, f32[2,1,24,3072]{3,2,1,0:T(8,128)} %param.9), kind=kLoop, calls=%fused_computation.18 | loop fusion | flops 442368 | bytes 1769472 | tf_op jit(solution)/shard_map/sub | solution.py:90
  24.0 2.2 %sub.37 = f32[2,24,4,768]{3,2,1,0:T(4,128)} reshape(f32[2,1,24,3072]{3,2,1,0:T(8,128)} %multiply_subtract_fusion.1) | data formatting | bytes 1179648 | tf_op jit(solution)/shard_map/sub | solution.py:90
  26.1 2.3 %dynamic-slice_bitcast_fusion.1 = (f32[96,768]{1,0:T(8,128)}, f32[96,768]{1,0:T(8,128)}, f32[96,768]{1,0:T(8,128)}, f32[96,768]{1,0:T(8,128)}) fusion(f32[1,2,384,768]{3,2,1,0:T(8,128)} %param.7, s32[]{:T(128)S(6)} %select_n.307, s32[]{:T(128)S(6)} %select_n.308, s32[]{:T(128)S(6)} %select_n.306), kind=kLoop, calls=%fused_computation.38 | loop fusion | bytes 2359308 | tf_op jit(solution)/shard_map/squeeze | solution.py:68
  31.0 1.1 fusion.38
  38.3 1.6 copy.41
  39.9 1.7 fusion.43
  41.7 2.7 %multiply_subtract_fusion = (f32[1,4,1,64,768]{4,3,2,1,0:T(8,128)}, f32[1,4,1,64,768]{4,3,2,1,0:T(8,128)}) fusion(f32[1,4,1,64,768]{4,3,2,1,0:T(8,128)} %param.11, f32[1,4,1,64,768]{4,3,2,1,0:T(8,128)S(1)} %bitcast.232, f32[1,4,1,64,768]{4,3,2,1,0:T(8,128)} %param.12), kind=kLoop, calls=%fused_computation.13 | loop fusion | flops 1179648 | bytes 3932160 | tf_op jit(solution)/shard_map/sub | solution.py:140
  45.2 2.8 %collective-permute-start.4 = (f32[96,768]{1,0:T(8,128)S(1)}, f32[96,768]{1,0:T(8,128)S(1)}, u32[]{:S(2)}, u32[]{:S(2)}) collective-permute-start(f32[96,768]{1,0:T(8,128)S(1)} %copy-done.10), channel_id=1, source_target_pairs={{8,0},{16,8},{24,16},{0,24},{9,1},{17,9},{25,17},{1,25},{10,2},{18... | collective-permute-start | bytes 884744 | tf_op jit(solution)/shard_map/ppermute | solution.py:57
  48.0 1.1 fusion.25
  49.3 1.7 collective-permute-start.3
  51.0 2.2 %collective-permute-start = (f32[96,768]{1,0:T(8,128)S(1)}, f32[96,768]{1,0:T(8,128)S(1)}, u32[]{:S(2)}, u32[]{:S(2)}) collective-permute-start(f32[96,768]{1,0:T(8,128)S(1)} %copy-done.7), channel_id=1, source_target_pairs={{8,0},{16,8},{24,16},{0,24},{9,1},{17,9},{25,17},{1,25},{10,2},{18... | collective-permute-start | bytes 884744 | tf_op jit(solution)/shard_map/ppermute | solution.py:57
  53.2 1.2 fusion.8
  55.3 11.8 %collective-permute-done.4 = f32[96,768]{1,0:T(8,128)S(1)} collective-permute-done((f32[96,768]{1,0:T(8,128)S(1)}, f32[96,768]{1,0:T(8,128)S(1)}, u32[]{:S(2)}, u32[]{:S(2)}) %collective-permute-start.4) | collective-permute-done | bytes 294944 | tf_op jit(solution)/shard_map/ppermute | solution.py:57
  67.2 1.9 %broadcast_in_dim.43 = f32[1024,768]{1,0:T(8,128)} broadcast(f32[]{:T(128)} %constant.117.clone.1), dimensions={} | broadcast | bytes 3145732 | tf_op jit(solution)/shard_map/broadcast_in_dim | solution.py:117
  70.0 3.0 %collective-permute-start.27 = (f32[128,768]{1,0:T(8,128)S(1)}, f32[128,768]{1,0:T(8,128)S(1)}, u32[]{:S(2)}, u32[]{:S(2)}) collective-permute-start(f32[128,768]{1,0:T(8,128)S(1)} %get-tuple-element.27), channel_id=1, source_target_pairs={{0,8},{8,16},{16,24},{24,0},{1,9},{9,17},{17,25},{25,1},{2,10},{10... | collective-permute-start | bytes 1179656 | tf_op jit(solution)/shard_map/ppermute | solution.py:57
  74.6 1.3 collective-permute-start.28
  75.8 12.2 %collective-permute-done.5 = f32[96,768]{1,0:T(8,128)S(1)} collective-permute-done((f32[96,768]{1,0:T(8,128)S(1)}, f32[96,768]{1,0:T(8,128)S(1)}, u32[]{:S(2)}, u32[]{:S(2)}) %collective-permute-start.5) | collective-permute-done | bytes 294944 | tf_op jit(solution)/shard_map/ppermute | solution.py:57
  88.9 1.3 collective-permute-done.27
  90.2 1.9 %collective-permute-start.2 = (f32[96,768]{1,0:T(8,128)S(1)}, f32[96,768]{1,0:T(8,128)S(1)}, u32[]{:S(2)}, u32[]{:S(2)}) collective-permute-start(f32[96,768]{1,0:T(8,128)S(1)} %get-tuple-element.16), channel_id=1, source_target_pairs={{0,8},{8,16},{16,24},{24,0},{1,9},{9,17},{17,25},{25,1},{2,10},{10... | collective-permute-start | bytes 884744 | tf_op jit(solution)/shard_map/ppermute | solution.py:57
  92.9 14.3 %collective-permute-done.28 = f32[128,768]{1,0:T(8,128)S(1)} collective-permute-done((f32[128,768]{1,0:T(8,128)S(1)}, f32[128,768]{1,0:T(8,128)S(1)}, u32[]{:S(2)}, u32[]{:S(2)}) %collective-permute-start.28) | collective-permute-done | bytes 393248 | tf_op jit(solution)/shard_map/ppermute | solution.py:57
  107.1 3.5 %collective-permute-start.21 = (f32[96,768]{1,0:T(8,128)}, f32[96,768]{1,0:T(8,128)}, u32[]{:S(2)}, u32[]{:S(2)}) collective-permute-start(f32[96,768]{1,0:T(8,128)} %get-tuple-element.6), channel_id=1, source_target_pairs={{8,0},{16,8},{24,16},{0,24},{9,1},{17,9},{25,17},{1,25},{10,2},{18... | collective-permute-start | bytes 884744 | tf_op jit(solution)/shard_map/ppermute | solution.py:57
  111.4 4.2 %collective-permute-done.30 = f32[128,768]{1,0:T(8,128)S(1)} collective-permute-done((f32[128,768]{1,0:T(8,128)S(1)}, f32[128,768]{1,0:T(8,128)S(1)}, u32[]{:S(2)}, u32[]{:S(2)}) %collective-permute-start.30) | collective-permute-done | bytes 393248 | tf_op jit(solution)/shard_map/ppermute | solution.py:57
  115.6 3.2 %collective-permute-start.32 = (f32[128,768]{1,0:T(8,128)S(1)}, f32[128,768]{1,0:T(8,128)S(1)}, u32[]{:S(2)}, u32[]{:S(2)}) collective-permute-start(f32[128,768]{1,0:T(8,128)S(1)} %collective-permute-done.30), channel_id=1, source_target_pairs={{8,0},{16,8},{24,16},{0,24},{9,1},{17,9},{25,17},{1,25},{10,2},{18... | collective-permute-start | bytes 1179656 | tf_op jit(solution)/shard_map/ppermute | solution.py:57
  120.3 1.6 collective-permute-done.2
  125.0 1.5 collective-permute-start.7
  126.4 10.3 %collective-permute-done.31 = f32[128,768]{1,0:T(8,128)S(1)} collective-permute-done((f32[128,768]{1,0:T(8,128)S(1)}, f32[128,768]{1,0:T(8,128)S(1)}, u32[]{:S(2)}, u32[]{:S(2)}) %collective-permute-start.31) | collective-permute-done | bytes 393248 | tf_op jit(solution)/shard_map/ppermute | solution.py:57
  137.5 5.7 %collective-permute-done.32 = f32[128,768]{1,0:T(8,128)S(1)} collective-permute-done((f32[128,768]{1,0:T(8,128)S(1)}, f32[128,768]{1,0:T(8,128)S(1)}, u32[]{:S(2)}, u32[]{:S(2)}) %collective-permute-start.32) | collective-permute-done | bytes 393248 | tf_op jit(solution)/shard_map/ppermute | solution.py:57
  143.1 1.7 collective-permute-start.19
  145.9 3.6 %collective-permute-start.20 = (f32[96,768]{1,0:T(8,128)}, f32[96,768]{1,0:T(8,128)}, u32[]{:S(2)}, u32[]{:S(2)}) collective-permute-start(f32[96,768]{1,0:T(8,128)} %get-tuple-element.8), channel_id=1, source_target_pairs={{8,0},{16,8},{24,16},{0,24},{9,1},{17,9},{25,17},{1,25},{10,2},{18... | collective-permute-start | bytes 884744 | tf_op jit(solution)/shard_map/ppermute | solution.py:57
  150.3 1.2 copy.32
  151.5 2.2 %div.21 = f32[2,1,24,3072]{3,2,1,0:T(8,128)} reshape(f32[2,24,4,768]{3,2,1,0:T(4,128)} %copy.32) | data formatting | bytes 1179648 | tf_op jit(solution)/shard_map/div | solution.py:133
  153.7 2.6 %multiply_subtract_fusion.2 = (f32[2,1,24,3072]{3,2,1,0:T(8,128)}, f32[2,1,24,3072]{3,2,1,0:T(8,128)}) fusion(f32[2,1,24,3072]{3,2,1,0:T(8,128)} %param.9, f32[2,1,24,3072]{3,2,1,0:T(8,128)} %param.10, f32[2,1,24,3072]{3,2,1,0:T(8,128)} %div.21), kind=kLoop, calls=%fused_computation.19 | loop fusion | flops 1032192 | bytes 2949120 | tf_op jit(solution)/shard_map/sub | solution.py:135
  156.2 5.6 %collective-permute-done.18 = f32[96,768]{1,0:T(8,128)} collective-permute-done((f32[96,768]{1,0:T(8,128)}, f32[96,768]{1,0:T(8,128)}, u32[]{:S(2)}, u32[]{:S(2)}) %collective-permute-start.18) | collective-permute-done | bytes 294944 | tf_op jit(solution)/shard_map/ppermute | solution.py:57
  161.8 1.7 bitcast_dynamic-update-slice_fusion.5
  163.6 1.7 bitcast_dynamic-update-slice_fusion.4
  165.3 1.3 collective-permute-done.20
  166.5 1.7 bitcast_dynamic-update-slice_fusion.3
  168.2 1.7 bitcast_dynamic-update-slice_fusion.2
  169.9 9.0 %collective-permute-done.22 = f32[96,768]{1,0:T(8,128)S(1)} collective-permute-done((f32[96,768]{1,0:T(8,128)}, f32[96,768]{1,0:T(8,128)S(1)}, u32[]{:S(2)}, u32[]{:S(2)}) %collective-permute-start.22) | collective-permute-done | bytes 294944 | tf_op jit(solution)/shard_map/ppermute | solution.py:57
  179.7 1.7 bitcast_dynamic-update-slice_fusion
  (101 shorter events, 26.3 us)
Async XLA Ops:
  0.6 11.4 %copy-start = (f32[1,1024,768]{2,1,0:T(8,128)S(1)}, f32[1,1024,768]{2,1,0:T(8,128)}, u32[]{:S(2)}) copy-start(f32[1,1024,768]{2,1,0:T(8,128)} %param.8) | copy-start | bytes 9437188
  5.5 6.5 %copy-start.1 = (f32[64,768]{1,0:T(8,128)S(1)}, f32[64,768]{1,0:T(8,128)}, u32[]{:S(2)}) copy-start(f32[64,768]{1,0:T(8,128)} %param.13) | copy-start | bytes 589828
  7.2 0.9 copy-start.2
  9.0 40.2 %collective-permute-start.24 = (f32[64,768]{1,0:T(8,128)}, f32[64,768]{1,0:T(8,128)}, u32[]{:S(2)}, u32[]{:S(2)}) collective-permute-start(f32[64,768]{1,0:T(8,128)} %get-tuple-element.28), channel_id=1, source_target_pairs={{0,3},{1,2},{2,1},{3,0},{4,7},{5,6},{6,5},{7,4},{8,11},{9,10},{10,... | collective-permute-start | bytes 589832 | tf_op jit(solution)/shard_map/ppermute | solution.py:34
  11.4 39.6 %collective-permute-start.25 = (f32[64,768]{1,0:T(8,128)}, f32[64,768]{1,0:T(8,128)}, u32[]{:S(2)}, u32[]{:S(2)}) collective-permute-start(f32[64,768]{1,0:T(8,128)} %get-tuple-element.30), channel_id=1, source_target_pairs={{0,2},{1,3},{2,0},{3,1},{4,6},{5,7},{6,4},{7,5},{8,10},{9,11},{10,... | collective-permute-start | bytes 589832 | tf_op jit(solution)/shard_map/ppermute | solution.py:34
  17.2 13.8 %collective-permute-start.10 = (f32[4,32,128]{2,1,0:T(8,128)}, f32[4,32,128]{2,1,0:T(8,128)}, u32[]{:S(2)}, u32[]{:S(2)}) collective-permute-start(f32[4,32,128]{2,1,0:T(8,128)} %get-tuple-element.48), channel_id=1, source_target_pairs={{8,0},{16,8},{24,16},{0,24},{9,1},{17,9},{25,17},{1,25},{10,2},{18... | collective-permute-start | bytes 196616 | tf_op jit(solution)/shard_map/ppermute | solution.py:57
  20.8 10.2 %collective-permute-start.11 = (f32[4,32,128]{2,1,0:T(8,128)}, f32[4,32,128]{2,1,0:T(8,128)}, u32[]{:S(2)}, u32[]{:S(2)}) collective-permute-start(f32[4,32,128]{2,1,0:T(8,128)} %get-tuple-element.49), channel_id=1, source_target_pairs={{0,16},{8,24},{16,0},{24,8},{1,17},{9,25},{17,1},{25,9},{2,18},{10... | collective-permute-start | bytes 196616 | tf_op jit(solution)/shard_map/ppermute | solution.py:57
  20.8 10.2 %collective-permute-start.9 = (f32[4,32,128]{2,1,0:T(8,128)}, f32[4,32,128]{2,1,0:T(8,128)}, u32[]{:S(2)}, u32[]{:S(2)}) collective-permute-start(f32[4,32,128]{2,1,0:T(8,128)} %get-tuple-element.47), channel_id=1, source_target_pairs={{0,8},{8,16},{16,24},{24,0},{1,9},{9,17},{17,25},{25,1},{2,10},{10... | collective-permute-start | bytes 196616 | tf_op jit(solution)/shard_map/ppermute | solution.py:57
  26.1 2.3 %copy-start.5 = (f32[2,24,4,768]{3,2,1,0:T(4,128)S(1)}, f32[2,24,4,768]{3,2,1,0:T(4,128)}, u32[]{:S(2)}) copy-start(f32[2,24,4,768]{3,2,1,0:T(4,128)} %sub.37) | copy-start | bytes 1769476
  32.2 3.4 %collective-permute-start.12 = (f32[32,128]{1,0:T(8,128)S(1)}, f32[32,128]{1,0:T(8,128)S(1)}, u32[]{:S(2)}, u32[]{:S(2)}) collective-permute-start(f32[32,128]{1,0:T(8,128)S(1)} %get-tuple-element.60), channel_id=1, source_target_pairs={{0,3},{1,2},{2,1},{3,0},{4,7},{5,6},{6,5},{7,4},{8,11},{9,10},{10,... | collective-permute-start | bytes 49160 | tf_op jit(solution)/shard_map/ppermute | solution.py:34
  32.8 3.9 %collective-permute-start.13 = (f32[32,128]{1,0:T(8,128)S(1)}, f32[32,128]{1,0:T(8,128)S(1)}, u32[]{:S(2)}, u32[]{:S(2)}) collective-permute-start(f32[32,128]{1,0:T(8,128)S(1)} %get-tuple-element.62), channel_id=1, source_target_pairs={{0,2},{1,3},{2,0},{3,1},{4,6},{5,7},{6,4},{7,5},{8,10},{9,11},{10,... | collective-permute-start | bytes 49160 | tf_op jit(solution)/shard_map/ppermute | solution.py:34
  33.8 3.7 %collective-permute-start.14 = (f32[32,128]{1,0:T(8,128)S(1)}, f32[32,128]{1,0:T(8,128)S(1)}, u32[]{:S(2)}, u32[]{:S(2)}) collective-permute-start(f32[32,128]{1,0:T(8,128)S(1)} %get-tuple-element.61), channel_id=1, source_target_pairs={{0,1},{1,0},{2,3},{3,2},{4,5},{5,4},{6,7},{7,6},{8,9},{9,8},{10,11... | collective-permute-start | bytes 49160 | tf_op jit(solution)/shard_map/ppermute | solution.py:34
  35.5 8.8 %collective-permute-start.15 = (f32[2,24,768]{2,1,0:T(8,128)}, f32[2,24,768]{2,1,0:T(8,128)}, u32[]{:S(2)}, u32[]{:S(2)}) collective-permute-start(f32[2,24,768]{2,1,0:T(8,128)} %bitcast.245), channel_id=1, source_target_pairs={{0,3},{1,2},{2,1},{3,0},{4,7},{5,6},{6,5},{7,4},{8,11},{9,10},{10,... | collective-permute-start | bytes 442376 | tf_op jit(solution)/shard_map/ppermute | solution.py:34
  36.7 8.5 %collective-permute-start.16 = (f32[2,24,768]{2,1,0:T(8,128)}, f32[2,24,768]{2,1,0:T(8,128)}, u32[]{:S(2)}, u32[]{:S(2)}) collective-permute-start(f32[2,24,768]{2,1,0:T(8,128)} %bitcast.244), channel_id=1, source_target_pairs={{0,2},{1,3},{2,0},{3,1},{4,6},{5,7},{6,4},{7,5},{8,10},{9,11},{10,... | collective-permute-start | bytes 442376 | tf_op jit(solution)/shard_map/ppermute | solution.py:34
  37.5 10.5 %collective-permute-start.17 = (f32[2,24,768]{2,1,0:T(8,128)}, f32[2,24,768]{2,1,0:T(8,128)}, u32[]{:S(2)}, u32[]{:S(2)}) collective-permute-start(f32[2,24,768]{2,1,0:T(8,128)} %bitcast.243), channel_id=1, source_target_pairs={{0,1},{1,0},{2,3},{3,2},{4,5},{5,4},{6,7},{7,6},{8,9},{9,8},{10,11... | collective-permute-start | bytes 442376 | tf_op jit(solution)/shard_map/ppermute | solution.py:34
  39.9 4.5 %copy-start.11 = (f32[64,768]{1,0:T(8,128)S(1)}, f32[64,768]{1,0:T(8,128)}, u32[]{:S(2)}) copy-start(f32[64,768]{1,0:T(8,128)} %get-tuple-element.29) | copy-start | bytes 589828
  39.9 5.2 %copy-start.10 = (f32[96,768]{1,0:T(8,128)S(1)}, f32[96,768]{1,0:T(8,128)}, u32[]{:S(2)}) copy-start(f32[96,768]{1,0:T(8,128)} %get-tuple-element.20) | copy-start | bytes 884740
  39.9 8.1 %copy-start.9 = (f32[96,768]{1,0:T(8,128)S(1)}, f32[96,768]{1,0:T(8,128)}, u32[]{:S(2)}) copy-start(f32[96,768]{1,0:T(8,128)} %get-tuple-element.18) | copy-start | bytes 884740
  44.4 4.9 %copy-start.8 = (f32[96,768]{1,0:T(8,128)S(1)}, f32[96,768]{1,0:T(8,128)}, u32[]{:S(2)}) copy-start(f32[96,768]{1,0:T(8,128)} %get-tuple-element.17) | copy-start | bytes 884740
  44.4 6.6 %copy-start.7 = (f32[96,768]{1,0:T(8,128)S(1)}, f32[96,768]{1,0:T(8,128)}, u32[]{:S(2)}) copy-start(f32[96,768]{1,0:T(8,128)} %get-tuple-element.19) | copy-start | bytes 884740
  44.4 8.8 %collective-permute-start.26 = (f32[64,768]{1,0:T(8,128)S(1)}, f32[64,768]{1,0:T(8,128)S(1)}, u32[]{:S(2)}, u32[]{:S(2)}) collective-permute-start(f32[64,768]{1,0:T(8,128)S(1)} %copy-done.11), channel_id=1, source_target_pairs={{0,1},{1,0},{2,3},{3,2},{4,5},{5,4},{6,7},{7,6},{8,9},{9,8},{10,11... | collective-permute-start | bytes 589832 | tf_op jit(solution)/shard_map/ppermute | solution.py:34
  45.2 22.0 %collective-permute-start.4 = (f32[96,768]{1,0:T(8,128)S(1)}, f32[96,768]{1,0:T(8,128)S(1)}, u32[]{:S(2)}, u32[]{:S(2)}) collective-permute-start(f32[96,768]{1,0:T(8,128)S(1)} %copy-done.10), channel_id=1, source_target_pairs={{8,0},{16,8},{24,16},{0,24},{9,1},{17,9},{25,17},{1,25},{10,2},{18... | collective-permute-start | bytes 884744 | tf_op jit(solution)/shard_map/ppermute | solution.py:57
  48.0 25.8 %collective-permute-start.1 = (f32[96,768]{1,0:T(8,128)S(1)}, f32[96,768]{1,0:T(8,128)S(1)}, u32[]{:S(2)}, u32[]{:S(2)}) collective-permute-start(f32[96,768]{1,0:T(8,128)S(1)} %copy-done.9), channel_id=1, source_target_pairs={{0,8},{8,16},{16,24},{24,0},{1,9},{9,17},{17,25},{25,1},{2,10},{10... | collective-permute-start | bytes 884744 | tf_op jit(solution)/shard_map/ppermute | solution.py:57
  49.2 5.3 %copy-start.6 = (f32[4,64,64]{2,1,0:T(8,128)S(1)}, f32[4,64,64]{2,1,0:T(8,128)}, u32[]{:S(2)}) copy-start(f32[4,64,64]{2,1,0:T(8,128)} %pad_maximum_fusion.1) | copy-start | bytes 196612
  49.3 25.3 %collective-permute-start.3 = (f32[96,768]{1,0:T(8,128)S(1)}, f32[96,768]{1,0:T(8,128)S(1)}, u32[]{:S(2)}, u32[]{:S(2)}) collective-permute-start(f32[96,768]{1,0:T(8,128)S(1)} %copy-done.8), channel_id=1, source_target_pairs={{0,8},{8,16},{16,24},{24,0},{1,9},{9,17},{17,25},{25,1},{2,10},{10... | collective-permute-start | bytes 884744 | tf_op jit(solution)/shard_map/ppermute | solution.py:57
  51.0 16.1 %copy-start.4 = (f32[1,2,384,768]{3,2,1,0:T(8,128)S(1)}, f32[1,2,384,768]{3,2,1,0:T(8,128)}, u32[]{:S(2)}) copy-start(f32[1,2,384,768]{3,2,1,0:T(8,128)} %param.7) | copy-start | bytes 7077892
  51.0 69.3 %collective-permute-start = (f32[96,768]{1,0:T(8,128)S(1)}, f32[96,768]{1,0:T(8,128)S(1)}, u32[]{:S(2)}, u32[]{:S(2)}) collective-permute-start(f32[96,768]{1,0:T(8,128)S(1)} %copy-done.7), channel_id=1, source_target_pairs={{8,0},{16,8},{24,16},{0,24},{9,1},{17,9},{25,17},{1,25},{10,2},{18... | collective-permute-start | bytes 884744 | tf_op jit(solution)/shard_map/ppermute | solution.py:57
  67.2 20.9 %collective-permute-start.5 = (f32[96,768]{1,0:T(8,128)S(1)}, f32[96,768]{1,0:T(8,128)S(1)}, u32[]{:S(2)}, u32[]{:S(2)}) collective-permute-start(f32[96,768]{1,0:T(8,128)S(1)} %bitcast_add_fusion.2), channel_id=1, source_target_pairs={{8,0},{16,8},{24,16},{0,24},{9,1},{17,9},{25,17},{1,25},{10,2},{18... | collective-permute-start | bytes 884744 | tf_op jit(solution)/shard_map/ppermute | solution.py:57
  70.0 20.3 %collective-permute-start.27 = (f32[128,768]{1,0:T(8,128)S(1)}, f32[128,768]{1,0:T(8,128)S(1)}, u32[]{:S(2)}, u32[]{:S(2)}) collective-permute-start(f32[128,768]{1,0:T(8,128)S(1)} %get-tuple-element.27), channel_id=1, source_target_pairs={{0,8},{8,16},{16,24},{24,0},{1,9},{9,17},{17,25},{25,1},{2,10},{10... | collective-permute-start | bytes 1179656 | tf_op jit(solution)/shard_map/ppermute | solution.py:57
  73.8 37.7 %collective-permute-start.29 = (f32[128,768]{1,0:T(8,128)S(1)}, f32[128,768]{1,0:T(8,128)S(1)}, u32[]{:S(2)}, u32[]{:S(2)}) collective-permute-start(f32[128,768]{1,0:T(8,128)S(1)} %get-tuple-element.27), channel_id=1, source_target_pairs={{8,0},{16,8},{24,16},{0,24},{9,1},{17,9},{25,17},{1,25},{10,2},{18... | collective-permute-start | bytes 1179656 | tf_op jit(solution)/shard_map/ppermute | solution.py:57
  74.6 32.6 %collective-permute-start.28 = (f32[128,768]{1,0:T(8,128)S(1)}, f32[128,768]{1,0:T(8,128)S(1)}, u32[]{:S(2)}, u32[]{:S(2)}) collective-permute-start(f32[128,768]{1,0:T(8,128)S(1)} %get-tuple-element.25), channel_id=1, source_target_pairs={{0,8},{8,16},{16,24},{24,0},{1,9},{9,17},{17,25},{25,1},{2,10},{10... | collective-permute-start | bytes 1179656 | tf_op jit(solution)/shard_map/ppermute | solution.py:57
  88.1 27.5 %collective-permute-start.30 = (f32[128,768]{1,0:T(8,128)S(1)}, f32[128,768]{1,0:T(8,128)S(1)}, u32[]{:S(2)}, u32[]{:S(2)}) collective-permute-start(f32[128,768]{1,0:T(8,128)S(1)} %get-tuple-element.25), channel_id=1, source_target_pairs={{8,0},{16,8},{24,16},{0,24},{9,1},{17,9},{25,17},{1,25},{10,2},{18... | collective-permute-start | bytes 1179656 | tf_op jit(solution)/shard_map/ppermute | solution.py:57
  90.2 31.7 %collective-permute-start.2 = (f32[96,768]{1,0:T(8,128)S(1)}, f32[96,768]{1,0:T(8,128)S(1)}, u32[]{:S(2)}, u32[]{:S(2)}) collective-permute-start(f32[96,768]{1,0:T(8,128)S(1)} %get-tuple-element.16), channel_id=1, source_target_pairs={{0,8},{8,16},{16,24},{24,0},{1,9},{9,17},{17,25},{25,1},{2,10},{10... | collective-permute-start | bytes 884744 | tf_op jit(solution)/shard_map/ppermute | solution.py:57
  107.1 38.5 %collective-permute-start.21 = (f32[96,768]{1,0:T(8,128)}, f32[96,768]{1,0:T(8,128)}, u32[]{:S(2)}, u32[]{:S(2)}) collective-permute-start(f32[96,768]{1,0:T(8,128)} %get-tuple-element.6), channel_id=1, source_target_pairs={{8,0},{16,8},{24,16},{0,24},{9,1},{17,9},{25,17},{1,25},{10,2},{18... | collective-permute-start | bytes 884744 | tf_op jit(solution)/shard_map/ppermute | solution.py:57
  111.4 25.3 %collective-permute-start.31 = (f32[128,768]{1,0:T(8,128)S(1)}, f32[128,768]{1,0:T(8,128)S(1)}, u32[]{:S(2)}, u32[]{:S(2)}) collective-permute-start(f32[128,768]{1,0:T(8,128)S(1)} %collective-permute-done.27), channel_id=1, source_target_pairs={{0,8},{8,16},{16,24},{24,0},{1,9},{9,17},{17,25},{25,1},{2,10},{10... | collective-permute-start | bytes 1179656 | tf_op jit(solution)/shard_map/ppermute | solution.py:57
  115.6 27.5 %collective-permute-start.32 = (f32[128,768]{1,0:T(8,128)S(1)}, f32[128,768]{1,0:T(8,128)S(1)}, u32[]{:S(2)}, u32[]{:S(2)}) collective-permute-start(f32[128,768]{1,0:T(8,128)S(1)} %collective-permute-done.30), channel_id=1, source_target_pairs={{8,0},{16,8},{24,16},{0,24},{9,1},{17,9},{25,17},{1,25},{10,2},{18... | collective-permute-start | bytes 1179656 | tf_op jit(solution)/shard_map/ppermute | solution.py:57
  124.8 25.3 %copy-start.3 = (f32[2,384,768]{2,1,0:T(8,128)}, f32[2,384,768]{2,1,0:T(8,128)S(1)}, u32[]{:S(2)}) copy-start(f32[2,384,768]{2,1,0:T(8,128)S(1)} %bitcast_dynamic-update-slice_fusion.6) | copy-start | bytes 7077892
  124.9 21.0 %collective-permute-start.6 = (f32[2,24,768]{2,1,0:T(8,128)S(1)}, f32[2,24,768]{2,1,0:T(8,128)S(1)}, u32[]{:S(2)}, u32[]{:S(2)}) collective-permute-start(f32[2,24,768]{2,1,0:T(8,128)S(1)} %get-tuple-element.35), channel_id=1, source_target_pairs={{0,3},{1,2},{2,1},{3,0},{4,7},{5,6},{6,5},{7,4},{8,11},{9,10},{10,... | collective-permute-start | bytes 442376 | tf_op jit(solution)/shard_map/ppermute | solution.py:34
  125.0 24.5 %collective-permute-start.7 = (f32[2,24,768]{2,1,0:T(8,128)S(1)}, f32[2,24,768]{2,1,0:T(8,128)S(1)}, u32[]{:S(2)}, u32[]{:S(2)}) collective-permute-start(f32[2,24,768]{2,1,0:T(8,128)S(1)} %get-tuple-element.36), channel_id=1, source_target_pairs={{0,2},{1,3},{2,0},{3,1},{4,6},{5,7},{6,4},{7,5},{8,10},{9,11},{10,... | collective-permute-start | bytes 442376 | tf_op jit(solution)/shard_map/ppermute | solution.py:34
  136.7 13.4 %collective-permute-start.8 = (f32[2,24,768]{2,1,0:T(8,128)S(1)}, f32[2,24,768]{2,1,0:T(8,128)S(1)}, u32[]{:S(2)}, u32[]{:S(2)}) collective-permute-start(f32[2,24,768]{2,1,0:T(8,128)S(1)} %get-tuple-element.34), channel_id=1, source_target_pairs={{0,1},{1,0},{2,3},{3,2},{4,5},{5,4},{6,7},{7,6},{8,9},{9,8},{10,11... | collective-permute-start | bytes 442376 | tf_op jit(solution)/shard_map/ppermute | solution.py:34
  143.1 20.4 %collective-permute-start.19 = (f32[96,768]{1,0:T(8,128)}, f32[96,768]{1,0:T(8,128)}, u32[]{:S(2)}, u32[]{:S(2)}) collective-permute-start(f32[96,768]{1,0:T(8,128)} %get-tuple-element.6), channel_id=1, source_target_pairs={{0,8},{8,16},{16,24},{24,0},{1,9},{9,17},{17,25},{25,1},{2,10},{10... | collective-permute-start | bytes 884744 | tf_op jit(solution)/shard_map/ppermute | solution.py:57
  145.7 16.2 %collective-permute-start.18 = (f32[96,768]{1,0:T(8,128)}, f32[96,768]{1,0:T(8,128)}, u32[]{:S(2)}, u32[]{:S(2)}) collective-permute-start(f32[96,768]{1,0:T(8,128)} %get-tuple-element.8), channel_id=1, source_target_pairs={{0,8},{8,16},{16,24},{24,0},{1,9},{9,17},{17,25},{25,1},{2,10},{10... | collective-permute-start | bytes 884744 | tf_op jit(solution)/shard_map/ppermute | solution.py:57
  145.9 20.6 %collective-permute-start.20 = (f32[96,768]{1,0:T(8,128)}, f32[96,768]{1,0:T(8,128)}, u32[]{:S(2)}, u32[]{:S(2)}) collective-permute-start(f32[96,768]{1,0:T(8,128)} %get-tuple-element.8), channel_id=1, source_target_pairs={{8,0},{16,8},{24,16},{0,24},{9,1},{17,9},{25,17},{1,25},{10,2},{18... | collective-permute-start | bytes 884744 | tf_op jit(solution)/shard_map/ppermute | solution.py:57
  149.5 30.2 %collective-permute-start.23 = (f32[96,768]{1,0:T(8,128)}, f32[96,768]{1,0:T(8,128)}, u32[]{:S(2)}, u32[]{:S(2)}) collective-permute-start(f32[96,768]{1,0:T(8,128)} %collective-permute-done.21), channel_id=1, source_target_pairs={{8,0},{16,8},{24,16},{0,24},{9,1},{17,9},{25,17},{1,25},{10,2},{18... | collective-permute-start | bytes 884744 | tf_op jit(solution)/shard_map/ppermute | solution.py:57
  161.8 17.1 %collective-permute-start.22 = (f32[96,768]{1,0:T(8,128)}, f32[96,768]{1,0:T(8,128)S(1)}, u32[]{:S(2)}, u32[]{:S(2)}) collective-permute-start(f32[96,768]{1,0:T(8,128)} %collective-permute-done.18), channel_id=1, source_target_pairs={{0,8},{8,16},{16,24},{24,0},{1,9},{9,17},{17,25},{25,1},{2,10},{10... | collective-permute-start | bytes 884744 | tf_op jit(solution)/shard_map/ppermute | solution.py:57

commit v2 on v0

v2 whole, which is shorter than its diff:
```python
import functools

import jax
import jax.numpy as jnp
from jax import lax
from jax.experimental import pallas as pl
from jax.experimental.pallas import tpu as pltpu
from jax.sharding import PartitionSpec as P

momentum = 0.9
outer_rate = 0.7
grad_weight = outer_rate * (1.0 + momentum)
moment_weight = outer_rate * momentum * momentum
vmem_limit = 48 * 1024 * 1024
f32 = jnp.float32
any_spec = pl.BlockSpec(memory_space=pl.ANY)
vmem_spec = pl.BlockSpec(memory_space=pltpu.VMEM)


def mul_t(a, b):
    return lax.dot_general(
        a, b, (((1,), (1,)), ((), ())), precision=lax.Precision.HIGHEST, preferred_element_type=f32
    )


def mul(a, b):
    return jnp.dot(a, b, precision=lax.Precision.HIGHEST, preferred_element_type=f32)


def shaped(*shape):
    return jax.ShapeDtypeStruct(shape, f32)


def call(body, outs, n_in, scratch=(), flops=0, size=0):
    return pl.pallas_call(
        body,
        out_shape=outs,
        in_specs=[vmem_spec] * n_in,
        out_specs=jax.tree.map(lambda _: vmem_spec, outs),
        scratch_shapes=scratch,
        compiler_params=pltpu.CompilerParams(vmem_limit_bytes=vmem_limit),
        cost_estimate=pl.CostEstimate(flops=flops, bytes_accessed=size, transcendentals=0),
    )


def wide_basis(basis):
    zero = jnp.zeros_like(basis)
    return jnp.concatenate([basis, zero]), jnp.concatenate([zero, basis])


def project_body(count, groups, pieces, me_ref, x_ref, basis_ref, *out_refs):
    step = pl.program_id(0)
    first, second = wide_basis(basis_ref[...])
    rows, width = x_ref.shape[1:]
    x = x_ref[0].reshape(pieces, 2, rows // pieces // 2, width)
    y = mul_t(x[:, 0].reshape(-1, width), first) + mul_t(x[:, 1].reshape(-1, width), second)
    y = y.reshape(pieces, rows // pieces // 2, -1)
    for i in range(count):

        @pl.when(step == i)
        def _(i=i):
            out_refs[i][...] = y


def project(inner_emb, basis, me, groups, pieces):
    rows, width = inner_emb.shape[1] // groups, inner_emb.shape[2]
    rank = basis.shape[0]
    shape = (pieces, rows // pieces // 2, 2 * rank)

    def source(i, me):
        return 0, me[0] ^ (groups - 1 - i), 0

    return pl.pallas_call(
        functools.partial(project_body, 4, groups, pieces),
        out_shape=[shaped(*shape)] * 4,
        grid_spec=pltpu.PrefetchScalarGridSpec(
            num_scalar_prefetch=1,
            grid=(4,),
            in_specs=[
                pl.BlockSpec((1, rows, width), source),
                pl.BlockSpec((rank, width), lambda i, me: (0, 0)),
            ],
            out_specs=[pl.BlockSpec(shape, lambda i, me: (0, 0, 0))] * 4,
        ),
        compiler_params=pltpu.CompilerParams(vmem_limit_bytes=vmem_limit),
        cost_estimate=pl.CostEstimate(
            flops=12 * groups * rows * width * rank,
            bytes_accessed=4 * groups * rows * (width + rank),
            transcendentals=0,
        ),
    )(me, inner_emb, basis)


def emb_base_body(outer_ref, moment_ref, basis_ref, base_ref, proj_ref):
    shape = base_ref.shape
    outer = outer_ref[0, :, 0].reshape(-1, shape[-1])
    moment = moment_ref[0, :, 0].reshape(-1, shape[-1])
    basis = basis_ref[...]
    proj = mul_t(outer, basis)
    proj_ref[...] = proj
    base = outer - moment_weight * moment - grad_weight * mul(proj, basis)
    base_ref[...] = base.reshape(shape)


def emb_block_body(scale, base_ref, p0, p1, p2, p3, basis_ref, block_ref, sum_ref):
    total = p0[...] + p1[...] + p2[...] + p3[...]
    sum_ref[...] = total
    pieces, half, wide = total.shape
    flat = total.reshape(pieces * half, wide)
    first, second = wide_basis(basis_ref[...])
    base = base_ref[...]
    block_ref[:, 0] = base[:, 0] + scale * mul(flat, first).reshape(pieces, half, -1)
    block_ref[:, 1] = base[:, 1] + scale * mul(flat, second).reshape(pieces, half, -1)


def emb_state_body(scale, outer_ref, moment_ref, proj_ref, back_ref, basis_ref, new_ref, moment_new_ref):
    pieces, half, wide = back_ref.shape
    basis = basis_ref[...]
    first, second = wide_basis(basis)
    flat = back_ref[...].reshape(pieces * half, wide)
    outer = outer_ref[0, :, 0]
    width = outer.shape[-1]
    own = mul(proj_ref[...], basis).reshape(pieces, 2, half, width)
    grad = jnp.concatenate(
        [
            own[:, i : i + 1] - scale * mul(flat, part).reshape(pieces, 1, half, width)
            for i, part in ((0, first), (1, second))
        ],
        axis=1,
    ).reshape(outer.shape)
    moment_new = momentum * moment_ref[0, :, 0] + grad
    moment_new_ref[0, :, 0] = moment_new
    new_ref[0, :, 0] = outer - outer_rate * (grad + momentum * moment_new)


def per_device(inner_dense, inner_emb, outer_dense, moment_dense, outer_emb, moment_emb, basis):
    groups = lax.axis_size("rep")
    tp_count = lax.axis_size("tp")
    me = lax.axis_index("rep")

    def send(x, d):
        return lax.ppermute(x, "rep", [(i, i ^ d) for i in range(groups)])

    def meet(*xs):
        return lax.optimization_barrier(xs)

    def swap(x):
        return lax.all_to_all(x, "tp", split_axis=0, concat_axis=0, tiled=True)

    rank, width = basis.shape
    dense = inner_dense[0]
    cols = dense.shape[2]
    block_rows = dense.shape[1] // groups
    flat_rows = outer_dense.shape[2]
    piece_rows = outer_emb.shape[3]
    half_rows = piece_rows // 2
    emb_rows = tp_count * piece_rows
    weight = grad_weight / groups

    def block(d):
        return lax.dynamic_slice(dense, (0, (me ^ d) * block_rows, 0), (2, block_rows, cols))

    far, inner_emb, outer_emb, outer_dense = meet(block(3), inner_emb, outer_emb, outer_dense)
    far = send(far, 1)

    p3, p2, p1, p0 = project(inner_emb, basis, me.reshape(1).astype(jnp.int32), groups, tp_count)
    emb_base, outer_proj = call(
        emb_base_body,
        [shaped(tp_count, piece_rows, width), shaped(emb_rows, rank)],
        3,
        flops=24 * emb_rows * width * rank,
        size=12 * emb_rows * width,
    )(outer_emb, moment_emb, basis)
    far, p3, p2, p1, emb_base = meet(far, p3, p2, p1, emb_base)
    p3, p2, p1 = send(p3, 3), send(p2, 2), send(p1, 1)
    emb_base = swap(emb_base)
    across = send(block(2) + far, 2)
    near = send(block(1), 1)
    dense_outer = outer_dense[:, 0]
    dense_moment = moment_dense[:, 0]
    dense_base = (1.0 - grad_weight) * dense_outer - moment_weight * dense_moment
    dense_base = jnp.stack([dense_base[:, :, j * cols : (j + 1) * cols] for j in range(tp_count)])

    emb_block, proj_sum = call(
        functools.partial(emb_block_body, weight),
        [shaped(tp_count, 2, half_rows, width), shaped(tp_count, half_rows, 2 * rank)],
        6,
        flops=24 * emb_rows * width * rank,
        size=8 * emb_rows * width,
    )(emb_base.reshape(tp_count, 2, half_rows, width), p0, p1, p2, p3, basis)
    emb_block, proj_sum, dense_base = meet(emb_block, proj_sum, dense_base)
    dense_base = swap(dense_base)
    across, near, emb_block = meet(across, near, emb_block)
    dense_sum = block(0) + near + across
    emb_block = emb_block.reshape(emb_rows, width)
    dense_block = (
        dense_base.transpose(1, 0, 2, 3).reshape(2, block_rows, cols) + weight * dense_sum
    )

    def gather(x):
        second = send(x, 2)
        first = send(x, 1)
        return x, first, second, send(second, 1)

    emb_all = gather(emb_block)
    dense_all = gather(dense_block)
    embed_train = jnp.zeros((groups * emb_rows, width), f32)
    for d, value in enumerate(emb_all):
        embed_train = lax.dynamic_update_slice(embed_train, value, ((me ^ d) * emb_rows, 0))
    dense_train = jnp.zeros(dense.shape, f32)
    for d, value in enumerate(dense_all):
        dense_train = lax.dynamic_update_slice(dense_train, value, (0, (me ^ d) * block_rows, 0))

    dense_back = swap(dense_sum.reshape(2, tp_count, flat_rows, cols).transpose(1, 0, 2, 3))
    dense_back = jnp.concatenate([dense_back[j] for j in range(tp_count)], axis=-1)
    grad_dense = dense_outer - dense_back / groups
    moment_new = momentum * dense_moment + grad_dense
    dense_new = dense_outer - outer_rate * (grad_dense + momentum * moment_new)
    emb_new, emb_moment_new = call(
        functools.partial(emb_state_body, 1.0 / groups),
        [shaped(*outer_emb.shape)] * 2,
        5,
        flops=36 * emb_rows * width * rank,
        size=16 * emb_rows * width,
    )(outer_emb, moment_emb, outer_proj, swap(proj_sum), basis)
    return (
        dense_new[:, None],
        moment_new[:, None],
        emb_new,
        emb_moment_new,
        dense_train,
        embed_train,
    )


def solution(mesh):
    in_specs = (
        P("rep", None, "shard", "tp"),
        P("rep", ("shard", "tp"), None),
        P(None, "shard", ("rep", "tp"), None),
        P(None, "shard", ("rep", "tp"), None),
        P("shard", None, ("rep", "tp"), None, None),
        P("shard", None, ("rep", "tp"), None, None),
        P(),
    )
    out_specs = (
        P(None, "shard", ("rep", "tp"), None),
        P(None, "shard", ("rep", "tp"), None),
        P("shard", None, ("rep", "tp"), None, None),
        P("shard", None, ("rep", "tp"), None, None),
        P(None, "shard", "tp"),
        P(("shard", "tp"), None),
    )
    return jax.shard_map(
        per_device, mesh=mesh, in_specs=in_specs, out_specs=out_specs, check_vma=False
    )
```

time: 335 us -> 166 us (0.50)
  blocking collectives: 89.4 us -> 0 us
  waiting for transfers between devices: 140 us -> 87.3 us
  local copies, waits for them, and re-layouts: 51.7 us -> 24.3 us
  starting transfers between devices: 7.7 us -> 34.6 us
  other arithmetic: 28.3 us -> 7.72 us
  between operations: 14.2 us -> 0.88 us
  Pallas kernels: 0 us -> 9.95 us
    all_to_all x2 -> x0, blocking collectives: 89.4 us -> none  [the longest x1 61.2 us: per_device(): lax.all_to_all(dense_local, ('rep', 'tp'), split_axis=1, concat_axis=2, t...]
    ppermute x0 -> x12, waiting for transfers between devices: none -> 81.4 us  [send(): return lax.ppermute(x, 'rep', [(i, i ^ d) for i in range(groups)])]
    all_gather x2 -> x0, waiting for transfers between devices: 70.9 us -> none  [the longest x1 70.9 us: per_device(): lax.all_gather(embed_cols, 'rep', axis=1, tiled=True)]
    all_to_all x2 -> x4, waiting for transfers between devices: 69.3 us -> 5.94 us  [swap(): return lax.all_to_all(x, 'tp', split_axis=0, concat_axis=0, tiled=True)]
    unnamed x31 -> x34, local copies, waits for them, and re-layouts: 36.4 us -> 8.34 us
    ppermute x0 -> x12, starting transfers between devices: none -> 20.9 us  [send(): return lax.ppermute(x, 'rep', [(i, i ^ d) for i in range(groups)])]
    unnamed x2 -> x0, other arithmetic: 14.9 us -> none
    dynamic_update_slice x0 -> x8, local copies, waits for them, and re-layouts: none -> 10.5 us  [the longest x4 7.12 us: per_device(): lax.dynamic_update_slice(embed_train, value, ((me ^ d) * emb_rows, 0))]
  transfers between devices with their start and end apart: 4 -> 16, of which waited for: 3 -> 10; matrix products, arithmetic and copies ran while one was open for 16% -> 13% of each run, Pallas kernels for 0% -> 6%
where the time goes in v2:
time: 166 us; the launch traced here: 165 us
  waiting for transfers between devices  87.3 us (53%)
  starting transfers between devices  34.6 us (21%)
  local copies, waits for them, and re-layouts  24.3 us (15%)
  Pallas kernels  9.95 us (6%)
  other arithmetic  7.72 us (5%)
    ppermute x12, waiting for transfers between devices, send(): return lax.ppermute(x, 'rep', [(i, i ^ d) for i in range(groups)])  81.4 us
    ppermute x12, starting transfers between devices, send(): return lax.ppermute(x, 'rep', [(i, i ^ d) for i in range(groups)])  20.9 us
    all_to_all x4, starting transfers between devices, swap(): return lax.all_to_all(x, 'tp', split_axis=0, concat_axis=0, tiled=True)  13.7 us
    unnamed x34, local copies, waits for them, and re-layouts  8.34 us
    dynamic_update_slice x4, local copies, waits for them, and re-layouts, per_device(): lax.dynamic_update_slice(embed_train, value, ((me ^ d) * emb_rows, 0))  7.12 us
    all_to_all x4, waiting for transfers between devices, swap(): return lax.all_to_all(x, 'tp', split_axis=0, concat_axis=0, tiled=True)  5.94 us
    pallas_call x1, Pallas kernels, per_device(): call(emb_base_body, [shaped(tp_count, piece_rows, width), shaped(emb_rows...  3.49 us
    dynamic_update_slice x4, local copies, waits for them, and re-layouts, per_device(): lax.dynamic_update_slice(dense_train, value, (0, (me ^ d) * block_rows, 0))  3.37 us
  transfers between devices with their start and end apart: 16, of which 10 were waited for; matrix products, arithmetic and copies ran while one was open for 13% of the time, Pallas kernels for 6%

profile of v2, /device:TPU:0, one launch (start us, length us, event | category | flops | bytes accessed | tf_op | source)
XLA Modules:
  0.0 164.8 jit_solution(3512217598117557707)
XLA Ops:
  0.7 2.5 %dynamic-slice_bitcast_fusion = (f32[2,96,768]{2,1,0:T(8,128)}, f32[2,96,768]{2,1,0:T(8,128)}) fusion(f32[1,2,384,768]{3,2,1,0:T(8,128)} %param.7, s32[]{:T(128)S(6)} %select_n.31, s32[]{:T(128)S(6)} %select_n.28), kind=kLoop, calls=%fused_computation.11 | loop fusion | bytes 2359304 | tf_op jit(solution)/shard_map/dynamic_slice | solution.py:161
  3.1 3.0 %collective-permute-start = (f32[2,96,768]{2,1,0:T(8,128)}, f32[2,96,768]{2,1,0:T(8,128)}, u32[]{:S(2)}, u32[]{:S(2)}) collective-permute-start(f32[2,96,768]{2,1,0:T(8,128)} %get-tuple-element.32), channel_id=1, source_target_pairs={{0,8},{8,0},{16,24},{24,16},{1,9},{9,1},{17,25},{25,17},{2,10},{10... | collective-permute-start | bytes 1769480 | tf_op jit(solution)/shard_map/ppermute | solution.py:142
  6.2 1.9 %copy-done.2 = f32[1,1024,768]{2,1,0:T(8,128)S(1)} copy-done((f32[1,1024,768]{2,1,0:T(8,128)S(1)}, f32[1,1024,768]{2,1,0:T(8,128)}, u32[]{:S(2)}) %copy-start.2) | copy-done | bytes 3145752
  8.1 3.1 %shard_map.118 = (f32[4,32,128]{2,1,0:T(8,128)S(1)}, f32[4,32,128]{2,1,0:T(8,128)S(1)}, f32[4,32,128]{2,1,0:T(8,128)S(1)}, f32[4,32,128]{2,1,0:T(8,128)S(1)}) custom-call(s32[1]{0:T(128)} %bitcast.3.me_ref, f32[1,1024,768]{2,1,0:T(8,128)S(1)} %copy-done.2, f32[64,768]{1,0:T(8,128)S(1)} %copy-done.3), custom_call_target="tpu_custom_call" | custom-call | flops 603979776 | bytes 3407872 | tf_op jit(solution)/shard_map/pallas_call | solution.py:73
  11.2 3.5 %shard_map.119 = (f32[4,64,768]{2,1,0:T(8,128)}, f32[256,64]{1,0:T(8,128)S(1)}) custom-call(f32[1,4,1,64,768]{4,3,2,1,0:T(8,128)S(1)} %copy-done, f32[1,4,1,64,768]{4,3,2,1,0:T(8,128)S(1)} %copy-done.1, f32[64,768]{1,0:T(8,128)S(1)} %copy-done.3), custom_call_target="tpu_custom_call" | custom-call | flops 301989888 | bytes 2359296 | tf_op jit(solution)/shard_map/pallas_call | solution.py:167
  14.7 1.2 subtract_bitcast_fusion
  15.9 4.7 %collective-permute-done = f32[2,96,768]{2,1,0:T(8,128)} collective-permute-done((f32[2,96,768]{2,1,0:T(8,128)}, f32[2,96,768]{2,1,0:T(8,128)}, u32[]{:S(2)}, u32[]{:S(2)}) %collective-permute-start) | collective-permute-done | bytes 589856 | tf_op jit(solution)/shard_map/ppermute | solution.py:142
  20.6 3.5 %all-to-all-start = ((f32[4,64,768]{2,1,0:T(8,128)}), f32[4,64,768]{2,1,0:T(8,128)S(1)}, u32[]{:S(2)}, u32[]{:S(2)}) async-start(f32[4,64,768]{2,1,0:T(8,128)} %get-tuple-element.40), calls=%async_computation | async-start | bytes 1572864 | tf_op jit(solution)/shard_map/all_to_all | solution.py:148
  24.1 2.1 %bitcast_add_fusion.1 = f32[2,96,768]{2,1,0:T(8,128)} fusion(f32[2,96,768]{2,1,0:T(8,128)} %collective-permute-done, f32[1,2,384,768]{3,2,1,0:T(8,128)} %param.7, s32[]{:T(128)S(6)} %select_n.30), kind=kLoop, calls=%fused_computation.4 | loop fusion | flops 147456 | bytes 1769476 | tf_op jit(solution)/shard_map/add | solution.py:177
  26.3 3.1 %collective-permute-start.1 = (f32[2,96,768]{2,1,0:T(8,128)}, f32[2,96,768]{2,1,0:T(8,128)}, u32[]{:S(2)}, u32[]{:S(2)}) collective-permute-start(f32[2,96,768]{2,1,0:T(8,128)} %bitcast_add_fusion.1), channel_id=1, source_target_pairs={{0,16},{8,24},{16,0},{24,8},{1,17},{9,25},{17,1},{25,9},{2,18},{10... | collective-permute-start | bytes 1769480 | tf_op jit(solution)/shard_map/ppermute | solution.py:142
  29.4 1.6 collective-permute-start.3
  31.4 2.5 %collective-permute-start.5 = (f32[4,32,128]{2,1,0:T(8,128)S(1)}, f32[4,32,128]{2,1,0:T(8,128)S(1)}, u32[]{:S(2)}, u32[]{:S(2)}) collective-permute-start(f32[4,32,128]{2,1,0:T(8,128)S(1)} %get-tuple-element.44), channel_id=1, source_target_pairs={{0,24},{8,16},{16,8},{24,0},{1,25},{9,17},{17,9},{25,1},{2,26},{10... | collective-permute-start | bytes 196616 | tf_op jit(solution)/shard_map/ppermute | solution.py:142
  33.8 0.9 pad_maximum_fusion
  34.7 12.1 %collective-permute-done.3.p1 = f32[4,32,128]{2,1,0:T(8,128)S(1)} collective-permute-done((f32[4,32,128]{2,1,0:T(8,128)S(1)}, f32[4,32,128]{2,1,0:T(8,128)S(1)}, u32[]{:S(2)}, u32[]{:S(2)}) %collective-permute-start.3) | collective-permute-done | bytes 65568 | tf_op jit(solution)/shard_map/ppermute | solution.py:142
  47.5 13.2 %collective-permute-done.4.p2 = f32[4,32,128]{2,1,0:T(8,128)S(1)} collective-permute-done((f32[4,32,128]{2,1,0:T(8,128)S(1)}, f32[4,32,128]{2,1,0:T(8,128)S(1)}, u32[]{:S(2)}, u32[]{:S(2)}) %collective-permute-start.4) | collective-permute-done | bytes 65568 | tf_op jit(solution)/shard_map/ppermute | solution.py:142
  60.6 0.6 copy-done.6
  61.9 0.8 copy-done.5
  62.7 0.8 copy-done.7
  63.6 0.8 copy-done.9
  64.4 0.8 shard_map.120
  65.8 3.5 %all-to-all-start.3 = ((f32[4,2,24,768]{3,2,1,0:T(8,128)}), f32[4,2,24,768]{3,2,1,0:T(8,128)S(1)}, u32[]{:S(2)}, u32[]{:S(2)}) async-start(f32[4,2,24,768]{3,2,1,0:T(8,128)} %pad_maximum_fusion), calls=%async_computation.3 | async-start | bytes 1179648 | tf_op jit(solution)/shard_map/all_to_all | solution.py:148
  69.3 3.4 %collective-permute-start.10 = (f32[256,768]{1,0:T(8,128)S(1)}, f32[256,768]{1,0:T(8,128)}, u32[]{:S(2)}, u32[]{:S(2)}) collective-permute-start(f32[256,768]{1,0:T(8,128)S(1)} %bitcast.46), channel_id=1, source_target_pairs={{0,16},{8,24},{16,0},{24,8},{1,17},{9,25},{17,1},{25,9},{2,18},{10... | collective-permute-start | bytes 2359304 | tf_op jit(solution)/shard_map/ppermute | solution.py:142
  72.7 1.0 collective-permute-start.9
  73.6 5.2 %all-to-all-done.3 = f32[4,2,24,768]{3,2,1,0:T(8,128)S(1)} async-done(((f32[4,2,24,768]{3,2,1,0:T(8,128)}), f32[4,2,24,768]{3,2,1,0:T(8,128)S(1)}, u32[]{:S(2)}, u32[]{:S(2)}) %all-to-all-start.3) | async-done | bytes 589856 | tf_op jit(solution)/shard_map/all_to_all | solution.py:148
  78.8 3.3 %all-to-all-start.2 = ((f32[4,32,128]{2,1,0:T(8,128)}), f32[4,32,128]{2,1,0:T(8,128)S(1)}, u32[]{:S(2)}, u32[]{:S(2)}) async-start(f32[4,32,128]{2,1,0:T(8,128)} %copy-done.10), calls=%async_computation.2 | async-start | bytes 131072 | tf_op jit(solution)/shard_map/all_to_all | solution.py:148
  82.1 2.4 %bitcast_add_fusion = (f32[2,96,768]{2,1,0:T(8,128)}, f32[2,96,768]{2,1,0:T(8,128)S(1)}) fusion(f32[2,4,24,768]{3,2,1,0:T(8,128)S(1)} %copy.17, f32[2,96,768]{2,1,0:T(8,128)} %collective-permute-done.1, f32[2,96,768]{2,1,0:T(8,128)} %collective-permute-done.2, f32[1,2,384,768]{3,2,1,0:T(8,128)} %param.7, s32[]{:T(128)S(6)} %select_n.29), kind=kLoop, calls=%fused_computation.3 | loop fusion | flops 589824 | bytes 3538948 | tf_op jit(solution)/shard_map/add | solution.py:197
  84.5 0.9 copy.19
  85.4 0.8 all-to-all-done.2.back_ref
  86.2 3.5 %all-to-all-start.1 = ((f32[4,2,24,768]{3,2,1,0:T(8,128)}), f32[4,2,24,768]{3,2,1,0:T(8,128)S(1)}, u32[]{:S(2)}, u32[]{:S(2)}) async-start(f32[4,2,24,768]{3,2,1,0:T(8,128)} %bitcast.50), calls=%async_computation.1 | async-start | bytes 1179648 | tf_op jit(solution)/shard_map/all_to_all | solution.py:148
  89.7 1.9 %broadcast_in_dim.9 = f32[1024,768]{1,0:T(8,128)} broadcast(f32[]{:T(128)} %constant.37.clone.1), dimensions={} | broadcast | bytes 3145732 | tf_op jit(solution)/shard_map/broadcast_in_dim | solution.py:207
  91.5 0.9 constant_dynamic-update-slice_fusion.3
  92.5 2.6 %shard_map.121 = (f32[1,4,1,64,768]{4,3,2,1,0:T(8,128)}, f32[1,4,1,64,768]{4,3,2,1,0:T(8,128)}) custom-call(f32[1,4,1,64,768]{4,3,2,1,0:T(8,128)S(1)} %copy-done, f32[1,4,1,64,768]{4,3,2,1,0:T(8,128)S(1)} %copy-done.1, f32[256,64]{1,0:T(8,128)S(1)} %get-tuple-element.50.proj_ref, f32[4,32,128]{2,1,0:T(8,128)S(1)} %all-to-all-done.2.back_ref, ...), custom_call_target="tpu_custom_call" | custom-call | flops 452984832 | bytes 3145728 | tf_op jit(solution)/shard_map/pallas_call | solution.py:219
  95.0 1.3 collective-permute-start.6
  96.4 2.9 %collective-permute-start.7 = (f32[2,96,768]{2,1,0:T(8,128)}, f32[2,96,768]{2,1,0:T(8,128)}, u32[]{:S(2)}, u32[]{:S(2)}) collective-permute-start(f32[2,96,768]{2,1,0:T(8,128)} %get-tuple-element.56), channel_id=1, source_target_pairs={{0,16},{8,24},{16,0},{24,8},{1,17},{9,25},{17,1},{25,9},{2,18},{10... | collective-permute-start | bytes 1769480 | tf_op jit(solution)/shard_map/ppermute | solution.py:142
  99.4 1.1 constant_dynamic-update-slice_fusion.7
  100.6 7.5 %collective-permute-done.10 = f32[256,768]{1,0:T(8,128)} collective-permute-done((f32[256,768]{1,0:T(8,128)S(1)}, f32[256,768]{1,0:T(8,128)}, u32[]{:S(2)}, u32[]{:S(2)}) %collective-permute-start.10) | collective-permute-done | bytes 786464 | tf_op jit(solution)/shard_map/ppermute | solution.py:142
  108.4 13.7 %collective-permute-done.9 = f32[256,768]{1,0:T(8,128)} collective-permute-done((f32[256,768]{1,0:T(8,128)S(1)}, f32[256,768]{1,0:T(8,128)}, u32[]{:S(2)}, u32[]{:S(2)}) %collective-permute-start.9) | collective-permute-done | bytes 786464 | tf_op jit(solution)/shard_map/ppermute | solution.py:142
  122.1 2.1 %constant_dynamic-update-slice_fusion.2 = f32[1024,768]{1,0:T(8,128)} fusion(f32[1024,768]{1,0:T(8,128)} %constant_dynamic-update-slice_fusion.3, f32[256,768]{1,0:T(8,128)} %collective-permute-done.9, s32[]{:T(128)S(6)} %select_n.33), kind=kLoop, calls=%fused_computation.23 | loop fusion | bytes 1572868 | tf_op jit(solution)/shard_map/dynamic_update_slice | solution.py:209
  124.1 2.1 %constant_dynamic-update-slice_fusion.1 = f32[1024,768]{1,0:T(8,128)} fusion(f32[1024,768]{1,0:T(8,128)} %constant_dynamic-update-slice_fusion.2, f32[256,768]{1,0:T(8,128)} %collective-permute-done.10, s32[]{:T(128)S(6)} %select_n.34), kind=kLoop, calls=%fused_computation.22 | loop fusion | bytes 1572868 | tf_op jit(solution)/shard_map/dynamic_update_slice | solution.py:209
  126.2 6.6 %collective-permute-done.7 = f32[2,96,768]{2,1,0:T(8,128)} collective-permute-done((f32[2,96,768]{2,1,0:T(8,128)}, f32[2,96,768]{2,1,0:T(8,128)}, u32[]{:S(2)}, u32[]{:S(2)}) %collective-permute-start.7) | collective-permute-done | bytes 589856 | tf_op jit(solution)/shard_map/ppermute | solution.py:142
  132.8 1.4 collective-permute-start.8
  134.2 1.2 multiply_subtract_fusion
  135.4 1.1 constant_dynamic-update-slice_fusion.6
  136.5 1.1 constant_dynamic-update-slice_fusion.5
  137.7 13.9 %collective-permute-done.11 = f32[256,768]{1,0:T(8,128)} collective-permute-done((f32[256,768]{1,0:T(8,128)}, f32[256,768]{1,0:T(8,128)}, u32[]{:S(2)}, u32[]{:S(2)}) %collective-permute-start.11) | collective-permute-done | bytes 786464 | tf_op jit(solution)/shard_map/ppermute | solution.py:142
  151.6 2.1 %constant_dynamic-update-slice_fusion = f32[1024,768]{1,0:T(8,128)} fusion(f32[1024,768]{1,0:T(8,128)} %constant_dynamic-update-slice_fusion.1, f32[256,768]{1,0:T(8,128)} %collective-permute-done.11, s32[]{:T(128)S(6)} %select_n.35), kind=kLoop, calls=%fused_computation.21 | loop fusion | bytes 1572868 | tf_op jit(solution)/shard_map/dynamic_update_slice | solution.py:209
  153.6 9.7 %collective-permute-done.8 = f32[2,96,768]{2,1,0:T(8,128)S(1)} collective-permute-done((f32[2,96,768]{2,1,0:T(8,128)}, f32[2,96,768]{2,1,0:T(8,128)S(1)}, u32[]{:S(2)}, u32[]{:S(2)}) %collective-permute-start.8) | collective-permute-done | bytes 589856 | tf_op jit(solution)/shard_map/ppermute | solution.py:142
  163.4 1.4 copy-done.13
  (42 shorter events, 2.9 us)
Async XLA Ops:
  0.6 5.6 %copy-start.3 = (f32[64,768]{1,0:T(8,128)S(1)}, f32[64,768]{1,0:T(8,128)}, u32[]{:S(2)}) copy-start(f32[64,768]{1,0:T(8,128)} %basis_ref.7) | copy-start | bytes 589828
  0.7 10.6 %copy-start = (f32[1,4,1,64,768]{4,3,2,1,0:T(8,128)S(1)}, f32[1,4,1,64,768]{4,3,2,1,0:T(8,128)}, u32[]{:S(2)}) copy-start(f32[1,4,1,64,768]{4,3,2,1,0:T(8,128)} %outer_ref.1) | copy-start | bytes 2359300
  0.7 10.6 %copy-start.1 = (f32[1,4,1,64,768]{4,3,2,1,0:T(8,128)S(1)}, f32[1,4,1,64,768]{4,3,2,1,0:T(8,128)}, u32[]{:S(2)}) copy-start(f32[1,4,1,64,768]{4,3,2,1,0:T(8,128)} %moment_ref.3) | copy-start | bytes 2359300
  3.1 17.5 %collective-permute-start = (f32[2,96,768]{2,1,0:T(8,128)}, f32[2,96,768]{2,1,0:T(8,128)}, u32[]{:S(2)}, u32[]{:S(2)}) collective-permute-start(f32[2,96,768]{2,1,0:T(8,128)} %get-tuple-element.32), channel_id=1, source_target_pairs={{0,8},{8,0},{16,24},{24,16},{1,9},{9,1},{17,25},{25,17},{2,10},{10... | collective-permute-start | bytes 1769480 | tf_op jit(solution)/shard_map/ppermute | solution.py:142
  6.2 63.1 %collective-permute-start.2 = (f32[2,96,768]{2,1,0:T(8,128)}, f32[2,96,768]{2,1,0:T(8,128)}, u32[]{:S(2)}, u32[]{:S(2)}) collective-permute-start(f32[2,96,768]{2,1,0:T(8,128)} %get-tuple-element.60), channel_id=1, source_target_pairs={{0,8},{8,0},{16,24},{24,16},{1,9},{9,1},{17,25},{25,17},{2,10},{10... | collective-permute-start | bytes 1769480 | tf_op jit(solution)/shard_map/ppermute | solution.py:142
  6.2 1.9 %copy-start.2 = (f32[1,1024,768]{2,1,0:T(8,128)S(1)}, f32[1,1024,768]{2,1,0:T(8,128)}, u32[]{:S(2)}) copy-start(f32[1,1024,768]{2,1,0:T(8,128)} %x_ref) | copy-start | bytes 9437188
  8.1 6.6 %copy-start.14 = (f32[2,1,24,3072]{3,2,1,0:T(8,128)S(1)}, f32[2,1,24,3072]{3,2,1,0:T(8,128)}, u32[]{:S(2)}) copy-start(f32[2,1,24,3072]{3,2,1,0:T(8,128)} %param.9) | copy-start | bytes 1769476
  20.6 41.2 %all-to-all-start = ((f32[4,64,768]{2,1,0:T(8,128)}), f32[4,64,768]{2,1,0:T(8,128)S(1)}, u32[]{:S(2)}, u32[]{:S(2)}) async-start(f32[4,64,768]{2,1,0:T(8,128)} %get-tuple-element.40), calls=%async_computation | async-start | bytes 1572864 | tf_op jit(solution)/shard_map/all_to_all | solution.py:148
  26.3 43.0 %collective-permute-start.1 = (f32[2,96,768]{2,1,0:T(8,128)}, f32[2,96,768]{2,1,0:T(8,128)}, u32[]{:S(2)}, u32[]{:S(2)}) collective-permute-start(f32[2,96,768]{2,1,0:T(8,128)} %bitcast_add_fusion.1), channel_id=1, source_target_pairs={{0,16},{8,24},{16,0},{24,8},{1,17},{9,25},{17,1},{25,9},{2,18},{10... | collective-permute-start | bytes 1769480 | tf_op jit(solution)/shard_map/ppermute | solution.py:142
  29.4 17.4 %collective-permute-start.3 = (f32[4,32,128]{2,1,0:T(8,128)S(1)}, f32[4,32,128]{2,1,0:T(8,128)S(1)}, u32[]{:S(2)}, u32[]{:S(2)}) collective-permute-start(f32[4,32,128]{2,1,0:T(8,128)S(1)} %get-tuple-element.42), channel_id=1, source_target_pairs={{0,8},{8,0},{16,24},{24,16},{1,9},{9,1},{17,25},{25,17},{2,10},{10... | collective-permute-start | bytes 196616 | tf_op jit(solution)/shard_map/ppermute | solution.py:142
  31.0 29.6 %collective-permute-start.4 = (f32[4,32,128]{2,1,0:T(8,128)S(1)}, f32[4,32,128]{2,1,0:T(8,128)S(1)}, u32[]{:S(2)}, u32[]{:S(2)}) collective-permute-start(f32[4,32,128]{2,1,0:T(8,128)S(1)} %get-tuple-element.43), channel_id=1, source_target_pairs={{0,16},{8,24},{16,0},{24,8},{1,17},{9,25},{17,1},{25,9},{2,18},{10... | collective-permute-start | bytes 196616 | tf_op jit(solution)/shard_map/ppermute | solution.py:142
  31.4 29.9 %collective-permute-start.5 = (f32[4,32,128]{2,1,0:T(8,128)S(1)}, f32[4,32,128]{2,1,0:T(8,128)S(1)}, u32[]{:S(2)}, u32[]{:S(2)}) collective-permute-start(f32[4,32,128]{2,1,0:T(8,128)S(1)} %get-tuple-element.44), channel_id=1, source_target_pairs={{0,24},{8,16},{16,8},{24,0},{1,25},{9,17},{17,9},{25,1},{2,26},{10... | collective-permute-start | bytes 196616 | tf_op jit(solution)/shard_map/ppermute | solution.py:142
  46.8 0.6 copy-start.4
  60.6 0.6 copy-start.6
  61.3 0.6 copy-start.8
  61.9 0.8 copy-start.5
  62.7 0.8 copy-start.7
  63.6 0.8 copy-start.9
  65.2 0.6 copy-start.10
  65.8 13.0 %all-to-all-start.3 = ((f32[4,2,24,768]{3,2,1,0:T(8,128)}), f32[4,2,24,768]{3,2,1,0:T(8,128)S(1)}, u32[]{:S(2)}, u32[]{:S(2)}) async-start(f32[4,2,24,768]{3,2,1,0:T(8,128)} %pad_maximum_fusion), calls=%async_computation.3 | async-start | bytes 1179648 | tf_op jit(solution)/shard_map/all_to_all | solution.py:148
  69.3 38.8 %collective-permute-start.10 = (f32[256,768]{1,0:T(8,128)S(1)}, f32[256,768]{1,0:T(8,128)}, u32[]{:S(2)}, u32[]{:S(2)}) collective-permute-start(f32[256,768]{1,0:T(8,128)S(1)} %bitcast.46), channel_id=1, source_target_pairs={{0,16},{8,24},{16,0},{24,8},{1,17},{9,25},{17,1},{25,9},{2,18},{10... | collective-permute-start | bytes 2359304 | tf_op jit(solution)/shard_map/ppermute | solution.py:142
  72.7 49.4 %collective-permute-start.9 = (f32[256,768]{1,0:T(8,128)S(1)}, f32[256,768]{1,0:T(8,128)}, u32[]{:S(2)}, u32[]{:S(2)}) collective-permute-start(f32[256,768]{1,0:T(8,128)S(1)} %bitcast.47), channel_id=1, source_target_pairs={{0,8},{8,0},{16,24},{24,16},{1,9},{9,1},{17,25},{25,17},{2,10},{10... | collective-permute-start | bytes 2359304 | tf_op jit(solution)/shard_map/ppermute | solution.py:142
  78.8 7.4 %all-to-all-start.2 = ((f32[4,32,128]{2,1,0:T(8,128)}), f32[4,32,128]{2,1,0:T(8,128)S(1)}, u32[]{:S(2)}, u32[]{:S(2)}) async-start(f32[4,32,128]{2,1,0:T(8,128)} %copy-done.10), calls=%async_computation.2 | async-start | bytes 131072 | tf_op jit(solution)/shard_map/all_to_all | solution.py:148
  86.2 40.0 %all-to-all-start.1 = ((f32[4,2,24,768]{3,2,1,0:T(8,128)}), f32[4,2,24,768]{3,2,1,0:T(8,128)S(1)}, u32[]{:S(2)}, u32[]{:S(2)}) async-start(f32[4,2,24,768]{3,2,1,0:T(8,128)} %bitcast.50), calls=%async_computation.1 | async-start | bytes 1179648 | tf_op jit(solution)/shard_map/all_to_all | solution.py:148
  95.0 40.4 %collective-permute-start.6 = (f32[2,96,768]{2,1,0:T(8,128)}, f32[2,96,768]{2,1,0:T(8,128)}, u32[]{:S(2)}, u32[]{:S(2)}) collective-permute-start(f32[2,96,768]{2,1,0:T(8,128)} %get-tuple-element.56), channel_id=1, source_target_pairs={{0,8},{8,0},{16,24},{24,16},{1,9},{9,1},{17,25},{25,17},{2,10},{10... | collective-permute-start | bytes 1769480 | tf_op jit(solution)/shard_map/ppermute | solution.py:142
  96.4 36.4 %collective-permute-start.7 = (f32[2,96,768]{2,1,0:T(8,128)}, f32[2,96,768]{2,1,0:T(8,128)}, u32[]{:S(2)}, u32[]{:S(2)}) collective-permute-start(f32[2,96,768]{2,1,0:T(8,128)} %get-tuple-element.56), channel_id=1, source_target_pairs={{0,16},{8,24},{16,0},{24,8},{1,17},{9,25},{17,1},{25,9},{2,18},{10... | collective-permute-start | bytes 1769480 | tf_op jit(solution)/shard_map/ppermute | solution.py:142
  100.6 21.5 %copy-start.11 = (f32[2,384,768]{2,1,0:T(8,128)}, f32[2,384,768]{2,1,0:T(8,128)S(1)}, u32[]{:S(2)}) copy-start(f32[2,384,768]{2,1,0:T(8,128)S(1)} %constant_dynamic-update-slice_fusion.7) | copy-start | bytes 7077892
  100.6 33.7 %copy-start.15 = (f32[2,1,24,3072]{3,2,1,0:T(8,128)S(1)}, f32[2,1,24,3072]{3,2,1,0:T(8,128)}, u32[]{:S(2)}) copy-start(f32[2,1,24,3072]{3,2,1,0:T(8,128)} %param.9) | copy-start | bytes 1769476
  100.6 33.7 %copy-start.16 = (f32[2,1,24,3072]{3,2,1,0:T(8,128)S(1)}, f32[2,1,24,3072]{3,2,1,0:T(8,128)}, u32[]{:S(2)}) copy-start(f32[2,1,24,3072]{3,2,1,0:T(8,128)} %param.10) | copy-start | bytes 1769476
  108.1 43.5 %collective-permute-start.11 = (f32[256,768]{1,0:T(8,128)}, f32[256,768]{1,0:T(8,128)}, u32[]{:S(2)}, u32[]{:S(2)}) collective-permute-start(f32[256,768]{1,0:T(8,128)} %collective-permute-done.10), channel_id=1, source_target_pairs={{0,8},{8,0},{16,24},{24,16},{1,9},{9,1},{17,25},{25,17},{2,10},{10... | collective-permute-start | bytes 2359304 | tf_op jit(solution)/shard_map/ppermute | solution.py:142
  126.2 9.2 %copy-start.12 = (f32[2,384,768]{2,1,0:T(8,128)S(1)}, f32[2,384,768]{2,1,0:T(8,128)}, u32[]{:S(2)}) copy-start(f32[2,384,768]{2,1,0:T(8,128)} %copy-done.11) | copy-start | bytes 7077892
  132.8 30.5 %collective-permute-start.8 = (f32[2,96,768]{2,1,0:T(8,128)}, f32[2,96,768]{2,1,0:T(8,128)S(1)}, u32[]{:S(2)}, u32[]{:S(2)}) collective-permute-start(f32[2,96,768]{2,1,0:T(8,128)} %collective-permute-done.7), channel_id=1, source_target_pairs={{0,8},{8,0},{16,24},{24,16},{1,9},{9,1},{17,25},{25,17},{2,10},{10... | collective-permute-start | bytes 1769480 | tf_op jit(solution)/shard_map/ppermute | solution.py:142
  163.4 1.4 copy-start.13

commit v3 on v2

--- a/solution.py
+++ b/solution.py
@@ -39,7 +39,7 @@
         out_specs=jax.tree.map(lambda _: vmem_spec, outs),
         scratch_shapes=scratch,
         compiler_params=pltpu.CompilerParams(vmem_limit_bytes=vmem_limit),
-        cost_estimate=pl.CostEstimate(flops=flops, bytes_accessed=size, transcendentals=0),
+        cost_estimate=pl.CostEstimate(flops=0, bytes_accessed=0, transcendentals=0),
     )
 
 
@@ -84,8 +84,8 @@
         ),
         compiler_params=pltpu.CompilerParams(vmem_limit_bytes=vmem_limit),
         cost_estimate=pl.CostEstimate(
-            flops=12 * groups * rows * width * rank,
-            bytes_accessed=4 * groups * rows * (width + rank),
+            flops=0,
+            bytes_accessed=0,
             transcendentals=0,
         ),
     )(me, inner_emb, basis)
@@ -160,10 +160,14 @@
     def block(d):
         return lax.dynamic_slice(dense, (0, (me ^ d) * block_rows, 0), (2, block_rows, cols))
 
-    far, inner_emb, outer_emb, outer_dense = meet(block(3), inner_emb, outer_emb, outer_dense)
+    far, inner_emb, outer_emb, outer_dense, dense = meet(
+        block(3), inner_emb, outer_emb, outer_dense, dense
+    )
     far = send(far, 1)
 
     p3, p2, p1, p0 = project(inner_emb, basis, me.reshape(1).astype(jnp.int32), groups, tp_count)
+    p3, p2, p1, p0, outer_emb = meet(p3, p2, p1, p0, outer_emb)
+    p3, p2, p1 = send(p3, 3), send(p2, 2), send(p1, 1)
     emb_base, outer_proj = call(
         emb_base_body,
         [shaped(tp_count, piece_rows, width), shaped(emb_rows, rank)],
@@ -171,11 +175,11 @@
         flops=24 * emb_rows * width * rank,
         size=12 * emb_rows * width,
     )(outer_emb, moment_emb, basis)
-    far, p3, p2, p1, emb_base = meet(far, p3, p2, p1, emb_base)
-    p3, p2, p1 = send(p3, 3), send(p2, 2), send(p1, 1)
+    own, near, second = block(0), block(1), block(2)
+    far, p3, p2, p1, emb_base, near = meet(far, p3, p2, p1, emb_base, near)
     emb_base = swap(emb_base)
-    across = send(block(2) + far, 2)
-    near = send(block(1), 1)
+    across = send(second + far, 2)
+    near = send(near, 1)
     dense_outer = outer_dense[:, 0]
     dense_moment = moment_dense[:, 0]
     dense_base = (1.0 - grad_weight) * dense_outer - moment_weight * dense_moment
@@ -191,7 +195,7 @@
     emb_block, proj_sum, dense_base = meet(emb_block, proj_sum, dense_base)
     dense_base = swap(dense_base)
     across, near, emb_block = meet(across, near, emb_block)
-    dense_sum = block(0) + near + across
+    dense_sum = own + near + across
     emb_block = emb_block.reshape(emb_rows, width)
     dense_block = (
         dense_base.transpose(1, 0, 2, 3).reshape(2, block_rows, cols) + weight * dense_sum

time: 166 us -> 154 us (0.928)
  waiting for transfers between devices: 87.3 us -> 77.3 us
  starting transfers between devices: 34.6 us -> 31.3 us
    ppermute x12, waiting for transfers between devices: 81.4 us -> 71.8 us  [send(): return lax.ppermute(x, 'rep', [(i, i ^ d) for i in range(groups)])]
    ppermute x12, starting transfers between devices: 20.9 us -> 17.6 us  [send(): return lax.ppermute(x, 'rep', [(i, i ^ d) for i in range(groups)])]
  transfers between devices with their start and end apart: 16 -> 16, of which waited for: 10 -> 9; matrix products, arithmetic and copies ran while one was open for 13% -> 15% of each run, Pallas kernels for 6% -> 6%
where the time goes in v3:
time: 154 us; the launch traced here: 153 us
  waiting for transfers between devices  77.3 us (50%)
  starting transfers between devices  31.3 us (20%)
  local copies, waits for them, and re-layouts  25.9 us (17%)
  Pallas kernels  9.95 us (6%)
  other arithmetic  7.88 us (5%)
    ppermute x12, waiting for transfers between devices, send(): return lax.ppermute(x, 'rep', [(i, i ^ d) for i in range(groups)])  71.8 us
    ppermute x12, starting transfers between devices, send(): return lax.ppermute(x, 'rep', [(i, i ^ d) for i in range(groups)])  17.6 us
    all_to_all x4, starting transfers between devices, swap(): return lax.all_to_all(x, 'tp', split_axis=0, concat_axis=0, tiled=True)  13.7 us
    unnamed x34, local copies, waits for them, and re-layouts  9.27 us
    dynamic_update_slice x4, local copies, waits for them, and re-layouts, per_device(): lax.dynamic_update_slice(embed_train, value, ((me ^ d) * emb_rows, 0))  7.12 us
    all_to_all x4, waiting for transfers between devices, swap(): return lax.all_to_all(x, 'tp', split_axis=0, concat_axis=0, tiled=True)  5.5 us
    pallas_call x1, Pallas kernels, per_device(): call(emb_base_body, [shaped(tp_count, piece_rows, width), shaped(emb_rows...  3.49 us
    dynamic_update_slice x4, local copies, waits for them, and re-layouts, per_device(): lax.dynamic_update_slice(dense_train, value, (0, (me ^ d) * block_rows, 0))  3.37 us
  transfers between devices with their start and end apart: 16, of which 9 were waited for; matrix products, arithmetic and copies ran while one was open for 15% of the time, Pallas kernels for 6%

profile of v3, /device:TPU:0, one launch (start us, length us, event | category | flops | bytes accessed | tf_op | source)
XLA Modules:
  0.0 153.2 jit_solution(7715605889576380985)
XLA Ops:
  0.7 1.2 dynamic-slice_bitcast_fusion
  1.9 3.1 %collective-permute-start = (f32[2,96,768]{2,1,0:T(8,128)S(1)}, f32[2,96,768]{2,1,0:T(8,128)}, u32[]{:S(2)}, u32[]{:S(2)}) collective-permute-start(f32[2,96,768]{2,1,0:T(8,128)S(1)} %dynamic-slice_bitcast_fusion), channel_id=1, source_target_pairs={{0,8},{8,0},{16,24},{24,16},{1,9},{9,1},{17,25},{25,17},{2,10},{10... | collective-permute-start | bytes 1769480 | tf_op jit(solution)/shard_map/ppermute | solution.py:142
  5.0 1.9 %copy-done.2 = f32[1,1024,768]{2,1,0:T(8,128)S(1)} copy-done((f32[1,1024,768]{2,1,0:T(8,128)S(1)}, f32[1,1024,768]{2,1,0:T(8,128)}, u32[]{:S(2)}) %copy-start.2) | copy-done | bytes 3145752
  6.9 0.9 copy-done.3
  7.8 3.1 %shard_map.118 = (f32[4,32,128]{2,1,0:T(8,128)S(1)}, f32[4,32,128]{2,1,0:T(8,128)S(1)}, f32[4,32,128]{2,1,0:T(8,128)S(1)}, f32[4,32,128]{2,1,0:T(8,128)S(1)}) custom-call(s32[1]{0:T(128)} %bitcast.2.me_ref, f32[1,1024,768]{2,1,0:T(8,128)S(1)} %copy-done.2, f32[64,768]{1,0:T(8,128)S(1)} %copy-done.3), custom_call_target="tpu_custom_call" | custom-call | tf_op jit(solution)/shard_map/pallas_call | solution.py:73
  10.9 2.5 %collective-permute-start.1 = (f32[4,32,128]{2,1,0:T(8,128)S(1)}, f32[4,32,128]{2,1,0:T(8,128)S(1)}, u32[]{:S(2)}, u32[]{:S(2)}) collective-permute-start(f32[4,32,128]{2,1,0:T(8,128)S(1)} %get-tuple-element.47), channel_id=1, source_target_pairs={{0,24},{8,16},{16,8},{24,0},{1,25},{9,17},{17,9},{25,1},{2,26},{10... | collective-permute-start | bytes 196616 | tf_op jit(solution)/shard_map/ppermute | solution.py:142
  13.7 1.7 %collective-permute-start.3 = (f32[4,32,128]{2,1,0:T(8,128)S(1)}, f32[4,32,128]{2,1,0:T(8,128)S(1)}, u32[]{:S(2)}, u32[]{:S(2)}) collective-permute-start(f32[4,32,128]{2,1,0:T(8,128)S(1)} %get-tuple-element.49), channel_id=1, source_target_pairs={{0,8},{8,0},{16,24},{24,16},{1,9},{9,1},{17,25},{25,17},{2,10},{10... | collective-permute-start | bytes 196616 | tf_op jit(solution)/shard_map/ppermute | solution.py:142
  15.4 3.5 %shard_map.119 = (f32[4,64,768]{2,1,0:T(8,128)}, f32[256,64]{1,0:T(8,128)S(1)}) custom-call(f32[1,4,1,64,768]{4,3,2,1,0:T(8,128)S(1)} %copy-done, f32[1,4,1,64,768]{4,3,2,1,0:T(8,128)S(1)} %copy-done.1, f32[64,768]{1,0:T(8,128)S(1)} %copy-done.4), custom_call_target="tpu_custom_call" | custom-call | tf_op jit(solution)/shard_map/pallas_call | solution.py:171
  18.9 1.9 %constant_dynamic-slice_fusion = f32[2,96,768]{2,1,0:T(8,128)} fusion(f32[2,384,768]{2,1,0:T(8,128)} %bitcast.43, s32[]{:T(128)S(6)} %select_n.31), kind=kLoop, calls=%fused_computation.27 | loop fusion | bytes 1179652 | tf_op jit(solution)/shard_map/dynamic_slice | solution.py:161
  20.8 2.2 %collective-permute-done.1.p3 = f32[4,32,128]{2,1,0:T(8,128)S(1)} collective-permute-done((f32[4,32,128]{2,1,0:T(8,128)S(1)}, f32[4,32,128]{2,1,0:T(8,128)S(1)}, u32[]{:S(2)}, u32[]{:S(2)}) %collective-permute-start.1) | collective-permute-done | bytes 65568 | tf_op jit(solution)/shard_map/ppermute | solution.py:142
  24.9 3.5 %all-to-all-start = ((f32[4,64,768]{2,1,0:T(8,128)}), f32[4,64,768]{2,1,0:T(8,128)S(1)}, u32[]{:S(2)}, u32[]{:S(2)}) async-start(f32[4,64,768]{2,1,0:T(8,128)} %get-tuple-element.54), calls=%async_computation | async-start | bytes 1572864 | tf_op jit(solution)/shard_map/all_to_all | solution.py:148
  28.4 2.1 %dynamic-slice_add_fusion = f32[2,96,768]{2,1,0:T(8,128)} fusion(f32[2,96,768]{2,1,0:T(8,128)} %collective-permute-done, f32[2,384,768]{2,1,0:T(8,128)} %bitcast.44, s32[]{:T(128)S(6)} %select_n.30), kind=kLoop, calls=%fused_computation.9 | loop fusion | flops 147456 | bytes 1769476 | tf_op jit(solution)/shard_map/add | solution.py:181
  30.6 1.0 collective-permute-start.4
  31.5 1.6 %collective-permute-start.5 = (f32[2,96,768]{2,1,0:T(8,128)}, f32[2,96,768]{2,1,0:T(8,128)}, u32[]{:S(2)}, u32[]{:S(2)}) collective-permute-start(f32[2,96,768]{2,1,0:T(8,128)} %constant_dynamic-slice_fusion), channel_id=1, source_target_pairs={{0,8},{8,0},{16,24},{24,16},{1,9},{9,1},{17,25},{25,17},{2,10},{10... | collective-permute-start | bytes 1769480 | tf_op jit(solution)/shard_map/ppermute | solution.py:142
  33.1 1.3 subtract_bitcast_fusion
  34.5 0.9 pad_maximum_fusion
  35.4 4.7 %all-to-all-done = f32[4,64,768]{2,1,0:T(8,128)S(1)} async-done(((f32[4,64,768]{2,1,0:T(8,128)}), f32[4,64,768]{2,1,0:T(8,128)S(1)}, u32[]{:S(2)}, u32[]{:S(2)}) %all-to-all-start) | async-done | bytes 786464 | tf_op jit(solution)/shard_map/all_to_all | solution.py:148
  40.1 0.8 copy-done.6
  40.9 0.8 copy-done.8
  41.7 0.8 copy-done.10
  42.6 0.8 shard_map.120
  44.0 3.5 %all-to-all-start.3 = ((f32[4,2,24,768]{3,2,1,0:T(8,128)}), f32[4,2,24,768]{3,2,1,0:T(8,128)S(1)}, u32[]{:S(2)}, u32[]{:S(2)}) async-start(f32[4,2,24,768]{3,2,1,0:T(8,128)} %pad_maximum_fusion), calls=%async_computation.3 | async-start | bytes 1179648 | tf_op jit(solution)/shard_map/all_to_all | solution.py:148
  47.5 12.7 %collective-permute-done.4 = f32[2,96,768]{2,1,0:T(8,128)} collective-permute-done((f32[2,96,768]{2,1,0:T(8,128)}, f32[2,96,768]{2,1,0:T(8,128)}, u32[]{:S(2)}, u32[]{:S(2)}) %collective-permute-start.4) | collective-permute-done | bytes 589856 | tf_op jit(solution)/shard_map/ppermute | solution.py:142
  60.1 0.9 collective-permute-start.10
  61.1 1.7 %collective-permute-start.9 = (f32[256,768]{1,0:T(8,128)S(1)}, f32[256,768]{1,0:T(8,128)}, u32[]{:S(2)}, u32[]{:S(2)}) collective-permute-start(f32[256,768]{1,0:T(8,128)S(1)} %bitcast.39), channel_id=1, source_target_pairs={{0,8},{8,0},{16,24},{24,16},{1,9},{9,1},{17,25},{25,17},{2,10},{10... | collective-permute-start | bytes 2359304 | tf_op jit(solution)/shard_map/ppermute | solution.py:142
  62.8 3.3 %all-to-all-start.2 = ((f32[4,32,128]{2,1,0:T(8,128)}), f32[4,32,128]{2,1,0:T(8,128)S(1)}, u32[]{:S(2)}, u32[]{:S(2)}) async-start(f32[4,32,128]{2,1,0:T(8,128)} %copy-done.11), calls=%async_computation.2 | async-start | bytes 131072 | tf_op jit(solution)/shard_map/all_to_all | solution.py:148
  66.1 2.4 %bitcast_add_fusion = (f32[2,96,768]{2,1,0:T(8,128)}, f32[2,96,768]{2,1,0:T(8,128)S(1)}) fusion(f32[2,4,24,768]{3,2,1,0:T(8,128)S(1)} %copy.17, f32[2,96,768]{2,1,0:T(8,128)} %collective-permute-done.4, f32[2,96,768]{2,1,0:T(8,128)} %collective-permute-done.5, f32[2,384,768]{2,1,0:T(8,128)} %bitcast.45, s32[]{:T(128)S(6)} %select_n.29), kind=kLoop, calls=%fused_computation.3 | loop fusion | flops 589824 | bytes 3538948 | tf_op jit(solution)/shard_map/add | solution.py:201
  68.5 0.9 copy.19
  69.4 0.8 all-to-all-done.2.back_ref
  70.1 3.5 %all-to-all-start.1 = ((f32[4,2,24,768]{3,2,1,0:T(8,128)}), f32[4,2,24,768]{3,2,1,0:T(8,128)S(1)}, u32[]{:S(2)}, u32[]{:S(2)}) async-start(f32[4,2,24,768]{3,2,1,0:T(8,128)} %bitcast.42), calls=%async_computation.1 | async-start | bytes 1179648 | tf_op jit(solution)/shard_map/all_to_all | solution.py:148
  73.6 1.9 %broadcast_in_dim.9 = f32[1024,768]{1,0:T(8,128)} broadcast(f32[]{:T(128)} %constant.14.clone.1), dimensions={} | broadcast | bytes 3145732 | tf_op jit(solution)/shard_map/broadcast_in_dim | solution.py:211
  75.5 0.9 constant_dynamic-update-slice_fusion.3
  76.4 2.6 %shard_map.121 = (f32[1,4,1,64,768]{4,3,2,1,0:T(8,128)}, f32[1,4,1,64,768]{4,3,2,1,0:T(8,128)}) custom-call(f32[1,4,1,64,768]{4,3,2,1,0:T(8,128)S(1)} %copy-done, f32[1,4,1,64,768]{4,3,2,1,0:T(8,128)S(1)} %copy-done.1, f32[256,64]{1,0:T(8,128)S(1)} %get-tuple-element.64.proj_ref, f32[4,32,128]{2,1,0:T(8,128)S(1)} %all-to-all-done.2.back_ref, ...), custom_call_target="tpu_custom_call" | custom-call | tf_op jit(solution)/shard_map/pallas_call | solution.py:223
  79.3 2.0 %collective-permute-start.7 = (f32[2,96,768]{2,1,0:T(8,128)}, f32[2,96,768]{2,1,0:T(8,128)}, u32[]{:S(2)}, u32[]{:S(2)}) collective-permute-start(f32[2,96,768]{2,1,0:T(8,128)} %get-tuple-element.70), channel_id=1, source_target_pairs={{0,16},{8,24},{16,0},{24,8},{1,17},{9,25},{17,1},{25,9},{2,18},{10... | collective-permute-start | bytes 1769480 | tf_op jit(solution)/shard_map/ppermute | solution.py:142
  81.5 1.1 constant_dynamic-update-slice_fusion.7
  82.6 14.3 %collective-permute-done.10 = f32[256,768]{1,0:T(8,128)} collective-permute-done((f32[256,768]{1,0:T(8,128)S(1)}, f32[256,768]{1,0:T(8,128)}, u32[]{:S(2)}, u32[]{:S(2)}) %collective-permute-start.10) | collective-permute-done | bytes 786464 | tf_op jit(solution)/shard_map/ppermute | solution.py:142
  97.0 12.0 %collective-permute-done.9 = f32[256,768]{1,0:T(8,128)} collective-permute-done((f32[256,768]{1,0:T(8,128)S(1)}, f32[256,768]{1,0:T(8,128)}, u32[]{:S(2)}, u32[]{:S(2)}) %collective-permute-start.9) | collective-permute-done | bytes 786464 | tf_op jit(solution)/shard_map/ppermute | solution.py:142
  109.0 2.1 %constant_dynamic-update-slice_fusion.2 = f32[1024,768]{1,0:T(8,128)} fusion(f32[1024,768]{1,0:T(8,128)} %constant_dynamic-update-slice_fusion.3, f32[256,768]{1,0:T(8,128)} %collective-permute-done.9, s32[]{:T(128)S(6)} %select_n.33), kind=kLoop, calls=%fused_computation.21 | loop fusion | bytes 1572868 | tf_op jit(solution)/shard_map/dynamic_update_slice | solution.py:213
  111.0 2.1 %constant_dynamic-update-slice_fusion.1 = f32[1024,768]{1,0:T(8,128)} fusion(f32[1024,768]{1,0:T(8,128)} %constant_dynamic-update-slice_fusion.2, f32[256,768]{1,0:T(8,128)} %collective-permute-done.10, s32[]{:T(128)S(6)} %select_n.34), kind=kLoop, calls=%fused_computation.20 | loop fusion | bytes 1572868 | tf_op jit(solution)/shard_map/dynamic_update_slice | solution.py:213
  113.1 8.2 %collective-permute-done.7 = f32[2,96,768]{2,1,0:T(8,128)} collective-permute-done((f32[2,96,768]{2,1,0:T(8,128)}, f32[2,96,768]{2,1,0:T(8,128)}, u32[]{:S(2)}, u32[]{:S(2)}) %collective-permute-start.7) | collective-permute-done | bytes 589856 | tf_op jit(solution)/shard_map/ppermute | solution.py:142
  121.3 2.5 %collective-permute-start.8 = (f32[2,96,768]{2,1,0:T(8,128)}, f32[2,96,768]{2,1,0:T(8,128)S(1)}, u32[]{:S(2)}, u32[]{:S(2)}) collective-permute-start(f32[2,96,768]{2,1,0:T(8,128)} %collective-permute-done.7), channel_id=1, source_target_pairs={{0,8},{8,0},{16,24},{24,16},{1,9},{9,1},{17,25},{25,17},{2,10},{10... | collective-permute-start | bytes 1769480 | tf_op jit(solution)/shard_map/ppermute | solution.py:142
  123.9 1.2 multiply_subtract_fusion
  125.0 1.1 constant_dynamic-update-slice_fusion.6
  126.1 1.1 constant_dynamic-update-slice_fusion.5
  127.3 12.0 %collective-permute-done.11 = f32[256,768]{1,0:T(8,128)} collective-permute-done((f32[256,768]{1,0:T(8,128)}, f32[256,768]{1,0:T(8,128)}, u32[]{:S(2)}, u32[]{:S(2)}) %collective-permute-start.11) | collective-permute-done | bytes 786464 | tf_op jit(solution)/shard_map/ppermute | solution.py:142
  139.3 2.1 %constant_dynamic-update-slice_fusion = f32[1024,768]{1,0:T(8,128)} fusion(f32[1024,768]{1,0:T(8,128)} %constant_dynamic-update-slice_fusion.1, f32[256,768]{1,0:T(8,128)} %collective-permute-done.11, s32[]{:T(128)S(6)} %select_n.35), kind=kLoop, calls=%fused_computation.19 | loop fusion | bytes 1572868 | tf_op jit(solution)/shard_map/dynamic_update_slice | solution.py:213
  141.4 10.4 %collective-permute-done.8 = f32[2,96,768]{2,1,0:T(8,128)S(1)} collective-permute-done((f32[2,96,768]{2,1,0:T(8,128)}, f32[2,96,768]{2,1,0:T(8,128)S(1)}, u32[]{:S(2)}, u32[]{:S(2)}) %collective-permute-start.8) | collective-permute-done | bytes 589856 | tf_op jit(solution)/shard_map/ppermute | solution.py:142
  151.8 1.4 copy-done.14
  (43 shorter events, 3.4 us)
Async XLA Ops:
  0.6 14.8 %copy-start = (f32[1,4,1,64,768]{4,3,2,1,0:T(8,128)S(1)}, f32[1,4,1,64,768]{4,3,2,1,0:T(8,128)}, u32[]{:S(2)}) copy-start(f32[1,4,1,64,768]{4,3,2,1,0:T(8,128)} %outer_ref.1) | copy-start | bytes 2359300
  0.6 14.7 %copy-start.1 = (f32[1,4,1,64,768]{4,3,2,1,0:T(8,128)S(1)}, f32[1,4,1,64,768]{4,3,2,1,0:T(8,128)}, u32[]{:S(2)}) copy-start(f32[1,4,1,64,768]{4,3,2,1,0:T(8,128)} %moment_ref.3) | copy-start | bytes 2359300
  1.9 23.1 %collective-permute-start = (f32[2,96,768]{2,1,0:T(8,128)S(1)}, f32[2,96,768]{2,1,0:T(8,128)}, u32[]{:S(2)}, u32[]{:S(2)}) collective-permute-start(f32[2,96,768]{2,1,0:T(8,128)S(1)} %dynamic-slice_bitcast_fusion), channel_id=1, source_target_pairs={{0,8},{8,0},{16,24},{24,16},{1,9},{9,1},{17,25},{25,17},{2,10},{10... | collective-permute-start | bytes 1769480 | tf_op jit(solution)/shard_map/ppermute | solution.py:142
  5.0 1.9 %copy-start.2 = (f32[1,1024,768]{2,1,0:T(8,128)S(1)}, f32[1,1024,768]{2,1,0:T(8,128)}, u32[]{:S(2)}) copy-start(f32[1,1024,768]{2,1,0:T(8,128)} %x_ref) | copy-start | bytes 9437188
  6.9 0.9 copy-start.3
  7.8 7.6 %copy-start.4 = (f32[64,768]{1,0:T(8,128)S(1)}, f32[64,768]{1,0:T(8,128)}, u32[]{:S(2)}) copy-start(f32[64,768]{1,0:T(8,128)} %basis_ref.7) | copy-start | bytes 589828
  10.9 12.1 %collective-permute-start.1 = (f32[4,32,128]{2,1,0:T(8,128)S(1)}, f32[4,32,128]{2,1,0:T(8,128)S(1)}, u32[]{:S(2)}, u32[]{:S(2)}) collective-permute-start(f32[4,32,128]{2,1,0:T(8,128)S(1)} %get-tuple-element.47), channel_id=1, source_target_pairs={{0,24},{8,16},{16,8},{24,0},{1,25},{9,17},{17,9},{25,1},{2,26},{10... | collective-permute-start | bytes 196616 | tf_op jit(solution)/shard_map/ppermute | solution.py:142
  13.5 10.2 %collective-permute-start.2 = (f32[4,32,128]{2,1,0:T(8,128)S(1)}, f32[4,32,128]{2,1,0:T(8,128)S(1)}, u32[]{:S(2)}, u32[]{:S(2)}) collective-permute-start(f32[4,32,128]{2,1,0:T(8,128)S(1)} %get-tuple-element.48), channel_id=1, source_target_pairs={{0,16},{8,24},{16,0},{24,8},{1,17},{9,25},{17,1},{25,9},{2,18},{10... | collective-permute-start | bytes 196616 | tf_op jit(solution)/shard_map/ppermute | solution.py:142
  13.7 10.6 %collective-permute-start.3 = (f32[4,32,128]{2,1,0:T(8,128)S(1)}, f32[4,32,128]{2,1,0:T(8,128)S(1)}, u32[]{:S(2)}, u32[]{:S(2)}) collective-permute-start(f32[4,32,128]{2,1,0:T(8,128)S(1)} %get-tuple-element.49), channel_id=1, source_target_pairs={{0,8},{8,0},{16,24},{24,16},{1,9},{9,1},{17,25},{25,17},{2,10},{10... | collective-permute-start | bytes 196616 | tf_op jit(solution)/shard_map/ppermute | solution.py:142
  23.0 0.6 copy-start.5
  23.7 0.6 copy-start.7
  24.3 0.6 copy-start.9
  24.9 15.1 %all-to-all-start = ((f32[4,64,768]{2,1,0:T(8,128)}), f32[4,64,768]{2,1,0:T(8,128)S(1)}, u32[]{:S(2)}, u32[]{:S(2)}) async-start(f32[4,64,768]{2,1,0:T(8,128)} %get-tuple-element.54), calls=%async_computation | async-start | bytes 1572864 | tf_op jit(solution)/shard_map/all_to_all | solution.py:148
  30.6 29.5 %collective-permute-start.4 = (f32[2,96,768]{2,1,0:T(8,128)}, f32[2,96,768]{2,1,0:T(8,128)}, u32[]{:S(2)}, u32[]{:S(2)}) collective-permute-start(f32[2,96,768]{2,1,0:T(8,128)} %dynamic-slice_add_fusion), channel_id=1, source_target_pairs={{0,16},{8,24},{16,0},{24,8},{1,17},{9,25},{17,1},{25,9},{2,18},{10... | collective-permute-start | bytes 1769480 | tf_op jit(solution)/shard_map/ppermute | solution.py:142
  31.5 28.6 %collective-permute-start.5 = (f32[2,96,768]{2,1,0:T(8,128)}, f32[2,96,768]{2,1,0:T(8,128)}, u32[]{:S(2)}, u32[]{:S(2)}) collective-permute-start(f32[2,96,768]{2,1,0:T(8,128)} %constant_dynamic-slice_fusion), channel_id=1, source_target_pairs={{0,8},{8,0},{16,24},{24,16},{1,9},{9,1},{17,25},{25,17},{2,10},{10... | collective-permute-start | bytes 1769480 | tf_op jit(solution)/shard_map/ppermute | solution.py:142
  40.1 0.8 copy-start.6
  40.9 0.8 copy-start.8
  41.7 0.8 copy-start.10
  43.4 0.6 copy-start.11
  44.0 18.8 %all-to-all-start.3 = ((f32[4,2,24,768]{3,2,1,0:T(8,128)}), f32[4,2,24,768]{3,2,1,0:T(8,128)S(1)}, u32[]{:S(2)}, u32[]{:S(2)}) async-start(f32[4,2,24,768]{3,2,1,0:T(8,128)} %pad_maximum_fusion), calls=%async_computation.3 | async-start | bytes 1179648 | tf_op jit(solution)/shard_map/all_to_all | solution.py:148
  60.1 36.8 %collective-permute-start.10 = (f32[256,768]{1,0:T(8,128)S(1)}, f32[256,768]{1,0:T(8,128)}, u32[]{:S(2)}, u32[]{:S(2)}) collective-permute-start(f32[256,768]{1,0:T(8,128)S(1)} %bitcast.38), channel_id=1, source_target_pairs={{0,16},{8,24},{16,0},{24,8},{1,17},{9,25},{17,1},{25,9},{2,18},{10... | collective-permute-start | bytes 2359304 | tf_op jit(solution)/shard_map/ppermute | solution.py:142
  61.1 47.9 %collective-permute-start.9 = (f32[256,768]{1,0:T(8,128)S(1)}, f32[256,768]{1,0:T(8,128)}, u32[]{:S(2)}, u32[]{:S(2)}) collective-permute-start(f32[256,768]{1,0:T(8,128)S(1)} %bitcast.39), channel_id=1, source_target_pairs={{0,8},{8,0},{16,24},{24,16},{1,9},{9,1},{17,25},{25,17},{2,10},{10... | collective-permute-start | bytes 2359304 | tf_op jit(solution)/shard_map/ppermute | solution.py:142
  62.8 7.4 %all-to-all-start.2 = ((f32[4,32,128]{2,1,0:T(8,128)}), f32[4,32,128]{2,1,0:T(8,128)S(1)}, u32[]{:S(2)}, u32[]{:S(2)}) async-start(f32[4,32,128]{2,1,0:T(8,128)} %copy-done.11), calls=%async_computation.2 | async-start | bytes 131072 | tf_op jit(solution)/shard_map/all_to_all | solution.py:148
  70.1 42.9 %all-to-all-start.1 = ((f32[4,2,24,768]{3,2,1,0:T(8,128)}), f32[4,2,24,768]{3,2,1,0:T(8,128)S(1)}, u32[]{:S(2)}, u32[]{:S(2)}) async-start(f32[4,2,24,768]{3,2,1,0:T(8,128)} %bitcast.42), calls=%async_computation.1 | async-start | bytes 1179648 | tf_op jit(solution)/shard_map/all_to_all | solution.py:148
  79.0 46.0 %collective-permute-start.6 = (f32[2,96,768]{2,1,0:T(8,128)}, f32[2,96,768]{2,1,0:T(8,128)}, u32[]{:S(2)}, u32[]{:S(2)}) collective-permute-start(f32[2,96,768]{2,1,0:T(8,128)} %get-tuple-element.70), channel_id=1, source_target_pairs={{0,8},{8,0},{16,24},{24,16},{1,9},{9,1},{17,25},{25,17},{2,10},{10... | collective-permute-start | bytes 1769480 | tf_op jit(solution)/shard_map/ppermute | solution.py:142
  79.3 42.0 %collective-permute-start.7 = (f32[2,96,768]{2,1,0:T(8,128)}, f32[2,96,768]{2,1,0:T(8,128)}, u32[]{:S(2)}, u32[]{:S(2)}) collective-permute-start(f32[2,96,768]{2,1,0:T(8,128)} %get-tuple-element.70), channel_id=1, source_target_pairs={{0,16},{8,24},{16,0},{24,8},{1,17},{9,25},{17,1},{25,9},{2,18},{10... | collective-permute-start | bytes 1769480 | tf_op jit(solution)/shard_map/ppermute | solution.py:142
  82.6 26.3 %copy-start.12 = (f32[2,384,768]{2,1,0:T(8,128)}, f32[2,384,768]{2,1,0:T(8,128)S(1)}, u32[]{:S(2)}) copy-start(f32[2,384,768]{2,1,0:T(8,128)S(1)} %constant_dynamic-update-slice_fusion.7) | copy-start | bytes 7077892
  82.6 41.2 %copy-start.15 = (f32[2,1,24,3072]{3,2,1,0:T(8,128)S(1)}, f32[2,1,24,3072]{3,2,1,0:T(8,128)}, u32[]{:S(2)}) copy-start(f32[2,1,24,3072]{3,2,1,0:T(8,128)} %param.9) | copy-start | bytes 1769476
  82.6 41.2 %copy-start.16 = (f32[2,1,24,3072]{3,2,1,0:T(8,128)S(1)}, f32[2,1,24,3072]{3,2,1,0:T(8,128)}, u32[]{:S(2)}) copy-start(f32[2,1,24,3072]{3,2,1,0:T(8,128)} %param.10) | copy-start | bytes 1769476
  97.0 42.3 %collective-permute-start.11 = (f32[256,768]{1,0:T(8,128)}, f32[256,768]{1,0:T(8,128)}, u32[]{:S(2)}, u32[]{:S(2)}) collective-permute-start(f32[256,768]{1,0:T(8,128)} %collective-permute-done.10), channel_id=1, source_target_pairs={{0,8},{8,0},{16,24},{24,16},{1,9},{9,1},{17,25},{25,17},{2,10},{10... | collective-permute-start | bytes 2359304 | tf_op jit(solution)/shard_map/ppermute | solution.py:142
  113.1 11.9 %copy-start.13 = (f32[2,384,768]{2,1,0:T(8,128)S(1)}, f32[2,384,768]{2,1,0:T(8,128)}, u32[]{:S(2)}) copy-start(f32[2,384,768]{2,1,0:T(8,128)} %copy-done.12) | copy-start | bytes 7077892
  121.3 30.4 %collective-permute-start.8 = (f32[2,96,768]{2,1,0:T(8,128)}, f32[2,96,768]{2,1,0:T(8,128)S(1)}, u32[]{:S(2)}, u32[]{:S(2)}) collective-permute-start(f32[2,96,768]{2,1,0:T(8,128)} %collective-permute-done.7), channel_id=1, source_target_pairs={{0,8},{8,0},{16,24},{24,16},{1,9},{9,1},{17,25},{25,17},{2,10},{10... | collective-permute-start | bytes 1769480 | tf_op jit(solution)/shard_map/ppermute | solution.py:142
  151.8 1.4 copy-start.14

commit v4 on v3

--- a/solution.py
+++ b/solution.py
@@ -176,7 +176,7 @@
         size=12 * emb_rows * width,
     )(outer_emb, moment_emb, basis)
     own, near, second = block(0), block(1), block(2)
-    far, p3, p2, p1, emb_base, near = meet(far, p3, p2, p1, emb_base, near)
+    far, emb_base, near = meet(far, emb_base, near)
     emb_base = swap(emb_base)
     across = send(second + far, 2)
     near = send(near, 1)
@@ -206,8 +206,13 @@
         first = send(x, 1)
         return x, first, second, send(second, 1)
 
-    emb_all = gather(emb_block)
-    dense_all = gather(dense_block)
+    emb_second, emb_first = send(emb_block, 2), send(emb_block, 1)
+    dense_second, dense_first = send(dense_block, 2), send(dense_block, 1)
+    emb_fwd, dense_fwd = emb_second, dense_second
+    emb_far = send(emb_fwd, 1)
+    dense_far = send(dense_fwd, 1)
+    emb_all = (emb_block, emb_first, emb_second, emb_far)
+    dense_all = (dense_block, dense_first, dense_second, dense_far)
     embed_train = jnp.zeros((groups * emb_rows, width), f32)
     for d, value in enumerate(emb_all):
         embed_train = lax.dynamic_update_slice(embed_train, value, ((me ^ d) * emb_rows, 0))

time: 154 us -> 151 us (0.981)
  waiting for transfers between devices: 77.3 us -> 71.6 us
  starting transfers between devices: 31.3 us -> 33.3 us
    all_to_all x4, waiting for transfers between devices: 5.5 us -> 1.43 us  [swap(): return lax.all_to_all(x, 'tp', split_axis=0, concat_axis=0, tiled=True)]
    ppermute x12, starting transfers between devices: 17.6 us -> 19.6 us  [send(): return lax.ppermute(x, 'rep', [(i, i ^ d) for i in range(groups)])]
    ppermute x12, waiting for transfers between devices: 71.8 us -> 70.2 us  [send(): return lax.ppermute(x, 'rep', [(i, i ^ d) for i in range(groups)])]
  transfers between devices with their start and end apart: 16 -> 16, of which waited for: 9 -> 9; matrix products, arithmetic and copies ran while one was open for 15% -> 16% of each run, Pallas kernels for 6% -> 7%
where the time goes in v4:
time: 151 us; the launch traced here: 150 us
  waiting for transfers between devices  71.6 us (47%)
  starting transfers between devices  33.3 us (22%)
  local copies, waits for them, and re-layouts  25.9 us (17%)
  Pallas kernels  9.95 us (7%)
  other arithmetic  7.88 us (5%)
    ppermute x12, waiting for transfers between devices, send(): return lax.ppermute(x, 'rep', [(i, i ^ d) for i in range(groups)])  70.2 us
    ppermute x12, starting transfers between devices, send(): return lax.ppermute(x, 'rep', [(i, i ^ d) for i in range(groups)])  19.6 us
    all_to_all x4, starting transfers between devices, swap(): return lax.all_to_all(x, 'tp', split_axis=0, concat_axis=0, tiled=True)  13.7 us
    unnamed x34, local copies, waits for them, and re-layouts  9.28 us
    dynamic_update_slice x4, local copies, waits for them, and re-layouts, per_device(): lax.dynamic_update_slice(embed_train, value, ((me ^ d) * emb_rows, 0))  7.12 us
    pallas_call x1, Pallas kernels, per_device(): call(emb_base_body, [shaped(tp_count, piece_rows, width), shaped(emb_rows...  3.49 us
    dynamic_update_slice x4, local copies, waits for them, and re-layouts, per_device(): lax.dynamic_update_slice(dense_train, value, (0, (me ^ d) * block_rows, 0))  3.37 us
    dynamic_slice x2, local copies, waits for them, and re-layouts, block(): lax.dynamic_slice(dense, (0, (me ^ d) * block_rows, 0), (2, block_rows, c...  3.14 us
  transfers between devices with their start and end apart: 16, of which 9 were waited for; matrix products, arithmetic and copies ran while one was open for 16% of the time, Pallas kernels for 7%

profile of v4, /device:TPU:0, one launch (start us, length us, event | category | flops | bytes accessed | tf_op | source)
XLA Modules:
  0.0 149.5 jit_solution(6144793167355864441)
XLA Ops:
  0.7 1.2 dynamic-slice_bitcast_fusion
  1.9 3.1 %collective-permute-start = (f32[2,96,768]{2,1,0:T(8,128)S(1)}, f32[2,96,768]{2,1,0:T(8,128)}, u32[]{:S(2)}, u32[]{:S(2)}) collective-permute-start(f32[2,96,768]{2,1,0:T(8,128)S(1)} %dynamic-slice_bitcast_fusion), channel_id=1, source_target_pairs={{0,8},{8,0},{16,24},{24,16},{1,9},{9,1},{17,25},{25,17},{2,10},{10... | collective-permute-start | bytes 1769480 | tf_op jit(solution)/shard_map/ppermute | solution.py:142
  5.0 1.9 %copy-done.2 = f32[1,1024,768]{2,1,0:T(8,128)S(1)} copy-done((f32[1,1024,768]{2,1,0:T(8,128)S(1)}, f32[1,1024,768]{2,1,0:T(8,128)}, u32[]{:S(2)}) %copy-start.2) | copy-done | bytes 3145752
  6.9 0.9 copy-done.3
  7.8 3.1 %shard_map.118 = (f32[4,32,128]{2,1,0:T(8,128)S(1)}, f32[4,32,128]{2,1,0:T(8,128)S(1)}, f32[4,32,128]{2,1,0:T(8,128)S(1)}, f32[4,32,128]{2,1,0:T(8,128)S(1)}) custom-call(s32[1]{0:T(128)} %bitcast.2.me_ref, f32[1,1024,768]{2,1,0:T(8,128)S(1)} %copy-done.2, f32[64,768]{1,0:T(8,128)S(1)} %copy-done.3), custom_call_target="tpu_custom_call" | custom-call | tf_op jit(solution)/shard_map/pallas_call | solution.py:73
  11.0 3.0 %collective-permute-start.4 = (f32[4,32,128]{2,1,0:T(8,128)S(1)}, f32[4,32,128]{2,1,0:T(8,128)S(1)}, u32[]{:S(2)}, u32[]{:S(2)}) collective-permute-start(f32[4,32,128]{2,1,0:T(8,128)S(1)} %get-tuple-element.51), channel_id=1, source_target_pairs={{0,16},{8,24},{16,0},{24,8},{1,17},{9,25},{17,1},{25,9},{2,18},{10... | collective-permute-start | bytes 196616 | tf_op jit(solution)/shard_map/ppermute | solution.py:142
  14.0 1.3 collective-permute-start.5
  15.4 3.5 %shard_map.119 = (f32[4,64,768]{2,1,0:T(8,128)}, f32[256,64]{1,0:T(8,128)S(1)}) custom-call(f32[1,4,1,64,768]{4,3,2,1,0:T(8,128)S(1)} %copy-done, f32[1,4,1,64,768]{4,3,2,1,0:T(8,128)S(1)} %copy-done.1, f32[64,768]{1,0:T(8,128)S(1)} %copy-done.4), custom_call_target="tpu_custom_call" | custom-call | tf_op jit(solution)/shard_map/pallas_call | solution.py:171
  18.9 1.9 %constant_dynamic-slice_fusion = f32[2,96,768]{2,1,0:T(8,128)} fusion(f32[2,384,768]{2,1,0:T(8,128)} %bitcast.43, s32[]{:T(128)S(6)} %select_n.31), kind=kLoop, calls=%fused_computation.27 | loop fusion | bytes 1179652 | tf_op jit(solution)/shard_map/dynamic_slice | solution.py:161
  20.8 3.5 %all-to-all-start = ((f32[4,64,768]{2,1,0:T(8,128)}), f32[4,64,768]{2,1,0:T(8,128)S(1)}, u32[]{:S(2)}, u32[]{:S(2)}) async-start(f32[4,64,768]{2,1,0:T(8,128)} %get-tuple-element.48), calls=%async_computation | async-start | bytes 1572864 | tf_op jit(solution)/shard_map/all_to_all | solution.py:148
  24.3 2.1 %dynamic-slice_add_fusion = f32[2,96,768]{2,1,0:T(8,128)} fusion(f32[2,96,768]{2,1,0:T(8,128)} %collective-permute-done, f32[2,384,768]{2,1,0:T(8,128)} %bitcast.44, s32[]{:T(128)S(6)} %select_n.30), kind=kLoop, calls=%fused_computation.9 | loop fusion | flops 147456 | bytes 1769476 | tf_op jit(solution)/shard_map/add | solution.py:181
  26.4 2.0 %collective-permute-start.1 = (f32[2,96,768]{2,1,0:T(8,128)}, f32[2,96,768]{2,1,0:T(8,128)}, u32[]{:S(2)}, u32[]{:S(2)}) collective-permute-start(f32[2,96,768]{2,1,0:T(8,128)} %dynamic-slice_add_fusion), channel_id=1, source_target_pairs={{0,16},{8,24},{16,0},{24,8},{1,17},{9,25},{17,1},{25,9},{2,18},{10... | collective-permute-start | bytes 1769480 | tf_op jit(solution)/shard_map/ppermute | solution.py:142
  28.4 2.7 %collective-permute-start.2 = (f32[2,96,768]{2,1,0:T(8,128)}, f32[2,96,768]{2,1,0:T(8,128)}, u32[]{:S(2)}, u32[]{:S(2)}) collective-permute-start(f32[2,96,768]{2,1,0:T(8,128)} %constant_dynamic-slice_fusion), channel_id=1, source_target_pairs={{0,8},{8,0},{16,24},{24,16},{1,9},{9,1},{17,25},{25,17},{2,10},{10... | collective-permute-start | bytes 1769480 | tf_op jit(solution)/shard_map/ppermute | solution.py:142
  31.2 1.3 subtract_bitcast_fusion
  32.5 0.9 pad_maximum_fusion
  33.4 0.6 copy-done.5
  35.3 0.6 all-to-all-done
  35.9 0.8 copy-done.6
  36.8 0.8 copy-done.8
  37.6 0.8 copy-done.10
  38.5 0.8 shard_map.120
  39.8 3.5 %all-to-all-start.3 = ((f32[4,2,24,768]{3,2,1,0:T(8,128)}), f32[4,2,24,768]{3,2,1,0:T(8,128)S(1)}, u32[]{:S(2)}, u32[]{:S(2)}) async-start(f32[4,2,24,768]{3,2,1,0:T(8,128)} %pad_maximum_fusion), calls=%async_computation.3 | async-start | bytes 1179648 | tf_op jit(solution)/shard_map/all_to_all | solution.py:148
  43.3 12.8 %collective-permute-done.1 = f32[2,96,768]{2,1,0:T(8,128)} collective-permute-done((f32[2,96,768]{2,1,0:T(8,128)}, f32[2,96,768]{2,1,0:T(8,128)}, u32[]{:S(2)}, u32[]{:S(2)}) %collective-permute-start.1) | collective-permute-done | bytes 589856 | tf_op jit(solution)/shard_map/ppermute | solution.py:142
  56.2 1.9 %collective-permute-start.10 = (f32[256,768]{1,0:T(8,128)S(1)}, f32[256,768]{1,0:T(8,128)}, u32[]{:S(2)}, u32[]{:S(2)}) collective-permute-start(f32[256,768]{1,0:T(8,128)S(1)} %bitcast.38), channel_id=1, source_target_pairs={{0,16},{8,24},{16,0},{24,8},{1,17},{9,25},{17,1},{25,9},{2,18},{10... | collective-permute-start | bytes 2359304 | tf_op jit(solution)/shard_map/ppermute | solution.py:142
  58.1 1.7 %collective-permute-start.9 = (f32[256,768]{1,0:T(8,128)S(1)}, f32[256,768]{1,0:T(8,128)}, u32[]{:S(2)}, u32[]{:S(2)}) collective-permute-start(f32[256,768]{1,0:T(8,128)S(1)} %bitcast.39), channel_id=1, source_target_pairs={{0,8},{8,0},{16,24},{24,16},{1,9},{9,1},{17,25},{25,17},{2,10},{10... | collective-permute-start | bytes 2359304 | tf_op jit(solution)/shard_map/ppermute | solution.py:142
  59.8 3.3 %all-to-all-start.2 = ((f32[4,32,128]{2,1,0:T(8,128)}), f32[4,32,128]{2,1,0:T(8,128)S(1)}, u32[]{:S(2)}, u32[]{:S(2)}) async-start(f32[4,32,128]{2,1,0:T(8,128)} %copy-done.11), calls=%async_computation.2 | async-start | bytes 131072 | tf_op jit(solution)/shard_map/all_to_all | solution.py:148
  63.1 2.4 %bitcast_add_fusion = (f32[2,96,768]{2,1,0:T(8,128)}, f32[2,96,768]{2,1,0:T(8,128)S(1)}) fusion(f32[2,4,24,768]{3,2,1,0:T(8,128)S(1)} %copy.17, f32[2,96,768]{2,1,0:T(8,128)} %collective-permute-done.1, f32[2,96,768]{2,1,0:T(8,128)} %collective-permute-done.2, f32[2,384,768]{2,1,0:T(8,128)} %bitcast.45, s32[]{:T(128)S(6)} %select_n.29), kind=kLoop, calls=%fused_computation.3 | loop fusion | flops 589824 | bytes 3538948 | tf_op jit(solution)/shard_map/add | solution.py:201
  65.5 0.9 copy.19
  66.4 0.8 all-to-all-done.2.back_ref
  67.2 3.5 %all-to-all-start.1 = ((f32[4,2,24,768]{3,2,1,0:T(8,128)}), f32[4,2,24,768]{3,2,1,0:T(8,128)S(1)}, u32[]{:S(2)}, u32[]{:S(2)}) async-start(f32[4,2,24,768]{3,2,1,0:T(8,128)} %bitcast.42), calls=%async_computation.1 | async-start | bytes 1179648 | tf_op jit(solution)/shard_map/all_to_all | solution.py:148
  70.7 1.9 %broadcast_in_dim.9 = f32[1024,768]{1,0:T(8,128)} broadcast(f32[]{:T(128)} %constant.14.clone.1), dimensions={} | broadcast | bytes 3145732 | tf_op jit(solution)/shard_map/broadcast_in_dim | solution.py:216
  72.5 0.9 constant_dynamic-update-slice_fusion.3
  73.5 2.6 %shard_map.121 = (f32[1,4,1,64,768]{4,3,2,1,0:T(8,128)}, f32[1,4,1,64,768]{4,3,2,1,0:T(8,128)}) custom-call(f32[1,4,1,64,768]{4,3,2,1,0:T(8,128)S(1)} %copy-done, f32[1,4,1,64,768]{4,3,2,1,0:T(8,128)S(1)} %copy-done.1, f32[256,64]{1,0:T(8,128)S(1)} %get-tuple-element.58.proj_ref, f32[4,32,128]{2,1,0:T(8,128)S(1)} %all-to-all-done.2.back_ref, ...), custom_call_target="tpu_custom_call" | custom-call | tf_op jit(solution)/shard_map/pallas_call | solution.py:228
  76.4 1.0 collective-permute-start.7
  77.5 1.1 constant_dynamic-update-slice_fusion.7
  78.7 15.2 %collective-permute-done.10 = f32[256,768]{1,0:T(8,128)} collective-permute-done((f32[256,768]{1,0:T(8,128)S(1)}, f32[256,768]{1,0:T(8,128)}, u32[]{:S(2)}, u32[]{:S(2)}) %collective-permute-start.10) | collective-permute-done | bytes 786464 | tf_op jit(solution)/shard_map/ppermute | solution.py:142
  93.9 12.3 %collective-permute-done.9 = f32[256,768]{1,0:T(8,128)} collective-permute-done((f32[256,768]{1,0:T(8,128)S(1)}, f32[256,768]{1,0:T(8,128)}, u32[]{:S(2)}, u32[]{:S(2)}) %collective-permute-start.9) | collective-permute-done | bytes 786464 | tf_op jit(solution)/shard_map/ppermute | solution.py:142
  106.2 2.1 %constant_dynamic-update-slice_fusion.2 = f32[1024,768]{1,0:T(8,128)} fusion(f32[1024,768]{1,0:T(8,128)} %constant_dynamic-update-slice_fusion.3, f32[256,768]{1,0:T(8,128)} %collective-permute-done.9, s32[]{:T(128)S(6)} %select_n.33), kind=kLoop, calls=%fused_computation.21 | loop fusion | bytes 1572868 | tf_op jit(solution)/shard_map/dynamic_update_slice | solution.py:218
  108.3 2.1 %constant_dynamic-update-slice_fusion.1 = f32[1024,768]{1,0:T(8,128)} fusion(f32[1024,768]{1,0:T(8,128)} %constant_dynamic-update-slice_fusion.2, f32[256,768]{1,0:T(8,128)} %collective-permute-done.10, s32[]{:T(128)S(6)} %select_n.34), kind=kLoop, calls=%fused_computation.20 | loop fusion | bytes 1572868 | tf_op jit(solution)/shard_map/dynamic_update_slice | solution.py:218
  110.4 7.9 %collective-permute-done.7 = f32[2,96,768]{2,1,0:T(8,128)} collective-permute-done((f32[2,96,768]{2,1,0:T(8,128)}, f32[2,96,768]{2,1,0:T(8,128)}, u32[]{:S(2)}, u32[]{:S(2)}) %collective-permute-start.7) | collective-permute-done | bytes 589856 | tf_op jit(solution)/shard_map/ppermute | solution.py:142
  118.3 2.4 %collective-permute-start.8 = (f32[2,96,768]{2,1,0:T(8,128)}, f32[2,96,768]{2,1,0:T(8,128)S(1)}, u32[]{:S(2)}, u32[]{:S(2)}) collective-permute-start(f32[2,96,768]{2,1,0:T(8,128)} %collective-permute-done.7), channel_id=1, source_target_pairs={{0,8},{8,0},{16,24},{24,16},{1,9},{9,1},{17,25},{25,17},{2,10},{10... | collective-permute-start | bytes 1769480 | tf_op jit(solution)/shard_map/ppermute | solution.py:142
  120.7 1.2 multiply_subtract_fusion
  121.9 1.1 constant_dynamic-update-slice_fusion.6
  123.0 1.1 constant_dynamic-update-slice_fusion.5
  124.1 11.6 %collective-permute-done.11 = f32[256,768]{1,0:T(8,128)} collective-permute-done((f32[256,768]{1,0:T(8,128)}, f32[256,768]{1,0:T(8,128)}, u32[]{:S(2)}, u32[]{:S(2)}) %collective-permute-start.11) | collective-permute-done | bytes 786464 | tf_op jit(solution)/shard_map/ppermute | solution.py:142
  135.7 2.1 %constant_dynamic-update-slice_fusion = f32[1024,768]{1,0:T(8,128)} fusion(f32[1024,768]{1,0:T(8,128)} %constant_dynamic-update-slice_fusion.1, f32[256,768]{1,0:T(8,128)} %collective-permute-done.11, s32[]{:T(128)S(6)} %select_n.35), kind=kLoop, calls=%fused_computation.19 | loop fusion | bytes 1572868 | tf_op jit(solution)/shard_map/dynamic_update_slice | solution.py:218
  137.8 10.3 %collective-permute-done.8 = f32[2,96,768]{2,1,0:T(8,128)S(1)} collective-permute-done((f32[2,96,768]{2,1,0:T(8,128)}, f32[2,96,768]{2,1,0:T(8,128)S(1)}, u32[]{:S(2)}, u32[]{:S(2)}) %collective-permute-start.8) | collective-permute-done | bytes 589856 | tf_op jit(solution)/shard_map/ppermute | solution.py:142
  148.1 1.4 copy-done.14
  (43 shorter events, 2.8 us)
Async XLA Ops:
  0.6 14.8 %copy-start = (f32[1,4,1,64,768]{4,3,2,1,0:T(8,128)S(1)}, f32[1,4,1,64,768]{4,3,2,1,0:T(8,128)}, u32[]{:S(2)}) copy-start(f32[1,4,1,64,768]{4,3,2,1,0:T(8,128)} %outer_ref.1) | copy-start | bytes 2359300
  0.6 14.7 %copy-start.1 = (f32[1,4,1,64,768]{4,3,2,1,0:T(8,128)S(1)}, f32[1,4,1,64,768]{4,3,2,1,0:T(8,128)}, u32[]{:S(2)}) copy-start(f32[1,4,1,64,768]{4,3,2,1,0:T(8,128)} %moment_ref.3) | copy-start | bytes 2359300
  1.9 18.9 %collective-permute-start = (f32[2,96,768]{2,1,0:T(8,128)S(1)}, f32[2,96,768]{2,1,0:T(8,128)}, u32[]{:S(2)}, u32[]{:S(2)}) collective-permute-start(f32[2,96,768]{2,1,0:T(8,128)S(1)} %dynamic-slice_bitcast_fusion), channel_id=1, source_target_pairs={{0,8},{8,0},{16,24},{24,16},{1,9},{9,1},{17,25},{25,17},{2,10},{10... | collective-permute-start | bytes 1769480 | tf_op jit(solution)/shard_map/ppermute | solution.py:142
  5.0 1.9 %copy-start.2 = (f32[1,1024,768]{2,1,0:T(8,128)S(1)}, f32[1,1024,768]{2,1,0:T(8,128)}, u32[]{:S(2)}) copy-start(f32[1,1024,768]{2,1,0:T(8,128)} %x_ref) | copy-start | bytes 9437188
  6.9 0.9 copy-start.3
  7.8 7.6 %copy-start.4 = (f32[64,768]{1,0:T(8,128)S(1)}, f32[64,768]{1,0:T(8,128)}, u32[]{:S(2)}) copy-start(f32[64,768]{1,0:T(8,128)} %basis_ref.7) | copy-start | bytes 589828
  10.9 22.5 %collective-permute-start.3 = (f32[4,32,128]{2,1,0:T(8,128)S(1)}, f32[4,32,128]{2,1,0:T(8,128)S(1)}, u32[]{:S(2)}, u32[]{:S(2)}) collective-permute-start(f32[4,32,128]{2,1,0:T(8,128)S(1)} %get-tuple-element.50), channel_id=1, source_target_pairs={{0,8},{8,0},{16,24},{24,16},{1,9},{9,1},{17,25},{25,17},{2,10},{10... | collective-permute-start | bytes 196616 | tf_op jit(solution)/shard_map/ppermute | solution.py:142
  11.0 23.0 %collective-permute-start.4 = (f32[4,32,128]{2,1,0:T(8,128)S(1)}, f32[4,32,128]{2,1,0:T(8,128)S(1)}, u32[]{:S(2)}, u32[]{:S(2)}) collective-permute-start(f32[4,32,128]{2,1,0:T(8,128)S(1)} %get-tuple-element.51), channel_id=1, source_target_pairs={{0,16},{8,24},{16,0},{24,8},{1,17},{9,25},{17,1},{25,9},{2,18},{10... | collective-permute-start | bytes 196616 | tf_op jit(solution)/shard_map/ppermute | solution.py:142
  14.0 20.6 %collective-permute-start.5 = (f32[4,32,128]{2,1,0:T(8,128)S(1)}, f32[4,32,128]{2,1,0:T(8,128)S(1)}, u32[]{:S(2)}, u32[]{:S(2)}) collective-permute-start(f32[4,32,128]{2,1,0:T(8,128)S(1)} %get-tuple-element.52), channel_id=1, source_target_pairs={{0,24},{8,16},{16,8},{24,0},{1,25},{9,17},{17,9},{25,1},{2,26},{10... | collective-permute-start | bytes 196616 | tf_op jit(solution)/shard_map/ppermute | solution.py:142
  20.8 15.1 %all-to-all-start = ((f32[4,64,768]{2,1,0:T(8,128)}), f32[4,64,768]{2,1,0:T(8,128)S(1)}, u32[]{:S(2)}, u32[]{:S(2)}) async-start(f32[4,64,768]{2,1,0:T(8,128)} %get-tuple-element.48), calls=%async_computation | async-start | bytes 1572864 | tf_op jit(solution)/shard_map/all_to_all | solution.py:148
  26.4 29.7 %collective-permute-start.1 = (f32[2,96,768]{2,1,0:T(8,128)}, f32[2,96,768]{2,1,0:T(8,128)}, u32[]{:S(2)}, u32[]{:S(2)}) collective-permute-start(f32[2,96,768]{2,1,0:T(8,128)} %dynamic-slice_add_fusion), channel_id=1, source_target_pairs={{0,16},{8,24},{16,0},{24,8},{1,17},{9,25},{17,1},{25,9},{2,18},{10... | collective-permute-start | bytes 1769480 | tf_op jit(solution)/shard_map/ppermute | solution.py:142
  28.4 27.7 %collective-permute-start.2 = (f32[2,96,768]{2,1,0:T(8,128)}, f32[2,96,768]{2,1,0:T(8,128)}, u32[]{:S(2)}, u32[]{:S(2)}) collective-permute-start(f32[2,96,768]{2,1,0:T(8,128)} %constant_dynamic-slice_fusion), channel_id=1, source_target_pairs={{0,8},{8,0},{16,24},{24,16},{1,9},{9,1},{17,25},{25,17},{2,10},{10... | collective-permute-start | bytes 1769480 | tf_op jit(solution)/shard_map/ppermute | solution.py:142
  33.4 0.6 copy-start.5
  34.0 0.6 copy-start.7
  34.7 0.6 copy-start.9
  35.9 0.8 copy-start.6
  36.8 0.8 copy-start.8
  37.6 0.8 copy-start.10
  39.2 0.6 copy-start.11
  39.8 20.0 %all-to-all-start.3 = ((f32[4,2,24,768]{3,2,1,0:T(8,128)}), f32[4,2,24,768]{3,2,1,0:T(8,128)S(1)}, u32[]{:S(2)}, u32[]{:S(2)}) async-start(f32[4,2,24,768]{3,2,1,0:T(8,128)} %pad_maximum_fusion), calls=%async_computation.3 | async-start | bytes 1179648 | tf_op jit(solution)/shard_map/all_to_all | solution.py:148
  56.2 37.7 %collective-permute-start.10 = (f32[256,768]{1,0:T(8,128)S(1)}, f32[256,768]{1,0:T(8,128)}, u32[]{:S(2)}, u32[]{:S(2)}) collective-permute-start(f32[256,768]{1,0:T(8,128)S(1)} %bitcast.38), channel_id=1, source_target_pairs={{0,16},{8,24},{16,0},{24,8},{1,17},{9,25},{17,1},{25,9},{2,18},{10... | collective-permute-start | bytes 2359304 | tf_op jit(solution)/shard_map/ppermute | solution.py:142
  58.1 48.1 %collective-permute-start.9 = (f32[256,768]{1,0:T(8,128)S(1)}, f32[256,768]{1,0:T(8,128)}, u32[]{:S(2)}, u32[]{:S(2)}) collective-permute-start(f32[256,768]{1,0:T(8,128)S(1)} %bitcast.39), channel_id=1, source_target_pairs={{0,8},{8,0},{16,24},{24,16},{1,9},{9,1},{17,25},{25,17},{2,10},{10... | collective-permute-start | bytes 2359304 | tf_op jit(solution)/shard_map/ppermute | solution.py:142
  59.8 7.4 %all-to-all-start.2 = ((f32[4,32,128]{2,1,0:T(8,128)}), f32[4,32,128]{2,1,0:T(8,128)S(1)}, u32[]{:S(2)}, u32[]{:S(2)}) async-start(f32[4,32,128]{2,1,0:T(8,128)} %copy-done.11), calls=%async_computation.2 | async-start | bytes 131072 | tf_op jit(solution)/shard_map/all_to_all | solution.py:148
  67.2 43.1 %all-to-all-start.1 = ((f32[4,2,24,768]{3,2,1,0:T(8,128)}), f32[4,2,24,768]{3,2,1,0:T(8,128)S(1)}, u32[]{:S(2)}, u32[]{:S(2)}) async-start(f32[4,2,24,768]{3,2,1,0:T(8,128)} %bitcast.42), calls=%async_computation.1 | async-start | bytes 1179648 | tf_op jit(solution)/shard_map/all_to_all | solution.py:148
  76.0 45.8 %collective-permute-start.6 = (f32[2,96,768]{2,1,0:T(8,128)}, f32[2,96,768]{2,1,0:T(8,128)}, u32[]{:S(2)}, u32[]{:S(2)}) collective-permute-start(f32[2,96,768]{2,1,0:T(8,128)} %get-tuple-element.64), channel_id=1, source_target_pairs={{0,8},{8,0},{16,24},{24,16},{1,9},{9,1},{17,25},{25,17},{2,10},{10... | collective-permute-start | bytes 1769480 | tf_op jit(solution)/shard_map/ppermute | solution.py:142
  76.4 41.9 %collective-permute-start.7 = (f32[2,96,768]{2,1,0:T(8,128)}, f32[2,96,768]{2,1,0:T(8,128)}, u32[]{:S(2)}, u32[]{:S(2)}) collective-permute-start(f32[2,96,768]{2,1,0:T(8,128)} %get-tuple-element.64), channel_id=1, source_target_pairs={{0,16},{8,24},{16,0},{24,8},{1,17},{9,25},{17,1},{25,9},{2,18},{10... | collective-permute-start | bytes 1769480 | tf_op jit(solution)/shard_map/ppermute | solution.py:142
  78.6 27.6 %copy-start.12 = (f32[2,384,768]{2,1,0:T(8,128)}, f32[2,384,768]{2,1,0:T(8,128)S(1)}, u32[]{:S(2)}) copy-start(f32[2,384,768]{2,1,0:T(8,128)S(1)} %constant_dynamic-update-slice_fusion.7) | copy-start | bytes 7077892
  78.7 42.0 %copy-start.15 = (f32[2,1,24,3072]{3,2,1,0:T(8,128)S(1)}, f32[2,1,24,3072]{3,2,1,0:T(8,128)}, u32[]{:S(2)}) copy-start(f32[2,1,24,3072]{3,2,1,0:T(8,128)} %param.9) | copy-start | bytes 1769476
  78.7 42.0 %copy-start.16 = (f32[2,1,24,3072]{3,2,1,0:T(8,128)S(1)}, f32[2,1,24,3072]{3,2,1,0:T(8,128)}, u32[]{:S(2)}) copy-start(f32[2,1,24,3072]{3,2,1,0:T(8,128)} %param.10) | copy-start | bytes 1769476
  93.9 41.8 %collective-permute-start.11 = (f32[256,768]{1,0:T(8,128)}, f32[256,768]{1,0:T(8,128)}, u32[]{:S(2)}, u32[]{:S(2)}) collective-permute-start(f32[256,768]{1,0:T(8,128)} %collective-permute-done.10), channel_id=1, source_target_pairs={{0,8},{8,0},{16,24},{24,16},{1,9},{9,1},{17,25},{25,17},{2,10},{10... | collective-permute-start | bytes 2359304 | tf_op jit(solution)/shard_map/ppermute | solution.py:142
  110.3 11.5 %copy-start.13 = (f32[2,384,768]{2,1,0:T(8,128)S(1)}, f32[2,384,768]{2,1,0:T(8,128)}, u32[]{:S(2)}) copy-start(f32[2,384,768]{2,1,0:T(8,128)} %copy-done.12) | copy-start | bytes 7077892
  118.3 29.7 %collective-permute-start.8 = (f32[2,96,768]{2,1,0:T(8,128)}, f32[2,96,768]{2,1,0:T(8,128)S(1)}, u32[]{:S(2)}, u32[]{:S(2)}) collective-permute-start(f32[2,96,768]{2,1,0:T(8,128)} %collective-permute-done.7), channel_id=1, source_target_pairs={{0,8},{8,0},{16,24},{24,16},{1,9},{9,1},{17,25},{25,17},{2,10},{10... | collective-permute-start | bytes 1769480 | tf_op jit(solution)/shard_map/ppermute | solution.py:142
  148.1 1.4 copy-start.14

commit v5 on v4

--- a/solution.py
+++ b/solution.py
@@ -160,10 +160,18 @@
     def block(d):
         return lax.dynamic_slice(dense, (0, (me ^ d) * block_rows, 0), (2, block_rows, cols))
 
-    far, inner_emb, outer_emb, outer_dense, dense = meet(
-        block(3), inner_emb, outer_emb, outer_dense, dense
-    )
-    far = send(far, 1)
+    def half(d, h):
+        return lax.dynamic_slice(dense, (h, (me ^ d) * block_rows, 0), (1, block_rows, cols))
+
+    low, high, inner_emb, outer_emb, outer_dense, dense = meet(
+        jnp.concatenate([half(3, 0), half(1, 0)]),
+        jnp.concatenate([half(2, 1), half(3, 1)]),
+        inner_emb,
+        outer_emb,
+        outer_dense,
+        dense,
+    )
+    low, high = send(low, 1), send(high, 2)
 
     p3, p2, p1, p0 = project(inner_emb, basis, me.reshape(1).astype(jnp.int32), groups, tp_count)
     p3, p2, p1, p0, outer_emb = meet(p3, p2, p1, p0, outer_emb)
@@ -175,11 +183,11 @@
         flops=24 * emb_rows * width * rank,
         size=12 * emb_rows * width,
     )(outer_emb, moment_emb, basis)
-    own, near, second = block(0), block(1), block(2)
-    far, emb_base, near = meet(far, emb_base, near)
+    own = block(0)
+    low, emb_base = meet(low, emb_base)
     emb_base = swap(emb_base)
-    across = send(second + far, 2)
-    near = send(near, 1)
+    across = send(half(2, 0) + low[:1], 2)
+    near = send(half(1, 1) + high[1:], 1)
     dense_outer = outer_dense[:, 0]
     dense_moment = moment_dense[:, 0]
     dense_base = (1.0 - grad_weight) * dense_outer - moment_weight * dense_moment
@@ -195,7 +203,7 @@
     emb_block, proj_sum, dense_base = meet(emb_block, proj_sum, dense_base)
     dense_base = swap(dense_base)
     across, near, emb_block = meet(across, near, emb_block)
-    dense_sum = own + near + across
+    dense_sum = own + jnp.concatenate([low[1:] + across, high[:1] + near])
     emb_block = emb_block.reshape(emb_rows, width)
     dense_block = (
         dense_base.transpose(1, 0, 2, 3).reshape(2, block_rows, cols) + weight * dense_sum

time: 151 us -> 149 us (0.987)
  waiting for transfers between devices: 71.6 us -> 66.5 us
  other arithmetic: 7.88 us -> 11.9 us
  local copies, waits for them, and re-layouts: 25.9 us -> 21.9 us
  starting transfers between devices: 33.3 us -> 36.4 us
    ppermute x12 -> x13, waiting for transfers between devices: 70.2 us -> 59.6 us  [send(): return lax.ppermute(x, 'rep', [(i, i ^ d) for i in range(groups)])]
    all_to_all x4, waiting for transfers between devices: 1.43 us -> 6.92 us  [swap(): return lax.all_to_all(x, 'tp', split_axis=0, concat_axis=0, tiled=True)]
    add x1 -> x3, other arithmetic: 2.13 us -> 5.7 us  [the longest x2 3.59 us: per_device(): dense_sum = own + jnp.concatenate([low[1:] + across, high[:1] + near])]
    unnamed x34, local copies, waits for them, and re-layouts: 9.28 us -> 5.86 us
    ppermute x12 -> x13, starting transfers between devices: 19.6 us -> 22.6 us  [send(): return lax.ppermute(x, 'rep', [(i, i ^ d) for i in range(groups)])]
    dynamic_slice x2 -> x1, local copies, waits for them, and re-layouts: 3.14 us -> 1.47 us  [half(): lax.dynamic_slice(dense, (h, (me ^ d) * block_rows, 0), (1, block_rows, c...]
  transfers between devices with their start and end apart: 16 -> 17, of which waited for: 9 -> 10; matrix products, arithmetic and copies ran while one was open for 16% -> 17% of each run, Pallas kernels for 7% -> 7%
where the time goes in v5:
time: 149 us; the launch traced here: 148 us
  waiting for transfers between devices  66.5 us (45%)
  starting transfers between devices  36.4 us (24%)
  local copies, waits for them, and re-layouts  21.9 us (15%)
  other arithmetic  11.9 us (8%)
  Pallas kernels  9.98 us (7%)
    ppermute x13, waiting for transfers between devices, send(): return lax.ppermute(x, 'rep', [(i, i ^ d) for i in range(groups)])  59.6 us
    ppermute x13, starting transfers between devices, send(): return lax.ppermute(x, 'rep', [(i, i ^ d) for i in range(groups)])  22.6 us
    all_to_all x4, starting transfers between devices, swap(): return lax.all_to_all(x, 'tp', split_axis=0, concat_axis=0, tiled=True)  13.7 us
    dynamic_update_slice x4, local copies, waits for them, and re-layouts, per_device(): lax.dynamic_update_slice(embed_train, value, ((me ^ d) * emb_rows, 0))  7.12 us
    all_to_all x4, waiting for transfers between devices, swap(): return lax.all_to_all(x, 'tp', split_axis=0, concat_axis=0, tiled=True)  6.92 us
    unnamed x34, local copies, waits for them, and re-layouts  5.86 us
    add x2, other arithmetic, per_device(): dense_sum = own + jnp.concatenate([low[1:] + across, high[:1] + near])  3.59 us
    pallas_call x1, Pallas kernels, per_device(): call(emb_base_body, [shaped(tp_count, piece_rows, width), shaped(emb_rows...  3.49 us
  transfers between devices with their start and end apart: 17, of which 10 were waited for; matrix products, arithmetic and copies ran while one was open for 17% of the time, Pallas kernels for 7%

profile of v5, /device:TPU:0, one launch (start us, length us, event | category | flops | bytes accessed | tf_op | source)
XLA Modules:
  0.0 147.6 jit_solution(3517901295874523162)
XLA Ops:
  0.7 1.5 dynamic-slice_bitcast_fusion.1
  2.2 1.1 pad_maximum_fusion
  3.3 3.0 %collective-permute-start = (f32[2,96,768]{2,1,0:T(8,128)}, f32[2,96,768]{2,1,0:T(8,128)}, u32[]{:S(2)}, u32[]{:S(2)}) collective-permute-start(f32[2,96,768]{2,1,0:T(8,128)} %get-tuple-element.37), channel_id=1, source_target_pairs={{0,8},{8,0},{16,24},{24,16},{1,9},{9,1},{17,25},{25,17},{2,10},{10... | collective-permute-start | bytes 1769480 | tf_op jit(solution)/shard_map/ppermute | solution.py:142
  6.3 2.6 %collective-permute-start.2 = (f32[2,96,768]{2,1,0:T(8,128)}, f32[2,96,768]{2,1,0:T(8,128)}, u32[]{:S(2)}, u32[]{:S(2)}) collective-permute-start(f32[2,96,768]{2,1,0:T(8,128)} %get-tuple-element.47), channel_id=1, source_target_pairs={{0,16},{8,24},{16,0},{24,8},{1,17},{9,25},{17,1},{25,9},{2,18},{10... | collective-permute-start | bytes 1769480 | tf_op jit(solution)/shard_map/ppermute | solution.py:142
  8.9 3.1 %shard_map.118 = (f32[4,32,128]{2,1,0:T(8,128)S(1)}, f32[4,32,128]{2,1,0:T(8,128)S(1)}, f32[4,32,128]{2,1,0:T(8,128)S(1)}, f32[4,32,128]{2,1,0:T(8,128)S(1)}) custom-call(s32[1]{0:T(128)} %bitcast.5.me_ref, f32[1,1024,768]{2,1,0:T(8,128)S(1)} %copy-done.2, f32[64,768]{1,0:T(8,128)S(1)} %copy-done.3), custom_call_target="tpu_custom_call" | custom-call | tf_op jit(solution)/shard_map/pallas_call | solution.py:73
  12.6 3.9 %collective-permute-start.6 = (f32[4,32,128]{2,1,0:T(8,128)S(1)}, f32[4,32,128]{2,1,0:T(8,128)S(1)}, u32[]{:S(2)}, u32[]{:S(2)}) collective-permute-start(f32[4,32,128]{2,1,0:T(8,128)S(1)} %get-tuple-element.52), channel_id=1, source_target_pairs={{0,24},{8,16},{16,8},{24,0},{1,25},{9,17},{17,9},{25,1},{2,26},{10... | collective-permute-start | bytes 196616 | tf_op jit(solution)/shard_map/ppermute | solution.py:142
  16.5 3.5 %shard_map.119 = (f32[4,64,768]{2,1,0:T(8,128)}, f32[256,64]{1,0:T(8,128)S(1)}) custom-call(f32[1,4,1,64,768]{4,3,2,1,0:T(8,128)S(1)} %copy-done, f32[1,4,1,64,768]{4,3,2,1,0:T(8,128)S(1)} %copy-done.1, f32[64,768]{1,0:T(8,128)S(1)} %copy-done.3), custom_call_target="tpu_custom_call" | custom-call | tf_op jit(solution)/shard_map/pallas_call | solution.py:179
  20.0 0.9 subtract_bitcast_fusion
  20.9 12.2 %collective-permute-done = f32[2,96,768]{2,1,0:T(8,128)} collective-permute-done((f32[2,96,768]{2,1,0:T(8,128)}, f32[2,96,768]{2,1,0:T(8,128)}, u32[]{:S(2)}, u32[]{:S(2)}) %collective-permute-start) | collective-permute-done | bytes 589856 | tf_op jit(solution)/shard_map/ppermute | solution.py:142
  33.1 3.5 %all-to-all-start = ((f32[4,64,768]{2,1,0:T(8,128)}), f32[4,64,768]{2,1,0:T(8,128)S(1)}, u32[]{:S(2)}, u32[]{:S(2)}) async-start(f32[4,64,768]{2,1,0:T(8,128)} %get-tuple-element.48), calls=%async_computation | async-start | bytes 1572864 | tf_op jit(solution)/shard_map/all_to_all | solution.py:148
  36.6 2.5 %collective-permute-done.2 = f32[2,96,768]{2,1,0:T(8,128)} collective-permute-done((f32[2,96,768]{2,1,0:T(8,128)}, f32[2,96,768]{2,1,0:T(8,128)}, u32[]{:S(2)}, u32[]{:S(2)}) %collective-permute-start.2) | collective-permute-done | bytes 589856 | tf_op jit(solution)/shard_map/ppermute | solution.py:142
  39.2 2.1 %slice_add_fusion.1 = (f32[1,96,768]{2,1,0:T(8,128)}, f32[1,96,768]{2,1,0:T(8,128)}) fusion(f32[2,96,768]{2,1,0:T(8,128)} %collective-permute-done.2, f32[2,384,768]{2,1,0:T(8,128)} %bitcast.47, s32[]{:T(128)S(6)} %select_n.32, f32[2,96,768]{2,1,0:T(8,128)} %collective-permute-done, s32[]{:T(128)S(6)} %select_n.33), kind=kLoop, calls=%fused_computation.12 | loop fusion | flops 147456 | bytes 1769480 | tf_op jit(solution)/shard_map/add | solution.py:190
  41.3 3.0 %collective-permute-start.3 = (f32[1,96,768]{2,1,0:T(8,128)}, f32[1,96,768]{2,1,0:T(8,128)}, u32[]{:S(2)}, u32[]{:S(2)}) collective-permute-start(f32[1,96,768]{2,1,0:T(8,128)} %get-tuple-element.68), channel_id=1, source_target_pairs={{0,8},{8,0},{16,24},{24,16},{1,9},{9,1},{17,25},{25,17},{2,10},{10... | collective-permute-start | bytes 884744 | tf_op jit(solution)/shard_map/ppermute | solution.py:142
  44.3 1.2 slice_bitcast_fusion.7
  45.5 0.9 pad_maximum_fusion.2
  46.4 0.6 copy-done.4
  48.3 0.8 copy-done.5
  49.1 0.8 copy-done.7
  50.0 0.8 copy-done.9
  50.8 0.8 shard_map.120
  51.6 4.2 %collective-permute-done.1 = f32[1,96,768]{2,1,0:T(8,128)} collective-permute-done((f32[1,96,768]{2,1,0:T(8,128)}, f32[1,96,768]{2,1,0:T(8,128)}, u32[]{:S(2)}, u32[]{:S(2)}) %collective-permute-start.1) | collective-permute-done | bytes 294944 | tf_op jit(solution)/shard_map/ppermute | solution.py:142
  56.1 2.6 %collective-permute-start.11 = (f32[256,768]{1,0:T(8,128)S(1)}, f32[256,768]{1,0:T(8,128)}, u32[]{:S(2)}, u32[]{:S(2)}) collective-permute-start(f32[256,768]{1,0:T(8,128)S(1)} %bitcast.45), channel_id=1, source_target_pairs={{0,16},{8,24},{16,0},{24,8},{1,17},{9,25},{17,1},{25,9},{2,18},{10... | collective-permute-start | bytes 2359304 | tf_op jit(solution)/shard_map/ppermute | solution.py:142
  58.6 3.5 %all-to-all-start.3 = ((f32[4,2,24,768]{3,2,1,0:T(8,128)}), f32[4,2,24,768]{3,2,1,0:T(8,128)S(1)}, u32[]{:S(2)}, u32[]{:S(2)}) async-start(f32[4,2,24,768]{3,2,1,0:T(8,128)} %pad_maximum_fusion.2), calls=%async_computation.3 | async-start | bytes 1179648 | tf_op jit(solution)/shard_map/all_to_all | solution.py:148
  62.1 1.8 %slice_add_fusion.3 = f32[1,96,768]{2,1,0:T(8,128)} fusion(f32[1,96,768]{2,1,0:T(8,128)} %collective-permute-done.1, f32[2,96,768]{2,1,0:T(8,128)} %collective-permute-done), kind=kLoop, calls=%fused_computation.14 | loop fusion | flops 73728 | bytes 884736 | tf_op jit(solution)/shard_map/add | solution.py:206
  63.9 1.8 %slice_add_fusion = f32[1,96,768]{2,1,0:T(8,128)} fusion(f32[1,96,768]{2,1,0:T(8,128)} %collective-permute-done.3, f32[2,96,768]{2,1,0:T(8,128)} %collective-permute-done.2), kind=kLoop, calls=%fused_computation.11 | loop fusion | flops 73728 | bytes 884736 | tf_op jit(solution)/shard_map/add | solution.py:206
  65.7 5.9 %all-to-all-done.3 = f32[4,2,24,768]{3,2,1,0:T(8,128)S(1)} async-done(((f32[4,2,24,768]{3,2,1,0:T(8,128)}), f32[4,2,24,768]{3,2,1,0:T(8,128)S(1)}, u32[]{:S(2)}, u32[]{:S(2)}) %all-to-all-start.3) | async-done | bytes 589856 | tf_op jit(solution)/shard_map/all_to_all | solution.py:148
  71.6 3.3 %all-to-all-start.2 = ((f32[4,32,128]{2,1,0:T(8,128)}), f32[4,32,128]{2,1,0:T(8,128)S(1)}, u32[]{:S(2)}, u32[]{:S(2)}) async-start(f32[4,32,128]{2,1,0:T(8,128)} %get-tuple-element.59), calls=%async_computation.2 | async-start | bytes 131072 | tf_op jit(solution)/shard_map/all_to_all | solution.py:148
  75.0 2.2 %bitcast_add_fusion = (f32[2,96,768]{2,1,0:T(8,128)}, f32[2,96,768]{2,1,0:T(8,128)S(1)}) fusion(f32[2,4,24,768]{3,2,1,0:T(8,128)S(1)} %copy.17, f32[1,96,768]{2,1,0:T(8,128)} %slice_add_fusion, f32[1,96,768]{2,1,0:T(8,128)} %slice_add_fusion.3, f32[2,384,768]{2,1,0:T(8,128)} %bitcast.48, s32[]{:T(128)S(6)} %select_n.34), kind=kLoop, calls=%fused_computation.6 | loop fusion | flops 589824 | bytes 2949124 | tf_op jit(solution)/shard_map/add | solution.py:209
  77.2 0.9 copy.19
  78.0 1.0 all-to-all-done.2.back_ref
  79.0 3.5 %all-to-all-start.1 = ((f32[4,2,24,768]{3,2,1,0:T(8,128)}), f32[4,2,24,768]{3,2,1,0:T(8,128)S(1)}, u32[]{:S(2)}, u32[]{:S(2)}) async-start(f32[4,2,24,768]{3,2,1,0:T(8,128)} %bitcast.49), calls=%async_computation.1 | async-start | bytes 1179648 | tf_op jit(solution)/shard_map/all_to_all | solution.py:148
  82.5 1.9 %broadcast_in_dim.9 = f32[1024,768]{1,0:T(8,128)} broadcast(f32[]{:T(128)} %constant.37.clone.1), dimensions={} | broadcast | bytes 3145732 | tf_op jit(solution)/shard_map/broadcast_in_dim | solution.py:224
  84.4 0.9 constant_dynamic-update-slice_fusion.3
  85.3 2.6 %shard_map.121 = (f32[1,4,1,64,768]{4,3,2,1,0:T(8,128)}, f32[1,4,1,64,768]{4,3,2,1,0:T(8,128)}) custom-call(f32[1,4,1,64,768]{4,3,2,1,0:T(8,128)S(1)} %copy-done, f32[1,4,1,64,768]{4,3,2,1,0:T(8,128)S(1)} %copy-done.1, f32[256,64]{1,0:T(8,128)S(1)} %get-tuple-element.58.proj_ref, f32[4,32,128]{2,1,0:T(8,128)S(1)} %all-to-all-done.2.back_ref, ...), custom_call_target="tpu_custom_call" | custom-call | tf_op jit(solution)/shard_map/pallas_call | solution.py:236
  88.2 1.8 %collective-permute-start.8 = (f32[2,96,768]{2,1,0:T(8,128)}, f32[2,96,768]{2,1,0:T(8,128)}, u32[]{:S(2)}, u32[]{:S(2)}) collective-permute-start(f32[2,96,768]{2,1,0:T(8,128)} %get-tuple-element.64), channel_id=1, source_target_pairs={{0,16},{8,24},{16,0},{24,8},{1,17},{9,25},{17,1},{25,9},{2,18},{10... | collective-permute-start | bytes 1769480 | tf_op jit(solution)/shard_map/ppermute | solution.py:142
  90.2 1.1 constant_dynamic-update-slice_fusion.7
  92.0 2.4 %collective-permute-start.12 = (f32[256,768]{1,0:T(8,128)}, f32[256,768]{1,0:T(8,128)}, u32[]{:S(2)}, u32[]{:S(2)}) collective-permute-start(f32[256,768]{1,0:T(8,128)} %collective-permute-done.11), channel_id=1, source_target_pairs={{0,8},{8,0},{16,24},{24,16},{1,9},{9,1},{17,25},{25,17},{2,10},{10... | collective-permute-start | bytes 2359304 | tf_op jit(solution)/shard_map/ppermute | solution.py:142
  94.4 2.1 %constant_dynamic-update-slice_fusion.2 = f32[1024,768]{1,0:T(8,128)} fusion(f32[1024,768]{1,0:T(8,128)} %constant_dynamic-update-slice_fusion.3, f32[256,768]{1,0:T(8,128)} %collective-permute-done.10, s32[]{:T(128)S(6)} %select_n.36), kind=kLoop, calls=%fused_computation.29 | loop fusion | bytes 1572868 | tf_op jit(solution)/shard_map/dynamic_update_slice | solution.py:226
  96.4 2.1 %constant_dynamic-update-slice_fusion.1 = f32[1024,768]{1,0:T(8,128)} fusion(f32[1024,768]{1,0:T(8,128)} %constant_dynamic-update-slice_fusion.2, f32[256,768]{1,0:T(8,128)} %collective-permute-done.11, s32[]{:T(128)S(6)} %select_n.37), kind=kLoop, calls=%fused_computation.28 | loop fusion | bytes 1572868 | tf_op jit(solution)/shard_map/dynamic_update_slice | solution.py:226
  98.6 19.0 %collective-permute-done.8 = f32[2,96,768]{2,1,0:T(8,128)} collective-permute-done((f32[2,96,768]{2,1,0:T(8,128)}, f32[2,96,768]{2,1,0:T(8,128)}, u32[]{:S(2)}, u32[]{:S(2)}) %collective-permute-start.8) | collective-permute-done | bytes 589856 | tf_op jit(solution)/shard_map/ppermute | solution.py:142
  117.5 2.2 %collective-permute-start.9 = (f32[2,96,768]{2,1,0:T(8,128)}, f32[2,96,768]{2,1,0:T(8,128)S(1)}, u32[]{:S(2)}, u32[]{:S(2)}) collective-permute-start(f32[2,96,768]{2,1,0:T(8,128)} %collective-permute-done.8), channel_id=1, source_target_pairs={{0,8},{8,0},{16,24},{24,16},{1,9},{9,1},{17,25},{25,17},{2,10},{10... | collective-permute-start | bytes 1769480 | tf_op jit(solution)/shard_map/ppermute | solution.py:142
  119.7 1.2 multiply_subtract_fusion
  120.9 1.1 constant_dynamic-update-slice_fusion.6
  122.0 1.1 constant_dynamic-update-slice_fusion.5
  123.1 10.8 %collective-permute-done.12 = f32[256,768]{1,0:T(8,128)} collective-permute-done((f32[256,768]{1,0:T(8,128)}, f32[256,768]{1,0:T(8,128)}, u32[]{:S(2)}, u32[]{:S(2)}) %collective-permute-start.12) | collective-permute-done | bytes 786464 | tf_op jit(solution)/shard_map/ppermute | solution.py:142
  133.9 2.1 %constant_dynamic-update-slice_fusion = f32[1024,768]{1,0:T(8,128)} fusion(f32[1024,768]{1,0:T(8,128)} %constant_dynamic-update-slice_fusion.1, f32[256,768]{1,0:T(8,128)} %collective-permute-done.12, s32[]{:T(128)S(6)} %select_n.38), kind=kLoop, calls=%fused_computation.27 | loop fusion | bytes 1572868 | tf_op jit(solution)/shard_map/dynamic_update_slice | solution.py:226
  136.0 10.2 %collective-permute-done.9 = f32[2,96,768]{2,1,0:T(8,128)S(1)} collective-permute-done((f32[2,96,768]{2,1,0:T(8,128)}, f32[2,96,768]{2,1,0:T(8,128)S(1)}, u32[]{:S(2)}, u32[]{:S(2)}) %collective-permute-start.9) | collective-permute-done | bytes 589856 | tf_op jit(solution)/shard_map/ppermute | solution.py:142
  146.2 1.4 copy-done.12
  (47 shorter events, 3.4 us)
Async XLA Ops:
  0.7 8.2 %copy-start.2 = (f32[1,1024,768]{2,1,0:T(8,128)S(1)}, f32[1,1024,768]{2,1,0:T(8,128)}, u32[]{:S(2)}) copy-start(f32[1,1024,768]{2,1,0:T(8,128)} %x_ref) | copy-start | bytes 9437188
  0.7 8.2 %copy-start.3 = (f32[64,768]{1,0:T(8,128)S(1)}, f32[64,768]{1,0:T(8,128)}, u32[]{:S(2)}) copy-start(f32[64,768]{1,0:T(8,128)} %basis_ref.7) | copy-start | bytes 589828
  2.1 14.3 %copy-start = (f32[1,4,1,64,768]{4,3,2,1,0:T(8,128)S(1)}, f32[1,4,1,64,768]{4,3,2,1,0:T(8,128)}, u32[]{:S(2)}) copy-start(f32[1,4,1,64,768]{4,3,2,1,0:T(8,128)} %outer_ref.1) | copy-start | bytes 2359300
  2.2 14.3 %copy-start.1 = (f32[1,4,1,64,768]{4,3,2,1,0:T(8,128)S(1)}, f32[1,4,1,64,768]{4,3,2,1,0:T(8,128)}, u32[]{:S(2)}) copy-start(f32[1,4,1,64,768]{4,3,2,1,0:T(8,128)} %moment_ref.3) | copy-start | bytes 2359300
  3.3 29.9 %collective-permute-start = (f32[2,96,768]{2,1,0:T(8,128)}, f32[2,96,768]{2,1,0:T(8,128)}, u32[]{:S(2)}, u32[]{:S(2)}) collective-permute-start(f32[2,96,768]{2,1,0:T(8,128)} %get-tuple-element.37), channel_id=1, source_target_pairs={{0,8},{8,0},{16,24},{24,16},{1,9},{9,1},{17,25},{25,17},{2,10},{10... | collective-permute-start | bytes 1769480 | tf_op jit(solution)/shard_map/ppermute | solution.py:142
  6.3 32.9 %collective-permute-start.2 = (f32[2,96,768]{2,1,0:T(8,128)}, f32[2,96,768]{2,1,0:T(8,128)}, u32[]{:S(2)}, u32[]{:S(2)}) collective-permute-start(f32[2,96,768]{2,1,0:T(8,128)} %get-tuple-element.47), channel_id=1, source_target_pairs={{0,16},{8,24},{16,0},{24,8},{1,17},{9,25},{17,1},{25,9},{2,18},{10... | collective-permute-start | bytes 1769480 | tf_op jit(solution)/shard_map/ppermute | solution.py:142
  8.9 11.1 %copy-start.13 = (f32[2,1,24,3072]{3,2,1,0:T(8,128)S(1)}, f32[2,1,24,3072]{3,2,1,0:T(8,128)}, u32[]{:S(2)}) copy-start(f32[2,1,24,3072]{3,2,1,0:T(8,128)} %param.9) | copy-start | bytes 1769476
  8.9 11.1 %copy-start.15 = (f32[2,1,24,3072]{3,2,1,0:T(8,128)S(1)}, f32[2,1,24,3072]{3,2,1,0:T(8,128)}, u32[]{:S(2)}) copy-start(f32[2,1,24,3072]{3,2,1,0:T(8,128)} %param.10) | copy-start | bytes 1769476
  12.0 34.3 %collective-permute-start.4 = (f32[4,32,128]{2,1,0:T(8,128)S(1)}, f32[4,32,128]{2,1,0:T(8,128)S(1)}, u32[]{:S(2)}, u32[]{:S(2)}) collective-permute-start(f32[4,32,128]{2,1,0:T(8,128)S(1)} %get-tuple-element.50), channel_id=1, source_target_pairs={{0,8},{8,0},{16,24},{24,16},{1,9},{9,1},{17,25},{25,17},{2,10},{10... | collective-permute-start | bytes 196616 | tf_op jit(solution)/shard_map/ppermute | solution.py:142
  12.6 34.4 %collective-permute-start.5 = (f32[4,32,128]{2,1,0:T(8,128)S(1)}, f32[4,32,128]{2,1,0:T(8,128)S(1)}, u32[]{:S(2)}, u32[]{:S(2)}) collective-permute-start(f32[4,32,128]{2,1,0:T(8,128)S(1)} %get-tuple-element.51), channel_id=1, source_target_pairs={{0,16},{8,24},{16,0},{24,8},{1,17},{9,25},{17,1},{25,9},{2,18},{10... | collective-permute-start | bytes 196616 | tf_op jit(solution)/shard_map/ppermute | solution.py:142
  12.6 35.0 %collective-permute-start.6 = (f32[4,32,128]{2,1,0:T(8,128)S(1)}, f32[4,32,128]{2,1,0:T(8,128)S(1)}, u32[]{:S(2)}, u32[]{:S(2)}) collective-permute-start(f32[4,32,128]{2,1,0:T(8,128)S(1)} %get-tuple-element.52), channel_id=1, source_target_pairs={{0,24},{8,16},{16,8},{24,0},{1,25},{9,17},{17,9},{25,1},{2,26},{10... | collective-permute-start | bytes 196616 | tf_op jit(solution)/shard_map/ppermute | solution.py:142
  33.1 15.1 %all-to-all-start = ((f32[4,64,768]{2,1,0:T(8,128)}), f32[4,64,768]{2,1,0:T(8,128)S(1)}, u32[]{:S(2)}, u32[]{:S(2)}) async-start(f32[4,64,768]{2,1,0:T(8,128)} %get-tuple-element.48), calls=%async_computation | async-start | bytes 1572864 | tf_op jit(solution)/shard_map/all_to_all | solution.py:148
  41.3 14.5 %collective-permute-start.1 = (f32[1,96,768]{2,1,0:T(8,128)}, f32[1,96,768]{2,1,0:T(8,128)}, u32[]{:S(2)}, u32[]{:S(2)}) collective-permute-start(f32[1,96,768]{2,1,0:T(8,128)} %get-tuple-element.69), channel_id=1, source_target_pairs={{0,16},{8,24},{16,0},{24,8},{1,17},{9,25},{17,1},{25,9},{2,18},{10... | collective-permute-start | bytes 884744 | tf_op jit(solution)/shard_map/ppermute | solution.py:142
  41.3 14.6 %collective-permute-start.3 = (f32[1,96,768]{2,1,0:T(8,128)}, f32[1,96,768]{2,1,0:T(8,128)}, u32[]{:S(2)}, u32[]{:S(2)}) collective-permute-start(f32[1,96,768]{2,1,0:T(8,128)} %get-tuple-element.68), channel_id=1, source_target_pairs={{0,8},{8,0},{16,24},{24,16},{1,9},{9,1},{17,25},{25,17},{2,10},{10... | collective-permute-start | bytes 884744 | tf_op jit(solution)/shard_map/ppermute | solution.py:142
  46.4 0.6 copy-start.4
  47.0 0.6 copy-start.6
  47.6 0.6 copy-start.8
  48.3 0.8 copy-start.5
  49.1 0.8 copy-start.7
  50.0 0.8 copy-start.9
  55.9 38.5 %collective-permute-start.10 = (f32[256,768]{1,0:T(8,128)S(1)}, f32[256,768]{1,0:T(8,128)}, u32[]{:S(2)}, u32[]{:S(2)}) collective-permute-start(f32[256,768]{1,0:T(8,128)S(1)} %bitcast.44), channel_id=1, source_target_pairs={{0,8},{8,0},{16,24},{24,16},{1,9},{9,1},{17,25},{25,17},{2,10},{10... | collective-permute-start | bytes 2359304 | tf_op jit(solution)/shard_map/ppermute | solution.py:142
  56.1 35.9 %collective-permute-start.11 = (f32[256,768]{1,0:T(8,128)S(1)}, f32[256,768]{1,0:T(8,128)}, u32[]{:S(2)}, u32[]{:S(2)}) collective-permute-start(f32[256,768]{1,0:T(8,128)S(1)} %bitcast.45), channel_id=1, source_target_pairs={{0,16},{8,24},{16,0},{24,8},{1,17},{9,25},{17,1},{25,9},{2,18},{10... | collective-permute-start | bytes 2359304 | tf_op jit(solution)/shard_map/ppermute | solution.py:142
  58.6 13.0 %all-to-all-start.3 = ((f32[4,2,24,768]{3,2,1,0:T(8,128)}), f32[4,2,24,768]{3,2,1,0:T(8,128)S(1)}, u32[]{:S(2)}, u32[]{:S(2)}) async-start(f32[4,2,24,768]{3,2,1,0:T(8,128)} %pad_maximum_fusion.2), calls=%async_computation.3 | async-start | bytes 1179648 | tf_op jit(solution)/shard_map/all_to_all | solution.py:148
  71.6 7.4 %all-to-all-start.2 = ((f32[4,32,128]{2,1,0:T(8,128)}), f32[4,32,128]{2,1,0:T(8,128)S(1)}, u32[]{:S(2)}, u32[]{:S(2)}) async-start(f32[4,32,128]{2,1,0:T(8,128)} %get-tuple-element.59), calls=%async_computation.2 | async-start | bytes 131072 | tf_op jit(solution)/shard_map/all_to_all | solution.py:148
  79.0 19.5 %all-to-all-start.1 = ((f32[4,2,24,768]{3,2,1,0:T(8,128)}), f32[4,2,24,768]{3,2,1,0:T(8,128)S(1)}, u32[]{:S(2)}, u32[]{:S(2)}) async-start(f32[4,2,24,768]{3,2,1,0:T(8,128)} %bitcast.49), calls=%async_computation.1 | async-start | bytes 1179648 | tf_op jit(solution)/shard_map/all_to_all | solution.py:148
  87.9 33.0 %collective-permute-start.7 = (f32[2,96,768]{2,1,0:T(8,128)}, f32[2,96,768]{2,1,0:T(8,128)}, u32[]{:S(2)}, u32[]{:S(2)}) collective-permute-start(f32[2,96,768]{2,1,0:T(8,128)} %get-tuple-element.64), channel_id=1, source_target_pairs={{0,8},{8,0},{16,24},{24,16},{1,9},{9,1},{17,25},{25,17},{2,10},{10... | collective-permute-start | bytes 1769480 | tf_op jit(solution)/shard_map/ppermute | solution.py:142
  88.2 29.3 %collective-permute-start.8 = (f32[2,96,768]{2,1,0:T(8,128)}, f32[2,96,768]{2,1,0:T(8,128)}, u32[]{:S(2)}, u32[]{:S(2)}) collective-permute-start(f32[2,96,768]{2,1,0:T(8,128)} %get-tuple-element.64), channel_id=1, source_target_pairs={{0,16},{8,24},{16,0},{24,8},{1,17},{9,25},{17,1},{25,9},{2,18},{10... | collective-permute-start | bytes 1769480 | tf_op jit(solution)/shard_map/ppermute | solution.py:142
  91.3 3.1 %copy-start.10 = (f32[2,384,768]{2,1,0:T(8,128)}, f32[2,384,768]{2,1,0:T(8,128)S(1)}, u32[]{:S(2)}) copy-start(f32[2,384,768]{2,1,0:T(8,128)S(1)} %constant_dynamic-update-slice_fusion.7) | copy-start | bytes 7077892
  91.3 28.4 %copy-start.14 = (f32[2,1,24,3072]{3,2,1,0:T(8,128)S(1)}, f32[2,1,24,3072]{3,2,1,0:T(8,128)}, u32[]{:S(2)}) copy-start(f32[2,1,24,3072]{3,2,1,0:T(8,128)} %param.9) | copy-start | bytes 1769476
  91.4 28.4 %copy-start.16 = (f32[2,1,24,3072]{3,2,1,0:T(8,128)S(1)}, f32[2,1,24,3072]{3,2,1,0:T(8,128)}, u32[]{:S(2)}) copy-start(f32[2,1,24,3072]{3,2,1,0:T(8,128)} %param.10) | copy-start | bytes 1769476
  92.0 41.9 %collective-permute-start.12 = (f32[256,768]{1,0:T(8,128)}, f32[256,768]{1,0:T(8,128)}, u32[]{:S(2)}, u32[]{:S(2)}) collective-permute-start(f32[256,768]{1,0:T(8,128)} %collective-permute-done.11), channel_id=1, source_target_pairs={{0,8},{8,0},{16,24},{24,16},{1,9},{9,1},{17,25},{25,17},{2,10},{10... | collective-permute-start | bytes 2359304 | tf_op jit(solution)/shard_map/ppermute | solution.py:142
  98.5 22.4 %copy-start.11 = (f32[2,384,768]{2,1,0:T(8,128)S(1)}, f32[2,384,768]{2,1,0:T(8,128)}, u32[]{:S(2)}) copy-start(f32[2,384,768]{2,1,0:T(8,128)} %copy-done.10) | copy-start | bytes 7077892
  117.5 28.6 %collective-permute-start.9 = (f32[2,96,768]{2,1,0:T(8,128)}, f32[2,96,768]{2,1,0:T(8,128)S(1)}, u32[]{:S(2)}, u32[]{:S(2)}) collective-permute-start(f32[2,96,768]{2,1,0:T(8,128)} %collective-permute-done.8), channel_id=1, source_target_pairs={{0,8},{8,0},{16,24},{24,16},{1,9},{9,1},{17,25},{25,17},{2,10},{10... | collective-permute-start | bytes 1769480 | tf_op jit(solution)/shard_map/ppermute | solution.py:142
  146.2 1.4 copy-start.12

commit v6 on v5

--- a/solution.py
+++ b/solution.py
@@ -202,7 +202,7 @@
     )(emb_base.reshape(tp_count, 2, half_rows, width), p0, p1, p2, p3, basis)
     emb_block, proj_sum, dense_base = meet(emb_block, proj_sum, dense_base)
     dense_base = swap(dense_base)
-    across, near, emb_block = meet(across, near, emb_block)
+    near, emb_block = meet(near, emb_block)
     dense_sum = own + jnp.concatenate([low[1:] + across, high[:1] + near])
     emb_block = emb_block.reshape(emb_rows, width)
     dense_block = (

time: 149 us -> 146 us (0.980)
  starting transfers between devices: 36.4 us -> 32.5 us
    ppermute x13, starting transfers between devices: 22.6 us -> 18.8 us  [send(): return lax.ppermute(x, 'rep', [(i, i ^ d) for i in range(groups)])]
  transfers between devices with their start and end apart: 17 -> 17, of which waited for: 10 -> 9; matrix products, arithmetic and copies ran while one was open for 17% -> 17% of each run, Pallas kernels for 7% -> 7%
where the time goes in v6:
time: 146 us
  waiting for transfers between devices  67.8 us (46%)
  starting transfers between devices  32.5 us (22%)
  local copies, waits for them, and re-layouts  22.4 us (15%)
  other arithmetic  11.9 us (8%)
  Pallas kernels  9.98 us (7%)
    ppermute x13, waiting for transfers between devices, send(): return lax.ppermute(x, 'rep', [(i, i ^ d) for i in range(groups)])  60.9 us
    ppermute x13, starting transfers between devices, send(): return lax.ppermute(x, 'rep', [(i, i ^ d) for i in range(groups)])  18.8 us
    all_to_all x4, starting transfers between devices, swap(): return lax.all_to_all(x, 'tp', split_axis=0, concat_axis=0, tiled=True)  13.7 us
    dynamic_update_slice x4, local copies, waits for them, and re-layouts, per_device(): lax.dynamic_update_slice(embed_train, value, ((me ^ d) * emb_rows, 0))  7.12 us
    all_to_all x4, waiting for transfers between devices, swap(): return lax.all_to_all(x, 'tp', split_axis=0, concat_axis=0, tiled=True)  6.91 us
    unnamed x34, local copies, waits for them, and re-layouts  6.36 us
    add x2, other arithmetic, per_device(): dense_sum = own + jnp.concatenate([low[1:] + across, high[:1] + near])  3.59 us
    pallas_call x1, Pallas kernels, per_device(): call(emb_base_body, [shaped(tp_count, piece_rows, width), shaped(emb_rows...  3.49 us
  transfers between devices with their start and end apart: 17, of which 9 were waited for; matrix products, arithmetic and copies ran while one was open for 17% of the time, Pallas kernels for 7%

profile of v6, /device:TPU:0, one launch (start us, length us, event | category | flops | bytes accessed | tf_op | source)
XLA Modules:
  0.0 145.5 jit_solution(4997090585849248686)
XLA Ops:
  0.7 1.5 %dynamic-slice_bitcast_fusion.1 = (f32[1,96,768]{2,1,0:T(8,128)S(1)}, f32[1,96,768]{2,1,0:T(8,128)S(1)}, f32[1,96,768]{2,1,0:T(8,128)S(1)}, f32[1,96,768]{2,1,0:T(8,128)S(1)}) fusion(f32[1,2,384,768]{3,2,1,0:T(8,128)} %param.7, s32[]{:T(128)S(6)} %select_n.33, s32[]{:T(128)S(6)} %select_n.32, s32[]{:T(128)S(6)} %select_n.31), kind=kLoop, calls=%fused_computation.16 | loop fusion | bytes 2359308 | tf_op jit(solution)/shard_map/dynamic_slice | solution.py:164
  2.2 1.1 pad_maximum_fusion
  3.3 3.0 %collective-permute-start = (f32[2,96,768]{2,1,0:T(8,128)}, f32[2,96,768]{2,1,0:T(8,128)}, u32[]{:S(2)}, u32[]{:S(2)}) collective-permute-start(f32[2,96,768]{2,1,0:T(8,128)} %get-tuple-element.36), channel_id=1, source_target_pairs={{0,8},{8,0},{16,24},{24,16},{1,9},{9,1},{17,25},{25,17},{2,10},{10... | collective-permute-start | bytes 1769480 | tf_op jit(solution)/shard_map/ppermute | solution.py:142
  6.3 2.6 %collective-permute-start.2 = (f32[2,96,768]{2,1,0:T(8,128)}, f32[2,96,768]{2,1,0:T(8,128)}, u32[]{:S(2)}, u32[]{:S(2)}) collective-permute-start(f32[2,96,768]{2,1,0:T(8,128)} %get-tuple-element.46), channel_id=1, source_target_pairs={{0,16},{8,24},{16,0},{24,8},{1,17},{9,25},{17,1},{25,9},{2,18},{10... | collective-permute-start | bytes 1769480 | tf_op jit(solution)/shard_map/ppermute | solution.py:142
  8.9 3.1 %shard_map.118 = (f32[4,32,128]{2,1,0:T(8,128)S(1)}, f32[4,32,128]{2,1,0:T(8,128)S(1)}, f32[4,32,128]{2,1,0:T(8,128)S(1)}, f32[4,32,128]{2,1,0:T(8,128)S(1)}) custom-call(s32[1]{0:T(128)} %bitcast.5.me_ref, f32[1,1024,768]{2,1,0:T(8,128)S(1)} %copy-done.2, f32[64,768]{1,0:T(8,128)S(1)} %copy-done.3), custom_call_target="tpu_custom_call" | custom-call | tf_op jit(solution)/shard_map/pallas_call | solution.py:73
  12.6 3.9 %collective-permute-start.6 = (f32[4,32,128]{2,1,0:T(8,128)S(1)}, f32[4,32,128]{2,1,0:T(8,128)S(1)}, u32[]{:S(2)}, u32[]{:S(2)}) collective-permute-start(f32[4,32,128]{2,1,0:T(8,128)S(1)} %get-tuple-element.51), channel_id=1, source_target_pairs={{0,24},{8,16},{16,8},{24,0},{1,25},{9,17},{17,9},{25,1},{2,26},{10... | collective-permute-start | bytes 196616 | tf_op jit(solution)/shard_map/ppermute | solution.py:142
  16.5 3.5 %shard_map.119 = (f32[4,64,768]{2,1,0:T(8,128)}, f32[256,64]{1,0:T(8,128)S(1)}) custom-call(f32[1,4,1,64,768]{4,3,2,1,0:T(8,128)S(1)} %copy-done, f32[1,4,1,64,768]{4,3,2,1,0:T(8,128)S(1)} %copy-done.1, f32[64,768]{1,0:T(8,128)S(1)} %copy-done.3), custom_call_target="tpu_custom_call" | custom-call | tf_op jit(solution)/shard_map/pallas_call | solution.py:179
  20.0 0.9 subtract_bitcast_fusion
  20.9 12.2 %collective-permute-done = f32[2,96,768]{2,1,0:T(8,128)} collective-permute-done((f32[2,96,768]{2,1,0:T(8,128)}, f32[2,96,768]{2,1,0:T(8,128)}, u32[]{:S(2)}, u32[]{:S(2)}) %collective-permute-start) | collective-permute-done | bytes 589856 | tf_op jit(solution)/shard_map/ppermute | solution.py:142
  33.1 3.5 %all-to-all-start = ((f32[4,64,768]{2,1,0:T(8,128)}), f32[4,64,768]{2,1,0:T(8,128)S(1)}, u32[]{:S(2)}, u32[]{:S(2)}) async-start(f32[4,64,768]{2,1,0:T(8,128)} %get-tuple-element.47), calls=%async_computation | async-start | bytes 1572864 | tf_op jit(solution)/shard_map/all_to_all | solution.py:148
  36.6 2.5 %collective-permute-done.2 = f32[2,96,768]{2,1,0:T(8,128)} collective-permute-done((f32[2,96,768]{2,1,0:T(8,128)}, f32[2,96,768]{2,1,0:T(8,128)}, u32[]{:S(2)}, u32[]{:S(2)}) %collective-permute-start.2) | collective-permute-done | bytes 589856 | tf_op jit(solution)/shard_map/ppermute | solution.py:142
  39.2 2.1 %slice_add_fusion.2 = (f32[1,96,768]{2,1,0:T(8,128)}, f32[1,96,768]{2,1,0:T(8,128)}) fusion(f32[2,96,768]{2,1,0:T(8,128)} %collective-permute-done, f32[2,384,768]{2,1,0:T(8,128)} %bitcast.47, s32[]{:T(128)S(6)} %select_n.33, f32[2,96,768]{2,1,0:T(8,128)} %collective-permute-done.2, s32[]{:T(128)S(6)} %select_n.32), kind=kLoop, calls=%fused_computation.13 | loop fusion | flops 147456 | bytes 1769480 | tf_op jit(solution)/shard_map/add | solution.py:189
  41.3 3.0 %collective-permute-start.1 = (f32[1,96,768]{2,1,0:T(8,128)}, f32[1,96,768]{2,1,0:T(8,128)}, u32[]{:S(2)}, u32[]{:S(2)}) collective-permute-start(f32[1,96,768]{2,1,0:T(8,128)} %get-tuple-element.66), channel_id=1, source_target_pairs={{0,16},{8,24},{16,0},{24,8},{1,17},{9,25},{17,1},{25,9},{2,18},{10... | collective-permute-start | bytes 884744 | tf_op jit(solution)/shard_map/ppermute | solution.py:142
  44.3 1.2 slice_bitcast_fusion.7
  45.5 0.9 pad_maximum_fusion.2
  46.4 0.6 copy-done.4
  47.0 0.6 copy-done.6
  47.6 0.6 copy-done.8
  48.3 0.8 copy-done.5
  49.1 0.8 copy-done.7
  50.0 0.8 copy-done.9
  50.8 0.8 shard_map.120
  51.6 3.0 %collective-permute-done.3 = f32[1,96,768]{2,1,0:T(8,128)} collective-permute-done((f32[1,96,768]{2,1,0:T(8,128)}, f32[1,96,768]{2,1,0:T(8,128)}, u32[]{:S(2)}, u32[]{:S(2)}) %collective-permute-start.3) | collective-permute-done | bytes 294944 | tf_op jit(solution)/shard_map/ppermute | solution.py:142
  54.6 2.0 %collective-permute-start.11 = (f32[256,768]{1,0:T(8,128)S(1)}, f32[256,768]{1,0:T(8,128)}, u32[]{:S(2)}, u32[]{:S(2)}) collective-permute-start(f32[256,768]{1,0:T(8,128)S(1)} %bitcast.45), channel_id=1, source_target_pairs={{0,16},{8,24},{16,0},{24,8},{1,17},{9,25},{17,1},{25,9},{2,18},{10... | collective-permute-start | bytes 2359304 | tf_op jit(solution)/shard_map/ppermute | solution.py:142
  56.6 3.5 %all-to-all-start.3 = ((f32[4,2,24,768]{3,2,1,0:T(8,128)}), f32[4,2,24,768]{3,2,1,0:T(8,128)S(1)}, u32[]{:S(2)}, u32[]{:S(2)}) async-start(f32[4,2,24,768]{3,2,1,0:T(8,128)} %pad_maximum_fusion.2), calls=%async_computation.3 | async-start | bytes 1179648 | tf_op jit(solution)/shard_map/all_to_all | solution.py:148
  60.1 1.8 %slice_add_fusion.3 = f32[1,96,768]{2,1,0:T(8,128)} fusion(f32[1,96,768]{2,1,0:T(8,128)} %collective-permute-done.1, f32[2,96,768]{2,1,0:T(8,128)} %collective-permute-done), kind=kLoop, calls=%fused_computation.14 | loop fusion | flops 73728 | bytes 884736 | tf_op jit(solution)/shard_map/add | solution.py:206
  61.9 1.8 %slice_add_fusion.1 = f32[1,96,768]{2,1,0:T(8,128)} fusion(f32[1,96,768]{2,1,0:T(8,128)} %collective-permute-done.3, f32[2,96,768]{2,1,0:T(8,128)} %collective-permute-done.2), kind=kLoop, calls=%fused_computation.12 | loop fusion | flops 73728 | bytes 884736 | tf_op jit(solution)/shard_map/add | solution.py:206
  63.7 5.9 %all-to-all-done.3 = f32[4,2,24,768]{3,2,1,0:T(8,128)S(1)} async-done(((f32[4,2,24,768]{3,2,1,0:T(8,128)}), f32[4,2,24,768]{3,2,1,0:T(8,128)S(1)}, u32[]{:S(2)}, u32[]{:S(2)}) %all-to-all-start.3) | async-done | bytes 589856 | tf_op jit(solution)/shard_map/all_to_all | solution.py:148
  69.6 3.3 %all-to-all-start.2 = ((f32[4,32,128]{2,1,0:T(8,128)}), f32[4,32,128]{2,1,0:T(8,128)S(1)}, u32[]{:S(2)}, u32[]{:S(2)}) async-start(f32[4,32,128]{2,1,0:T(8,128)} %get-tuple-element.57), calls=%async_computation.2 | async-start | bytes 131072 | tf_op jit(solution)/shard_map/all_to_all | solution.py:148
  72.9 2.2 %bitcast_add_fusion = (f32[2,96,768]{2,1,0:T(8,128)}, f32[2,96,768]{2,1,0:T(8,128)S(1)}) fusion(f32[2,4,24,768]{3,2,1,0:T(8,128)S(1)} %copy.17, f32[1,96,768]{2,1,0:T(8,128)} %slice_add_fusion.1, f32[1,96,768]{2,1,0:T(8,128)} %slice_add_fusion.3, f32[2,384,768]{2,1,0:T(8,128)} %bitcast.48, s32[]{:T(128)S(6)} %select_n.34), kind=kLoop, calls=%fused_computation.6 | loop fusion | flops 589824 | bytes 2949124 | tf_op jit(solution)/shard_map/add | solution.py:209
  75.1 0.9 copy.19
  76.0 1.0 all-to-all-done.2.back_ref
  77.0 3.5 %all-to-all-start.1 = ((f32[4,2,24,768]{3,2,1,0:T(8,128)}), f32[4,2,24,768]{3,2,1,0:T(8,128)S(1)}, u32[]{:S(2)}, u32[]{:S(2)}) async-start(f32[4,2,24,768]{3,2,1,0:T(8,128)} %bitcast.49), calls=%async_computation.1 | async-start | bytes 1179648 | tf_op jit(solution)/shard_map/all_to_all | solution.py:148
  80.4 1.9 %broadcast_in_dim.9 = f32[1024,768]{1,0:T(8,128)} broadcast(f32[]{:T(128)} %constant.37.clone.1), dimensions={} | broadcast | bytes 3145732 | tf_op jit(solution)/shard_map/broadcast_in_dim | solution.py:224
  82.3 0.9 constant_dynamic-update-slice_fusion.3
  83.2 2.6 %shard_map.121 = (f32[1,4,1,64,768]{4,3,2,1,0:T(8,128)}, f32[1,4,1,64,768]{4,3,2,1,0:T(8,128)}) custom-call(f32[1,4,1,64,768]{4,3,2,1,0:T(8,128)S(1)} %copy-done, f32[1,4,1,64,768]{4,3,2,1,0:T(8,128)S(1)} %copy-done.1, f32[256,64]{1,0:T(8,128)S(1)} %get-tuple-element.56.proj_ref, f32[4,32,128]{2,1,0:T(8,128)S(1)} %all-to-all-done.2.back_ref, ...), custom_call_target="tpu_custom_call" | custom-call | tf_op jit(solution)/shard_map/pallas_call | solution.py:236
  85.8 2.9 %collective-permute-start.8 = (f32[2,96,768]{2,1,0:T(8,128)}, f32[2,96,768]{2,1,0:T(8,128)}, u32[]{:S(2)}, u32[]{:S(2)}) collective-permute-start(f32[2,96,768]{2,1,0:T(8,128)} %get-tuple-element.62), channel_id=1, source_target_pairs={{0,16},{8,24},{16,0},{24,8},{1,17},{9,25},{17,1},{25,9},{2,18},{10... | collective-permute-start | bytes 1769480 | tf_op jit(solution)/shard_map/ppermute | solution.py:142
  88.9 1.1 constant_dynamic-update-slice_fusion.7
  91.4 2.1 %constant_dynamic-update-slice_fusion.2 = f32[1024,768]{1,0:T(8,128)} fusion(f32[1024,768]{1,0:T(8,128)} %constant_dynamic-update-slice_fusion.3, f32[256,768]{1,0:T(8,128)} %collective-permute-done.10, s32[]{:T(128)S(6)} %select_n.36), kind=kLoop, calls=%fused_computation.29 | loop fusion | bytes 1572868 | tf_op jit(solution)/shard_map/dynamic_update_slice | solution.py:226
  93.5 2.1 %constant_dynamic-update-slice_fusion.1 = f32[1024,768]{1,0:T(8,128)} fusion(f32[1024,768]{1,0:T(8,128)} %constant_dynamic-update-slice_fusion.2, f32[256,768]{1,0:T(8,128)} %collective-permute-done.11, s32[]{:T(128)S(6)} %select_n.37), kind=kLoop, calls=%fused_computation.28 | loop fusion | bytes 1572868 | tf_op jit(solution)/shard_map/dynamic_update_slice | solution.py:226
  95.6 20.2 %collective-permute-done.8 = f32[2,96,768]{2,1,0:T(8,128)} collective-permute-done((f32[2,96,768]{2,1,0:T(8,128)}, f32[2,96,768]{2,1,0:T(8,128)}, u32[]{:S(2)}, u32[]{:S(2)}) %collective-permute-start.8) | collective-permute-done | bytes 589856 | tf_op jit(solution)/shard_map/ppermute | solution.py:142
  116.3 1.2 multiply_subtract_fusion
  117.4 1.1 constant_dynamic-update-slice_fusion.6
  118.5 1.1 constant_dynamic-update-slice_fusion.5
  119.7 12.3 %collective-permute-done.12 = f32[256,768]{1,0:T(8,128)} collective-permute-done((f32[256,768]{1,0:T(8,128)}, f32[256,768]{1,0:T(8,128)}, u32[]{:S(2)}, u32[]{:S(2)}) %collective-permute-start.12) | collective-permute-done | bytes 786464 | tf_op jit(solution)/shard_map/ppermute | solution.py:142
  132.0 2.1 %constant_dynamic-update-slice_fusion = f32[1024,768]{1,0:T(8,128)} fusion(f32[1024,768]{1,0:T(8,128)} %constant_dynamic-update-slice_fusion.1, f32[256,768]{1,0:T(8,128)} %collective-permute-done.12, s32[]{:T(128)S(6)} %select_n.38), kind=kLoop, calls=%fused_computation.27 | loop fusion | bytes 1572868 | tf_op jit(solution)/shard_map/dynamic_update_slice | solution.py:226
  134.0 10.0 %collective-permute-done.9 = f32[2,96,768]{2,1,0:T(8,128)S(1)} collective-permute-done((f32[2,96,768]{2,1,0:T(8,128)}, f32[2,96,768]{2,1,0:T(8,128)S(1)}, u32[]{:S(2)}, u32[]{:S(2)}) %collective-permute-start.9) | collective-permute-done | bytes 589856 | tf_op jit(solution)/shard_map/ppermute | solution.py:142
  144.1 1.4 copy-done.12
  (47 shorter events, 2.7 us)
Async XLA Ops:
  0.7 8.2 %copy-start.2 = (f32[1,1024,768]{2,1,0:T(8,128)S(1)}, f32[1,1024,768]{2,1,0:T(8,128)}, u32[]{:S(2)}) copy-start(f32[1,1024,768]{2,1,0:T(8,128)} %x_ref) | copy-start | bytes 9437188
  0.7 8.2 %copy-start.3 = (f32[64,768]{1,0:T(8,128)S(1)}, f32[64,768]{1,0:T(8,128)}, u32[]{:S(2)}) copy-start(f32[64,768]{1,0:T(8,128)} %basis_ref.7) | copy-start | bytes 589828
  2.1 14.3 %copy-start = (f32[1,4,1,64,768]{4,3,2,1,0:T(8,128)S(1)}, f32[1,4,1,64,768]{4,3,2,1,0:T(8,128)}, u32[]{:S(2)}) copy-start(f32[1,4,1,64,768]{4,3,2,1,0:T(8,128)} %outer_ref.1) | copy-start | bytes 2359300
  2.2 14.3 %copy-start.1 = (f32[1,4,1,64,768]{4,3,2,1,0:T(8,128)S(1)}, f32[1,4,1,64,768]{4,3,2,1,0:T(8,128)}, u32[]{:S(2)}) copy-start(f32[1,4,1,64,768]{4,3,2,1,0:T(8,128)} %moment_ref.3) | copy-start | bytes 2359300
  3.3 29.9 %collective-permute-start = (f32[2,96,768]{2,1,0:T(8,128)}, f32[2,96,768]{2,1,0:T(8,128)}, u32[]{:S(2)}, u32[]{:S(2)}) collective-permute-start(f32[2,96,768]{2,1,0:T(8,128)} %get-tuple-element.36), channel_id=1, source_target_pairs={{0,8},{8,0},{16,24},{24,16},{1,9},{9,1},{17,25},{25,17},{2,10},{10... | collective-permute-start | bytes 1769480 | tf_op jit(solution)/shard_map/ppermute | solution.py:142
  6.3 32.9 %collective-permute-start.2 = (f32[2,96,768]{2,1,0:T(8,128)}, f32[2,96,768]{2,1,0:T(8,128)}, u32[]{:S(2)}, u32[]{:S(2)}) collective-permute-start(f32[2,96,768]{2,1,0:T(8,128)} %get-tuple-element.46), channel_id=1, source_target_pairs={{0,16},{8,24},{16,0},{24,8},{1,17},{9,25},{17,1},{25,9},{2,18},{10... | collective-permute-start | bytes 1769480 | tf_op jit(solution)/shard_map/ppermute | solution.py:142
  8.9 11.1 %copy-start.13 = (f32[2,1,24,3072]{3,2,1,0:T(8,128)S(1)}, f32[2,1,24,3072]{3,2,1,0:T(8,128)}, u32[]{:S(2)}) copy-start(f32[2,1,24,3072]{3,2,1,0:T(8,128)} %param.9) | copy-start | bytes 1769476
  8.9 11.1 %copy-start.15 = (f32[2,1,24,3072]{3,2,1,0:T(8,128)S(1)}, f32[2,1,24,3072]{3,2,1,0:T(8,128)}, u32[]{:S(2)}) copy-start(f32[2,1,24,3072]{3,2,1,0:T(8,128)} %param.10) | copy-start | bytes 1769476
  12.0 34.3 %collective-permute-start.4 = (f32[4,32,128]{2,1,0:T(8,128)S(1)}, f32[4,32,128]{2,1,0:T(8,128)S(1)}, u32[]{:S(2)}, u32[]{:S(2)}) collective-permute-start(f32[4,32,128]{2,1,0:T(8,128)S(1)} %get-tuple-element.49), channel_id=1, source_target_pairs={{0,8},{8,0},{16,24},{24,16},{1,9},{9,1},{17,25},{25,17},{2,10},{10... | collective-permute-start | bytes 196616 | tf_op jit(solution)/shard_map/ppermute | solution.py:142
  12.6 34.4 %collective-permute-start.5 = (f32[4,32,128]{2,1,0:T(8,128)S(1)}, f32[4,32,128]{2,1,0:T(8,128)S(1)}, u32[]{:S(2)}, u32[]{:S(2)}) collective-permute-start(f32[4,32,128]{2,1,0:T(8,128)S(1)} %get-tuple-element.50), channel_id=1, source_target_pairs={{0,16},{8,24},{16,0},{24,8},{1,17},{9,25},{17,1},{25,9},{2,18},{10... | collective-permute-start | bytes 196616 | tf_op jit(solution)/shard_map/ppermute | solution.py:142
  12.6 35.0 %collective-permute-start.6 = (f32[4,32,128]{2,1,0:T(8,128)S(1)}, f32[4,32,128]{2,1,0:T(8,128)S(1)}, u32[]{:S(2)}, u32[]{:S(2)}) collective-permute-start(f32[4,32,128]{2,1,0:T(8,128)S(1)} %get-tuple-element.51), channel_id=1, source_target_pairs={{0,24},{8,16},{16,8},{24,0},{1,25},{9,17},{17,9},{25,1},{2,26},{10... | collective-permute-start | bytes 196616 | tf_op jit(solution)/shard_map/ppermute | solution.py:142
  33.1 15.1 %all-to-all-start = ((f32[4,64,768]{2,1,0:T(8,128)}), f32[4,64,768]{2,1,0:T(8,128)S(1)}, u32[]{:S(2)}, u32[]{:S(2)}) async-start(f32[4,64,768]{2,1,0:T(8,128)} %get-tuple-element.47), calls=%async_computation | async-start | bytes 1572864 | tf_op jit(solution)/shard_map/all_to_all | solution.py:148
  41.3 13.3 %collective-permute-start.3 = (f32[1,96,768]{2,1,0:T(8,128)}, f32[1,96,768]{2,1,0:T(8,128)}, u32[]{:S(2)}, u32[]{:S(2)}) collective-permute-start(f32[1,96,768]{2,1,0:T(8,128)} %get-tuple-element.67), channel_id=1, source_target_pairs={{0,8},{8,0},{16,24},{24,16},{1,9},{9,1},{17,25},{25,17},{2,10},{10... | collective-permute-start | bytes 884744 | tf_op jit(solution)/shard_map/ppermute | solution.py:142
  41.3 18.8 %collective-permute-start.1 = (f32[1,96,768]{2,1,0:T(8,128)}, f32[1,96,768]{2,1,0:T(8,128)}, u32[]{:S(2)}, u32[]{:S(2)}) collective-permute-start(f32[1,96,768]{2,1,0:T(8,128)} %get-tuple-element.66), channel_id=1, source_target_pairs={{0,16},{8,24},{16,0},{24,8},{1,17},{9,25},{17,1},{25,9},{2,18},{10... | collective-permute-start | bytes 884744 | tf_op jit(solution)/shard_map/ppermute | solution.py:142
  46.4 0.6 copy-start.4
  47.0 0.6 copy-start.6
  47.6 0.6 copy-start.8
  48.3 0.8 copy-start.5
  49.1 0.8 copy-start.7
  50.0 0.8 copy-start.9
  54.6 36.4 %collective-permute-start.10 = (f32[256,768]{1,0:T(8,128)S(1)}, f32[256,768]{1,0:T(8,128)}, u32[]{:S(2)}, u32[]{:S(2)}) collective-permute-start(f32[256,768]{1,0:T(8,128)S(1)} %bitcast.44), channel_id=1, source_target_pairs={{0,8},{8,0},{16,24},{24,16},{1,9},{9,1},{17,25},{25,17},{2,10},{10... | collective-permute-start | bytes 2359304 | tf_op jit(solution)/shard_map/ppermute | solution.py:142
  54.6 36.0 %collective-permute-start.11 = (f32[256,768]{1,0:T(8,128)S(1)}, f32[256,768]{1,0:T(8,128)}, u32[]{:S(2)}, u32[]{:S(2)}) collective-permute-start(f32[256,768]{1,0:T(8,128)S(1)} %bitcast.45), channel_id=1, source_target_pairs={{0,16},{8,24},{16,0},{24,8},{1,17},{9,25},{17,1},{25,9},{2,18},{10... | collective-permute-start | bytes 2359304 | tf_op jit(solution)/shard_map/ppermute | solution.py:142
  56.6 13.0 %all-to-all-start.3 = ((f32[4,2,24,768]{3,2,1,0:T(8,128)}), f32[4,2,24,768]{3,2,1,0:T(8,128)S(1)}, u32[]{:S(2)}, u32[]{:S(2)}) async-start(f32[4,2,24,768]{3,2,1,0:T(8,128)} %pad_maximum_fusion.2), calls=%async_computation.3 | async-start | bytes 1179648 | tf_op jit(solution)/shard_map/all_to_all | solution.py:148
  69.6 7.4 %all-to-all-start.2 = ((f32[4,32,128]{2,1,0:T(8,128)}), f32[4,32,128]{2,1,0:T(8,128)S(1)}, u32[]{:S(2)}, u32[]{:S(2)}) async-start(f32[4,32,128]{2,1,0:T(8,128)} %get-tuple-element.57), calls=%async_computation.2 | async-start | bytes 131072 | tf_op jit(solution)/shard_map/all_to_all | solution.py:148
  77.0 18.6 %all-to-all-start.1 = ((f32[4,2,24,768]{3,2,1,0:T(8,128)}), f32[4,2,24,768]{3,2,1,0:T(8,128)S(1)}, u32[]{:S(2)}, u32[]{:S(2)}) async-start(f32[4,2,24,768]{3,2,1,0:T(8,128)} %bitcast.49), calls=%async_computation.1 | async-start | bytes 1179648 | tf_op jit(solution)/shard_map/all_to_all | solution.py:148
  85.8 31.6 %collective-permute-start.7 = (f32[2,96,768]{2,1,0:T(8,128)}, f32[2,96,768]{2,1,0:T(8,128)}, u32[]{:S(2)}, u32[]{:S(2)}) collective-permute-start(f32[2,96,768]{2,1,0:T(8,128)} %get-tuple-element.62), channel_id=1, source_target_pairs={{0,8},{8,0},{16,24},{24,16},{1,9},{9,1},{17,25},{25,17},{2,10},{10... | collective-permute-start | bytes 1769480 | tf_op jit(solution)/shard_map/ppermute | solution.py:142
  85.8 30.0 %collective-permute-start.8 = (f32[2,96,768]{2,1,0:T(8,128)}, f32[2,96,768]{2,1,0:T(8,128)}, u32[]{:S(2)}, u32[]{:S(2)}) collective-permute-start(f32[2,96,768]{2,1,0:T(8,128)} %get-tuple-element.62), channel_id=1, source_target_pairs={{0,16},{8,24},{16,0},{24,8},{1,17},{9,25},{17,1},{25,9},{2,18},{10... | collective-permute-start | bytes 1769480 | tf_op jit(solution)/shard_map/ppermute | solution.py:142
  90.0 1.4 copy-start.10
  90.0 26.2 %copy-start.14 = (f32[2,1,24,3072]{3,2,1,0:T(8,128)S(1)}, f32[2,1,24,3072]{3,2,1,0:T(8,128)}, u32[]{:S(2)}) copy-start(f32[2,1,24,3072]{3,2,1,0:T(8,128)} %param.9) | copy-start | bytes 1769476
  90.0 26.2 %copy-start.16 = (f32[2,1,24,3072]{3,2,1,0:T(8,128)S(1)}, f32[2,1,24,3072]{3,2,1,0:T(8,128)}, u32[]{:S(2)}) copy-start(f32[2,1,24,3072]{3,2,1,0:T(8,128)} %param.10) | copy-start | bytes 1769476
  90.6 41.4 %collective-permute-start.12 = (f32[256,768]{1,0:T(8,128)}, f32[256,768]{1,0:T(8,128)}, u32[]{:S(2)}, u32[]{:S(2)}) collective-permute-start(f32[256,768]{1,0:T(8,128)} %collective-permute-done.11), channel_id=1, source_target_pairs={{0,8},{8,0},{16,24},{24,16},{1,9},{9,1},{17,25},{25,17},{2,10},{10... | collective-permute-start | bytes 2359304 | tf_op jit(solution)/shard_map/ppermute | solution.py:142
  95.6 21.9 %copy-start.11 = (f32[2,384,768]{2,1,0:T(8,128)S(1)}, f32[2,384,768]{2,1,0:T(8,128)}, u32[]{:S(2)}) copy-start(f32[2,384,768]{2,1,0:T(8,128)} %copy-done.10) | copy-start | bytes 7077892
  115.8 28.3 %collective-permute-start.9 = (f32[2,96,768]{2,1,0:T(8,128)}, f32[2,96,768]{2,1,0:T(8,128)S(1)}, u32[]{:S(2)}, u32[]{:S(2)}) collective-permute-start(f32[2,96,768]{2,1,0:T(8,128)} %collective-permute-done.8), channel_id=1, source_target_pairs={{0,8},{8,0},{16,24},{24,16},{1,9},{9,1},{17,25},{25,17},{2,10},{10... | collective-permute-start | bytes 1769480 | tf_op jit(solution)/shard_map/ppermute | solution.py:142
  144.1 1.4 copy-start.12
